TPU v7x, 32 devices: a whole 2x2x4 slice. The times are simulated.
32 devices in a mesh: lon: 8 (over z, y), lat: 4 (over x, core).
Axes of the slice: x: 2, y: 2, z: 4, core: 2. Of those that a mesh axis runs over, the one named last changes fastest.
Arguments:
- sample_deviations: float32 [32, 32, 32, 1024], P(None, None, 'lat', 'lon'), may hold values from -6 to 6
- east_courant: float32 [32, 32, 1024], P(None, 'lat', 'lon'), may hold values from -0.45 to 0.45
- north_courant: float32 [32, 32, 1024], P(None, 'lat', 'lon'), may hold values from -0.45 to 0.45
- production: float32 [32, 32, 1024], P(None, 'lat', 'lon'), may hold values from -1.8 to 1.8
- loss_rate: float32 [32, 32, 1024], P(None, 'lat', 'lon'), may hold values from 0.02 to 0.3
- entry_count: int32 [32], P(('lon', 'lat')), may hold values from 24 to 48, as said below
- entry_row: int32 [1536], P(('lon', 'lat')), may hold values from 0 to 7
- entry_block: int32 [1536], P(('lon', 'lat')), may hold values from 0 to 15
- path_weight: bfloat16 [1536, 128, 128], P(('lon', 'lat')), may hold values from 0 to 0.15234375
- observed: float32 [16384], P(('lon', 'lat')), may hold values from -288 to 288
- obs_var: float32 [16384], P(('lon', 'lat')), may hold values from 64 to 4608, as said below
Outputs:
- updated_samples: float32 [32, 32, 32, 1024], P(None, None, 'lat', 'lon')
- prior_samples_in_path_space: float32 [32, 16384], P(None, ('lon', 'lat'))
- scaled_innovation: float32 [16384], P(('lon', 'lat'))
Inputs may be any that keep to these rules, and one draw needn't show every extreme that they name: `entry_count`: live crossing slots of each tile; some tile has all 48 live in every draw. `obs_var`: positive.
All inputs are finite; a program needn't handle non-finite values.
Results may differ from a plain program's by a relative error of at most 0.0025.
Values sent between devices are 32-bit elements; how exact they have to be, the bound alone decides.
No kernel may reach another device: no remote copies, remote signals or barrier semaphores. Data moves between devices by JAX's collectives and lax.ppermute only.
A program may use at most 64 MiB of HBM per device.

v0:
```python
import math

import jax
import jax.numpy as jnp
from jax import lax
from jax.sharding import PartitionSpec as P

ALTITUDE_LAYERS = 32
RAY_BLOCK = 128
BLOCKS_DEV = 4
SLOTS_TILE = 48


highest = lax.Precision.HIGHEST


def extended(x, sides, width, wrap):
    for axis, dim in sides:
        size, length = (lax.axis_size(axis), x.shape[dim])
        up = [(i, (i + 1) % size) for i in range(size if wrap else size - 1)]
        down = [(j, i) for i, j in up]
        last = lax.slice_in_dim(x, length - width, length, axis=dim)
        initial = lax.slice_in_dim(x, 0, width, axis=dim)
        before = lax.ppermute(last, axis, up)
        after = lax.ppermute(initial, axis, down)
        x = jnp.concatenate([before, x, after], axis=dim)
    return x


def advance(
    plasma_concentration,
    west_cell,
    east_cell,
    south_cell,
    north_cell,
    east_speed,
    north_speed,
    source,
    loss_rate,
):
    advected = (
        plasma_concentration
        - jnp.maximum(east_speed, 0.0) * (plasma_concentration - west_cell)
        - jnp.minimum(east_speed, 0.0) * (east_cell - plasma_concentration)
    )
    advected = (
        advected
        - jnp.maximum(north_speed, 0.0) * (plasma_concentration - south_cell)
        - jnp.minimum(north_speed, 0.0) * (north_cell - plasma_concentration)
    )
    return (1.0 - loss_rate) * advected + source


def analysis_weights(gram_sum, pull_sum):
    member_total = gram_sum.shape[0]
    identity = jnp.eye(member_total, dtype=gram_sum.dtype)
    factor_low = jnp.linalg.cholesky(gram_sum + (member_total - 1.0) * identity)
    halfway = lax.linalg.triangular_solve(factor_low, pull_sum[:, None], left_side=True, lower=True)
    mean_weights = lax.linalg.triangular_solve(
        factor_low, halfway, left_side=True, lower=True, transpose_a=True
    )
    inverse = lax.linalg.triangular_solve(factor_low, identity, left_side=True, lower=True)
    return mean_weights + math.sqrt(member_total - 1.0) * inverse.T


def ray_moments(ensemble, observed, obs_var):
    ray_mean = jnp.mean(ensemble, axis=0)
    spread = ensemble - ray_mean
    misfit = observed - ray_mean
    gram_sum = jnp.dot(spread / obs_var, spread.T, precision=highest)
    pull_sum = jnp.dot(spread, misfit / obs_var, precision=highest)
    return (gram_sum, pull_sum, misfit / jnp.sqrt(obs_var))


def per_device(
    sample_deviations,
    east_courant,
    north_courant,
    production,
    loss_rate,
    entry_count,
    entry_row,
    entry_block,
    path_weight,
    observed,
    obs_var,
):
    ensemble_size = sample_deviations.shape[0]
    plasma_concentration = sample_deviations
    for repeat in range(2):
        lon_framed = extended(plasma_concentration, (("lon", 3),), 1, True)
        lat_framed = extended(plasma_concentration, (("lat", 2),), 1, False)
        plasma_concentration = advance(
            plasma_concentration,
            lon_framed[..., :-2],
            lon_framed[..., 2:],
            lat_framed[..., :-2, :],
            lat_framed[..., 2:, :],
            east_courant,
            north_courant,
            production,
            loss_rate,
        )
    column_integral_total = (
        jnp.sum(plasma_concentration, axis=1) / math.sqrt(ALTITUDE_LAYERS)
    ).astype(jnp.bfloat16)
    picked = jnp.take(column_integral_total, entry_row, axis=1)
    partial_value = jnp.einsum(
        "mkc,kcr->kmr", picked, path_weight, preferred_element_type=jnp.float32
    )
    lat_size = lax.axis_size("lat")
    col_blocks = BLOCKS_DEV * lat_size
    live_slots = (jnp.arange(SLOTS_TILE) < entry_count[0]).astype(jnp.float32)
    slot_select = (entry_block[None, :] == jnp.arange(col_blocks)[:, None]).astype(
        jnp.float32
    ) * live_slots[None, :]
    summed = jnp.einsum("bk,kmr->mbr", slot_select, partial_value, precision=highest).reshape(
        ensemble_size, col_blocks * RAY_BLOCK
    )
    prior_samples_in_path_space = lax.psum_scatter(summed, "lat", scatter_dimension=1, tiled=True)
    gram_sum, pull_sum, scaled_innovation = ray_moments(
        prior_samples_in_path_space, observed, obs_var
    )
    gram_sum, pull_sum = lax.psum((gram_sum, pull_sum), ("lon", "lat"))
    transform = analysis_weights(gram_sum, pull_sum)
    raveled_grid_vector = plasma_concentration.reshape(ensemble_size, -1)
    centre = jnp.mean(raveled_grid_vector, axis=0)
    anomalies = raveled_grid_vector - centre
    updated_samples = centre + jnp.dot(transform.T, anomalies, precision=highest)
    return (
        updated_samples.reshape(plasma_concentration.shape),
        prior_samples_in_path_space,
        scaled_innovation,
    )


def solution(mesh):
    in_specs = (
        P(None, None, "lat", "lon"),
        P(None, "lat", "lon"),
        P(None, "lat", "lon"),
        P(None, "lat", "lon"),
        P(None, "lat", "lon"),
        P(("lon", "lat")),
        P(("lon", "lat")),
        P(("lon", "lat")),
        P(("lon", "lat"), None, None),
        P(("lon", "lat")),
        P(("lon", "lat")),
    )
    out_specs = (P(None, None, "lat", "lon"), P(None, ("lon", "lat")), P(("lon", "lat")))
    return jax.shard_map(
        per_device, mesh=mesh, in_specs=in_specs, out_specs=out_specs, check_vma=False
    )
```

profile of v0, /device:TPU:0, one launch (start us, length us, event | category | flops | bytes accessed | tf_op | source)
XLA Modules:
  0.0 201.4 jit_solution(16212824213112395093)
XLA Ops:
  7.2 8.1 %fusion.64 = (f32[32,32,8,1]{3,2,1,0:T(8,128)}, f32[32,32,8,1]{3,2,1,0:T(8,128)}) fusion(f32[32,32,8,128]{3,2,1,0:T(8,128)} %param.11), kind=kLoop, calls=%fused_computation.101 | loop fusion | bytes 131072 | tf_op jit(solution)/shard_map/slice | solution.py:22
  15.3 3.2 %copy.180 = f32[32,32,8,1]{1,2,3,0:T(8,128)S(1)} copy(f32[32,32,8,1]{3,2,1,0:T(8,128)} %get-tuple-element.12) | data formatting | bytes 65536
  18.6 3.0 %collective-permute-start = (f32[32,32,8,1]{1,2,3,0:T(8,128)S(1)}, f32[32,32,8,1]{1,2,3,0:T(8,128)}, u32[]{:S(2)}, u32[]{:S(2)}) collective-permute-start(f32[32,32,8,1]{1,2,3,0:T(8,128)S(1)} %copy.180), channel_id=1, source_target_pairs={{0,4},{4,8},{8,12},{12,16},{16,20},{20,24},{24,28},{28,0},{1,5},{5... | collective-permute-start | bytes 98312 | tf_op jit(solution)/shard_map/ppermute | solution.py:24
  21.6 3.8 %copy.181 = f32[32,32,8,1]{1,2,3,0:T(8,128)} copy(f32[32,32,8,1]{3,2,1,0:T(8,128)} %get-tuple-element.13) | data formatting | bytes 65536
  25.5 3.1 %collective-permute-start.1 = (f32[32,32,8,1]{1,2,3,0:T(8,128)}, f32[32,32,8,1]{1,2,3,0:T(8,128)}, u32[]{:S(2)}, u32[]{:S(2)}) collective-permute-start(f32[32,32,8,1]{1,2,3,0:T(8,128)} %copy.181), channel_id=1, source_target_pairs={{4,0},{8,4},{12,8},{16,12},{20,16},{24,20},{28,24},{0,28},{5,1},{9... | collective-permute-start | bytes 98312 | tf_op jit(solution)/shard_map/ppermute | solution.py:25
  28.6 5.4 %fusion.65 = (f32[32,32,1,128]{3,2,1,0:T(1,128)}, f32[32,32,1,128]{3,2,1,0:T(1,128)}) fusion(f32[32,32,8,128]{3,2,1,0:T(8,128)} %param.11), kind=kLoop, calls=%fused_computation.102 | loop fusion | bytes 2097152 | tf_op jit(solution)/shard_map/slice | solution.py:22
  38.5 3.8 %copy.159 = f32[32,32,8,1]{3,2,1,0:T(8,128)} copy(f32[32,32,8,1]{1,2,3,0:T(8,128)} %collective-permute-done) | data formatting | bytes 65536 | tf_op jit(solution)/shard_map/ppermute | solution.py:24
  42.3 3.8 %copy.161 = f32[32,32,8,1]{3,2,1,0:T(8,128)} copy(f32[32,32,8,1]{1,2,3,0:T(8,128)} %collective-permute-done.1) | data formatting | bytes 65536 | tf_op jit(solution)/shard_map/ppermute | solution.py:25
  46.2 12.7 %fusion.19 = f32[32,32,8,128]{3,2,1,0:T(8,128)S(1)} fusion(f32[32,32,8,128]{3,2,1,0:T(8,128)} %param.11, f32[32,32,1,128]{3,2,1,0:T(1,128)S(1)} %bitcast.69, f32[32,32,1,128]{3,2,1,0:T(1,128)S(1)} %bitcast.68, f32[32,32,8,1]{3,2,1,0:T(8,128)} %copy.161, f32[32,32,8,1]{3,2,1,0:T(8,128)} %copy.159, f32[32,8,128]{2,1,0:T(8,128)S(1)} %copy-done.2, ...), kind=kLoop, calls=%fused_computation.27 | loop fusion | flops 18874368 | bytes 10289152 | tf_op jit(solution)/shard_map/add | solution.py:51
  58.8 2.4 %fusion.63 = (f32[32,32,1,128]{3,2,1,0:T(1,128)}, f32[32,32,1,128]{3,2,1,0:T(1,128)}) fusion(f32[32,32,8,128]{3,2,1,0:T(8,128)S(1)} %fusion.19), kind=kLoop, calls=%fused_computation.100 | loop fusion | bytes 2097152 | tf_op jit(solution)/shard_map/slice | solution.py:22
  61.2 4.7 %collective-permute-start.6 = (f32[32,32,1,128]{3,1,2,0:T(8,128)}, f32[32,32,1,128]{3,1,2,0:T(8,128)S(1)}, u32[]{:S(2)}, u32[]{:S(2)}) collective-permute-start(f32[32,32,1,128]{3,1,2,0:T(8,128)} %bitcast.2), channel_id=1, source_target_pairs={{0,1},{1,2},{2,3},{4,5},{5,6},{6,7},{8,9},{9,10},{10,11},{12,13},{... | collective-permute-start | bytes 1572872 | tf_op jit(solution)/shard_map/ppermute | solution.py:24
  67.2 4.9 %fusion.62 = (f32[32,32,8,1]{3,2,1,0:T(8,128)}, f32[32,32,8,1]{3,2,1,0:T(8,128)}) fusion(f32[32,32,8,128]{3,2,1,0:T(8,128)S(1)} %fusion.19), kind=kLoop, calls=%fused_computation.99 | loop fusion | bytes 131072 | tf_op jit(solution)/shard_map/slice | solution.py:22
  72.1 3.2 %copy.166 = f32[32,32,8,1]{1,2,3,0:T(8,128)S(1)} copy(f32[32,32,8,1]{3,2,1,0:T(8,128)} %get-tuple-element.8) | data formatting | bytes 65536 | tf_op jit(solution)/shard_map/slice | solution.py:22
  75.4 3.8 %copy.168 = f32[32,32,8,1]{1,2,3,0:T(8,128)} copy(f32[32,32,8,1]{3,2,1,0:T(8,128)} %get-tuple-element.9) | data formatting | bytes 65536 | tf_op jit(solution)/shard_map/slice | solution.py:23
  79.2 4.7 %collective-permute-start.5 = (f32[32,32,8,1]{1,2,3,0:T(8,128)}, f32[32,32,8,1]{1,2,3,0:T(8,128)}, u32[]{:S(2)}, u32[]{:S(2)}) collective-permute-start(f32[32,32,8,1]{1,2,3,0:T(8,128)} %copy.168), channel_id=1, source_target_pairs={{4,0},{8,4},{12,8},{16,12},{20,16},{24,20},{28,24},{0,28},{5,1},{9... | collective-permute-start | bytes 98312 | tf_op jit(solution)/shard_map/ppermute | solution.py:25
  83.9 3.8 %copy.167 = f32[32,32,8,1]{3,2,1,0:T(8,128)} copy(f32[32,32,8,1]{1,2,3,0:T(8,128)} %collective-permute-done.4) | data formatting | bytes 65536 | tf_op jit(solution)/shard_map/ppermute | solution.py:24
  87.7 3.9 %copy.169 = f32[32,32,8,1]{3,2,1,0:T(8,128)} copy(f32[32,32,8,1]{1,2,3,0:T(8,128)} %collective-permute-done.5) | data formatting | bytes 65536 | tf_op jit(solution)/shard_map/ppermute | solution.py:25
  91.6 15.0 %fusion.60 = (f32[32,8,128]{2,1,0:T(8,128)S(1)}, f32[32,8,128]{2,1,0:T(8,128)S(1)}, f32[32,32,8,128]{3,2,1,0:T(8,128)}) fusion(f32[32,8,128]{2,1,0:T(8,128)S(1)} %copy-done.2, f32[32,32,8,128]{3,2,1,0:T(8,128)} %copy-done.1, f32[32,32,1,128]{3,2,1,0:T(1,128)S(1)} %bitcast.67, f32[32,8,128]{2,1,0:T(8,128)S(1)} %get-tuple-element.19, ...), kind=kLoop, calls=%fused_computation.98 | loop fusion | flops 20905984 | bytes 10551296 | tf_op jit(solution)/shard_map/reduce_sum | solution.py:127
  109.7 23.5 %reduce-scatter.2.cloned.1.call-done = f32[32,512]{1,0:T(8,128)} async-done(((f32[32,2048]{1,0:T(8,128)}), f32[32,512]{1,0:T(8,128)}) %reduce-scatter.2.cloned.1.call-update) | async-done | bytes 65552 | tf_op jit(solution)/shard_map/reduce_scatter | solution.py:120
  136.8 39.5 %all-reduce = (f32[32,32]{1,0:T(8,128)S(1)}, f32[32]{0:T(128)S(1)}) all-reduce(f32[32,32]{1,0:T(8,128)S(1)} %fusion.40, f32[32]{0:T(128)S(1)} %convolution_bitcast_fusion), channel_id=1, replica_groups=mesh['lon'=8,'lat'=4] {'lon','lat'}, use_global_device_ids=true, to_apply=%region_4.5 | all-reduce | flops 1056 | bytes 8448 | tf_op jit(solution)/shard_map/psum | solution.py:124
  176.3 2.9 %cholesky.17 = f32[32,32]{1,0:T(8,128)S(1)} custom-call(f32[32,32]{1,0:T(8,128)S(1)} %fusion.51), custom_call_target="Cholesky" | custom-call | tf_op jit(solution)/shard_map/jit(cholesky)/cholesky | solution.py:57
  180.6 2.4 %custom-call.10 = f32[1,32,32]{1,2,0:T(8,128)S(1)} custom-call(f32[1,32,32]{2,1,0:T(8,128)S(1)} %fusion.47), custom_call_target="InvertDiagBlocksLowerTriangular" | custom-call | tf_op jit(solution)/shard_map/triangular_solve | solution.py:59
  183.6 8.3 %fusion.29 = f32[4,8,256,128]{3,1,2,0:T(8,128)S(1)} fusion(f32[32,32]{1,0:T(8,128)S(1)} %fusion.31, f32[4,8,256,128]{3,2,1,0:T(8,128)} %bitcast.62, f32[32768]{0:T(1024)S(1)} %multiply_bitcast_fusion), kind=kOutput, calls=%fused_computation.40 | convolution fusion | flops 404750336 | bytes 8523776 | tf_op jit(solution)/shard_map/dot_general | solution.py:129
  191.8 2.8 %copy.186 = f32[4,8,256,128]{3,2,1,0:T(8,128)} copy(f32[4,8,256,128]{3,1,2,0:T(8,128)S(1)} %fusion.29) | data formatting | bytes 8388608
  (57 shorter events, 13.7 us)
Async XLA Ops:
  7.2 100.1 %copy-start = (bf16[48,128,128]{2,1,0:T(8,128)(2,1)S(1)}, bf16[48,128,128]{2,1,0:T(8,128)(2,1)}, u32[]{:S(2)}) copy-start(bf16[48,128,128]{2,1,0:T(8,128)(2,1)} %param.19) | copy-start | bytes 4718596
  7.2 126.0 %reduce-scatter.2.cloned.1.call-start = ((), (), s32[]{:S(2)}) async-start(), calls=%async_computation.1 | async-start | bytes 327680 | tf_op jit(solution)/shard_map/reduce_scatter | solution.py:120
  18.6 18.2 %copy-start.3 = (f32[32,8,128]{2,1,0:T(8,128)S(1)}, f32[32,8,128]{2,1,0:T(8,128)}, u32[]{:S(2)}) copy-start(f32[32,8,128]{2,1,0:T(8,128)} %param.15) | copy-start | bytes 393220
  18.6 18.2 %copy-start.8 = (s32[48]{0:T(128)S(1)}, s32[48]{0:T(128)}, u32[]{:S(2)}) copy-start(s32[48]{0:T(128)} %param.17) | copy-start | bytes 580
  18.6 18.3 %copy-start.4 = (f32[32,8,128]{2,1,0:T(8,128)S(1)}, f32[32,8,128]{2,1,0:T(8,128)}, u32[]{:S(2)}) copy-start(f32[32,8,128]{2,1,0:T(8,128)} %param.13) | copy-start | bytes 393220
  18.6 19.9 %collective-permute-start = (f32[32,32,8,1]{1,2,3,0:T(8,128)S(1)}, f32[32,32,8,1]{1,2,3,0:T(8,128)}, u32[]{:S(2)}, u32[]{:S(2)}) collective-permute-start(f32[32,32,8,1]{1,2,3,0:T(8,128)S(1)} %copy.180), channel_id=1, source_target_pairs={{0,4},{4,8},{8,12},{12,16},{16,20},{20,24},{24,28},{28,0},{1,5},{5... | collective-permute-start | bytes 98312 | tf_op jit(solution)/shard_map/ppermute | solution.py:24
  25.5 16.8 %collective-permute-start.1 = (f32[32,32,8,1]{1,2,3,0:T(8,128)}, f32[32,32,8,1]{1,2,3,0:T(8,128)}, u32[]{:S(2)}, u32[]{:S(2)}) collective-permute-start(f32[32,32,8,1]{1,2,3,0:T(8,128)} %copy.181), channel_id=1, source_target_pairs={{4,0},{8,4},{12,8},{16,12},{20,16},{24,20},{28,24},{0,28},{5,1},{9... | collective-permute-start | bytes 98312 | tf_op jit(solution)/shard_map/ppermute | solution.py:25
  34.0 12.1 %collective-permute-start.2 = (f32[32,32,1,128]{3,1,2,0:T(8,128)}, f32[32,32,1,128]{3,1,2,0:T(8,128)S(1)}, u32[]{:S(2)}, u32[]{:S(2)}) collective-permute-start(f32[32,32,1,128]{3,1,2,0:T(8,128)} %bitcast.20), channel_id=1, source_target_pairs={{0,1},{1,2},{2,3},{4,5},{5,6},{6,7},{8,9},{9,10},{10,11},{12,13},{... | collective-permute-start | bytes 1572872 | tf_op jit(solution)/shard_map/ppermute | solution.py:24
  35.5 10.7 %collective-permute-start.3 = (f32[32,32,1,128]{3,1,2,0:T(8,128)}, f32[32,32,1,128]{3,1,2,0:T(8,128)S(1)}, u32[]{:S(2)}, u32[]{:S(2)}) collective-permute-start(f32[32,32,1,128]{3,1,2,0:T(8,128)} %bitcast.21), channel_id=1, source_target_pairs={{1,0},{2,1},{3,2},{5,4},{6,5},{7,6},{9,8},{10,9},{11,10},{13,12},{... | collective-permute-start | bytes 1572872 | tf_op jit(solution)/shard_map/ppermute | solution.py:25
  38.5 7.7 %copy-start.2 = (f32[32,8,128]{2,1,0:T(8,128)S(1)}, f32[32,8,128]{2,1,0:T(8,128)}, u32[]{:S(2)}) copy-start(f32[32,8,128]{2,1,0:T(8,128)} %param.14) | copy-start | bytes 393220
  58.8 13.3 %copy-start.1 = (f32[32,32,8,128]{3,2,1,0:T(8,128)}, f32[32,32,8,128]{3,2,1,0:T(8,128)S(1)}, u32[]{:S(2)}) copy-start(f32[32,32,8,128]{3,2,1,0:T(8,128)S(1)} %fusion.19) | copy-start | bytes 12582916
  61.2 30.4 %collective-permute-start.6 = (f32[32,32,1,128]{3,1,2,0:T(8,128)}, f32[32,32,1,128]{3,1,2,0:T(8,128)S(1)}, u32[]{:S(2)}, u32[]{:S(2)}) collective-permute-start(f32[32,32,1,128]{3,1,2,0:T(8,128)} %bitcast.2), channel_id=1, source_target_pairs={{0,1},{1,2},{2,3},{4,5},{5,6},{6,7},{8,9},{9,10},{10,11},{12,13},{... | collective-permute-start | bytes 1572872 | tf_op jit(solution)/shard_map/ppermute | solution.py:24
  65.9 25.7 %collective-permute-start.7 = (f32[32,32,1,128]{3,1,2,0:T(8,128)}, f32[32,32,1,128]{3,1,2,0:T(8,128)S(1)}, u32[]{:S(2)}, u32[]{:S(2)}) collective-permute-start(f32[32,32,1,128]{3,1,2,0:T(8,128)} %bitcast.4), channel_id=1, source_target_pairs={{1,0},{2,1},{3,2},{5,4},{6,5},{7,6},{9,8},{10,9},{11,10},{13,12},{... | collective-permute-start | bytes 1572872 | tf_op jit(solution)/shard_map/ppermute | solution.py:25
  75.3 8.6 %collective-permute-start.4 = (f32[32,32,8,1]{1,2,3,0:T(8,128)S(1)}, f32[32,32,8,1]{1,2,3,0:T(8,128)}, u32[]{:S(2)}, u32[]{:S(2)}) collective-permute-start(f32[32,32,8,1]{1,2,3,0:T(8,128)S(1)} %copy.166), channel_id=1, source_target_pairs={{0,4},{4,8},{8,12},{12,16},{16,20},{20,24},{24,28},{28,0},{1,5},{5... | collective-permute-start | bytes 98312 | tf_op jit(solution)/shard_map/ppermute | solution.py:24
  79.2 8.5 %collective-permute-start.5 = (f32[32,32,8,1]{1,2,3,0:T(8,128)}, f32[32,32,8,1]{1,2,3,0:T(8,128)}, u32[]{:S(2)}, u32[]{:S(2)}) collective-permute-start(f32[32,32,8,1]{1,2,3,0:T(8,128)} %copy.168), channel_id=1, source_target_pairs={{4,0},{8,4},{12,8},{16,12},{20,16},{24,20},{28,24},{0,28},{5,1},{9... | collective-permute-start | bytes 98312 | tf_op jit(solution)/shard_map/ppermute | solution.py:25
  91.6 16.3 %copy-start.7 = (s32[48]{0:T(128)S(1)}, s32[48]{0:T(128)}, u32[]{:S(2)}) copy-start(s32[48]{0:T(128)} %param.18) | copy-start | bytes 580
  106.6 27.5 %copy-start.5 = (f32[512]{0:T(512)S(1)}, f32[512]{0:T(512)}, u32[]{:S(2)}) copy-start(f32[512]{0:T(512)} %param.20) | copy-start | bytes 6148
  106.6 27.5 %copy-start.6 = (f32[512]{0:T(512)S(1)}, f32[512]{0:T(512)}, u32[]{:S(2)}) copy-start(f32[512]{0:T(512)} %param.21) | copy-start | bytes 6148
Sparse Core Ops, SparseCore 0:
  109.8 23.3 reduce-scatter.1
where the time goes:
time: 202 us; the launch traced here: 201 us
  local copies, waits for them, and re-layouts  54.5 us (27%)
  blocking collectives  39.5 us (20%)
  other arithmetic  36.8 us (18%)
  waiting for transfers between devices  23.6 us (12%)
  starting transfers between devices  19.7 us (10%)
  between operations  14.9 us (7%)
  matrix products  12.5 us (6%)
    psum x1, blocking collectives, per_device(): gram_sum, pull_sum = lax.psum((gram_sum, pull_sum), ('lon', 'lat'))  39.5 us
    slice x5, local copies, waits for them, and re-layouts, extended(): last = lax.slice_in_dim(x, length - width, length, axis=dim)  24 us
    reduce_scatter x1, waiting for transfers between devices, per_device(): lax.psum_scatter(summed, 'lat', scatter_dimension=1, tiled=True)  23.5 us
    reduce_sum x1, other arithmetic, per_device(): centre = jnp.mean(raveled_grid_vector, axis=0)  15 us
    add x1, other arithmetic, advance(): return (1.0 - loss_rate) * advected + source  12.7 us
    unnamed x22, local copies, waits for them, and re-layouts  10.7 us
    ppermute x4, starting transfers between devices, extended(): after = lax.ppermute(initial, axis, down)  10.4 us
    ppermute x4, starting transfers between devices, extended(): before = lax.ppermute(last, axis, up)  9.26 us
  transfers between devices with their start and end apart: 9, of which 1 were waited for; matrix products, arithmetic and copies ran while one was open for 19% of the time, Pallas kernels for 0%

commit v1 on v0

v1 whole, which is shorter than its diff:
```python
import functools
import math

import jax
import jax.numpy as jnp
from jax import lax
from jax.experimental import pallas as pl
from jax.experimental.pallas import tpu as pltpu
from jax.sharding import PartitionSpec as P

SUB = 8
F32 = jnp.float32
BF16 = jnp.bfloat16
VMEM = pltpu.VMEM
SMEM = pltpu.SMEM
ANY = pl.ANY


def lanes_of(shape):
    return lax.broadcasted_iota(jnp.int32, shape, 1)


def subs_of(shape):
    return lax.broadcasted_iota(jnp.int32, shape, 0)


def pack_kernel(dims, chunks, x_hbm, e_hbm, n_hbm, p_hbm, d_hbm, north_hbm, south_hbm, edge_hbm,
                xs, fields, north, south, edge, in_sem, field_sem, out_sem):
    members, levels, rows, width = dims
    per = levels // chunks
    step = width // levels
    field_refs = (e_hbm, n_hbm, p_hbm, d_hbm)

    def load(c):
        return pltpu.make_async_copy(x_hbm.at[:, pl.ds(c * per, per)], xs.at[c], in_sem.at[c])

    def load_field(f):
        return pltpu.make_async_copy(field_refs[f], fields.at[f], field_sem.at[f])

    for f in range(4):
        load_field(f).start()
    for c in range(chunks):
        load(c).start()
    lane = lanes_of((SUB, width))
    level_of = ((lane + 2) // step) % levels
    edge[...] = jnp.zeros_like(edge)
    for f in range(4):
        load_field(f).wait()
    state_rows = 2 * levels * members
    for f in range(4):
        flat = fields.at[f]
        north[pl.ds(state_rows + f * levels, levels), :] = flat[pl.ds(rows - 1, levels, stride=rows), :]
        south[pl.ds(state_rows + f * levels, levels), :] = flat[pl.ds(0, levels, stride=rows), :]
        acc = jnp.zeros((SUB, width), F32)
        for l in range(levels):
            v = flat[pl.ds(l * rows, rows), :]
            acc = jnp.where(level_of == l, pltpu.roll(v, (step * l) % width, 1), acc)
        edge[pl.ds(rows * members + f * rows, rows), :] = acc

    def send(ref, hbm, c, k):
        part = pl.ds(c * per * 2 * members, per * 2 * members)
        return pltpu.make_async_copy(ref.at[part], hbm.at[part], out_sem.at[k, c])

    def send_tail(ref, hbm, k):
        part = pl.ds(state_rows, 4 * levels)
        return pltpu.make_async_copy(ref.at[part], hbm.at[part], out_sem.at[k, chunks])

    send_tail(north, north_hbm, 0).start()
    send_tail(south, south_hbm, 1).start()
    for c in range(chunks):
        load(c).wait()
        flat = xs.at[c].reshape(members * per * rows, width)

        def group(g, carry):
            for y in range(rows):
                at = pl.ds(pl.multiple_of(y * members + g * SUB, SUB), SUB)
                acc = edge[at, :]
                for li in range(per):
                    l = c * per + li
                    v = flat[pl.ds(g * SUB * per * rows + li * rows + y, SUB, stride=per * rows), :]
                    acc = jnp.where(level_of == l, pltpu.roll(v, (step * l) % width, 1), acc)
                    if y < 2:
                        south[pl.ds(pl.multiple_of((l * 2 + y) * members + g * SUB, SUB), SUB), :] = v
                    if y >= rows - 2:
                        north[pl.ds(pl.multiple_of((l * 2 + y - rows + 2) * members + g * SUB, SUB), SUB), :] = v
                edge[at, :] = acc
            return carry

        lax.fori_loop(0, members // SUB, group, 0)
        send(north, north_hbm, c, 0).start()
        send(south, south_hbm, c, 1).start()
    last = pltpu.make_async_copy(edge, edge_hbm, out_sem.at[2, 0])
    last.start()
    for c in range(chunks):
        send(north, north_hbm, c, 0).wait()
        send(south, south_hbm, c, 1).wait()
    send_tail(north, north_hbm, 0).wait()
    send_tail(south, south_hbm, 1).wait()
    last.wait()


def pack(x, fields, chunks=4):
    members, levels, rows, width = x.shape
    halo = 2 * levels * members + 4 * levels
    edge = rows * members + 4 * rows
    per = levels // chunks
    return pl.pallas_call(
        functools.partial(pack_kernel, x.shape, chunks),
        name="pack_halos",
        out_shape=(
            jax.ShapeDtypeStruct((halo, width), F32),
            jax.ShapeDtypeStruct((halo, width), F32),
            jax.ShapeDtypeStruct((edge, width), F32),
        ),
        in_specs=[pl.BlockSpec(memory_space=ANY)] * 5,
        out_specs=[pl.BlockSpec(memory_space=ANY)] * 3,
        scratch_shapes=[
            VMEM((chunks, members, per, rows, width), F32),
            VMEM((4, levels * rows, width), F32),
            VMEM((halo, width), F32),
            VMEM((halo, width), F32),
            VMEM((edge, width), F32),
            pltpu.SemaphoreType.DMA((chunks,)),
            pltpu.SemaphoreType.DMA((4,)),
            pltpu.SemaphoreType.DMA((3, chunks + 1)),
        ],
        cost_estimate=pl.CostEstimate(flops=4_000_000, bytes_accessed=8_000_000, transcendentals=0),
    )(x, *fields)


def stencil(e, n, p, d):
    keep = 1.0 - d
    ep, em = jnp.maximum(e, 0.0), jnp.minimum(e, 0.0)
    np_, nm = jnp.maximum(n, 0.0), jnp.minimum(n, 0.0)
    return (
        keep * (1.0 - ep + em - np_ + nm),
        keep * ep,
        -(keep * em),
        keep * np_,
        -(keep * nm),
        p,
    )


def forecast_kernel(dims, per, lat_size, slots, blocks_dev,
                    slot_of, row_of, count,
                    x_ref, below_ref, above_ref, belowc_ref, abovec_ref,
                    e_ref, n_ref, p_ref, d_ref,
                    edge, west, east, corner_s, corner_n, pw_hbm,
                    f_ref, *rest):
    members, levels, rows, width = dims
    outs, (halo, halo1, coef, strip, content, content16, rays, pw, pw_sem) = rest[:lat_size], rest[lat_size:]
    step_id = pl.program_id(0)
    groups = members // SUB
    step = width // levels
    lane = lanes_of((SUB, width))
    first, final = lane == 0, lane == width - 1
    from_west = ((lane + 2) % step) < 2
    tall = 2 * rows

    def tile(ref, start):
        return ref[pl.ds(pl.multiple_of(start, SUB), SUB), :]

    def spread(ref, k, row):
        return ref[k, pl.ds(row, SUB, stride=0), :]

    @pl.when(step_id == 0)
    def _():
        pltpu.make_async_copy(pw_hbm, pw, pw_sem).start()
        for g in range(groups):
            halo[pl.ds(g * SUB, SUB), :] = corner_s[pl.ds(g * SUB, SUB), :]
            halo[pl.ds((rows + 1) * members + g * SUB, SUB), :] = corner_n[pl.ds(g * SUB, SUB), :]
            for y in range(rows):
                at = pl.ds(y * members + g * SUB, SUB)
                halo[pl.ds((y + 1) * members + g * SUB, SUB), :] = jnp.where(from_west, west[at, :], east[at, :])
        merged = []
        for f in range(4):
            at = pl.ds(rows * members + f * rows, rows)
            merged.append(jnp.where(from_west, west[at, :], east[at, :]))
        for k, c in enumerate(stencil(*merged)):
            strip[k] = c
        for y in range(rows):
            c0, cw, ce, cs, cn, p = [spread(strip, k, y) for k in range(6)]
            for g in range(groups):
                at = pl.ds(y * members + g * SUB, SUB)
                own, aw, ae = edge[at, :], west[at, :], east[at, :]
                side_w = jnp.where(from_west, pltpu.roll(aw, 1, 1), pltpu.roll(own, 1, 1))
                side_e = jnp.where(from_west, pltpu.roll(own, width - 1, 1), pltpu.roll(ae, width - 1, 1))
                mid = halo[pl.ds((y + 1) * members + g * SUB, SUB), :]
                low = halo[pl.ds(y * members + g * SUB, SUB), :]
                high = halo[pl.ds((y + 2) * members + g * SUB, SUB), :]
                halo1[at, :] = (c0 * mid + cw * side_w) + (ce * side_e + cs * low) + (cn * high + p)
        content[...] = jnp.zeros_like(content)

    here = [r[...] for r in (e_ref, n_ref, p_ref, d_ref)]
    for li in range(per):
        part = slice(li * rows, (li + 1) * rows)
        for k, c in enumerate(stencil(*[h[part] for h in here])):
            coef[k, pl.ds(li * tall, rows), :] = c
    base = pl.multiple_of(step_id * per, per)
    for source, row in ((abovec_ref, rows), (belowc_ref, rows + 1)):
        got = [source[pl.ds(f * levels + base, per), :] for f in range(4)]
        for k, c in enumerate(stencil(*got)):
            coef[k, pl.ds(row, per, stride=tall), :] = c
    flat = x_ref.reshape(members * per * rows, width)

    def level(li, carry):
        l = base + li
        turn = (width - step * l) % width

        def coefs(y):
            row = li * tall + (y if y >= 0 else rows + 1)
            return [spread(coef, k, row) for k in range(6)]

        def start_row(y):
            if y < 0:
                return [tile(below_ref, (li * 2 + y + 2) * members + g * SUB) for g in range(groups)]
            if y >= rows:
                return [tile(above_ref, (li * 2 + y - rows) * members + g * SUB) for g in range(groups)]
            return [
                flat[pl.ds(g * SUB * per * rows + li * rows + y, SUB, stride=per * rows), :]
                for g in range(groups)
            ]

        def advance(mid, low, high, side, c):
            c0, cw, ce, cs, cn, p = c
            out = []
            for g in range(groups):
                edge_values = pltpu.roll(side[g], turn, 1)
                v = mid[g]
                w = pltpu.roll(jnp.where(final, edge_values, v), 1, 1)
                e = pltpu.roll(jnp.where(first, edge_values, v), width - 1, 1)
                out.append((c0 * v + cw * w) + (ce * e + cs * low[g]) + (cn * high[g] + p))
            return out

        before, now = start_row(-2), start_row(-1)
        older, old, older_c = None, None, None
        for y in range(-1, rows + 1):
            after = start_row(y + 1)
            c = coefs(y)
            side = [tile(halo, (y + 1) * members + g * SUB) for g in range(groups)]
            new = advance(now, before, after, side, c)
            if older is not None:
                y2 = y - 1
                side1 = [tile(halo1, y2 * members + g * SUB) for g in range(groups)]
                done = advance(old, older, new, side1, older_c)
                for g in range(groups):
                    at = pl.ds(y2 * members + g * SUB, SUB)
                    content[at, :] += done[g]
                    f_ref[pl.ds(pl.multiple_of((li * rows + y2) * members + g * SUB, SUB), SUB), :] = done[g]
            older, old, older_c = old, new, c
            before, now = now, after
        return carry

    lax.fori_loop(0, per, level, 0)

    @pl.when(step_id == pl.num_programs(0) - 1)
    def _():
        content16[...] = (content[...] / math.sqrt(levels)).astype(BF16)
        rays[...] = jnp.zeros_like(rays)
        pltpu.make_async_copy(pw_hbm, pw, pw_sem).wait()
        live = count[0]
        for k in range(slots):
            picked = content16[pl.ds(pl.multiple_of(row_of[k] * members, members), members), :]
            partial = jnp.dot(picked, pw[k], preferred_element_type=F32)
            partial = jnp.where(k < live, partial, 0.0)
            at = pl.ds(pl.multiple_of(slot_of[k] * members, members), members)
            rays[at, :] += partial
        size = blocks_dev * members
        for s in range(lat_size):
            outs[s][...] = rays[pl.ds(s * size, size), :]


def forecast(x, fields, below, above, edge, west, east, corner_s, corner_n, pw, slot_of, row_of, count,
             lat_size, blocks_dev, per=4):
    members, levels, rows, width = x.shape
    slots, _, block = pw.shape
    halo_rows = per * 2 * members
    tail = (2 * levels * members) // (4 * levels)
    whole = lambda shape: pl.BlockSpec(shape, lambda i: (0,) * len(shape))
    smem = pl.BlockSpec(memory_space=SMEM)
    field = pl.BlockSpec((per * rows, width), lambda i: (i, 0))
    size = blocks_dev * members
    return pl.pallas_call(
        functools.partial(forecast_kernel, x.shape, per, lat_size, slots, blocks_dev),
        name="forecast_rays",
        grid=(levels // per,),
        out_shape=[jax.ShapeDtypeStruct((levels * rows * members, width), F32)]
        + [jax.ShapeDtypeStruct((size, block), F32)] * lat_size,
        in_specs=[smem, smem, smem,
                  pl.BlockSpec((members, per, rows, width), lambda i: (0, i, 0, 0)),
                  pl.BlockSpec((halo_rows, width), lambda i: (i, 0)),
                  pl.BlockSpec((halo_rows, width), lambda i: (i, 0)),
                  pl.BlockSpec((4 * levels, width), lambda i: (tail, 0)),
                  pl.BlockSpec((4 * levels, width), lambda i: (tail, 0)),
                  field, field, field, field,
                  whole(edge.shape), whole(edge.shape), whole(edge.shape),
                  whole(corner_s.shape), whole(corner_s.shape),
                  pl.BlockSpec(memory_space=ANY)],
        out_specs=[pl.BlockSpec((per * rows * members, width), lambda i: (i, 0))] + [whole((size, block))] * lat_size,
        scratch_shapes=[
            VMEM(((rows + 2) * members, width), F32),
            VMEM((rows * members, width), F32),
            VMEM((6, per * 2 * rows, width), F32),
            VMEM((6, rows, width), F32),
            VMEM((rows * members, width), F32),
            VMEM((rows * members, width), BF16),
            VMEM((lat_size * size, block), F32),
            VMEM(pw.shape, BF16),
            pltpu.SemaphoreType.DMA,
        ],
        cost_estimate=pl.CostEstimate(flops=60_000_000, bytes_accessed=12_000_000, transcendentals=0),
    )(slot_of, row_of, count, x, below, above, below, above, *fields, edge, west, east, corner_s, corner_n, pw)


def spread_kernel(members, rows, width, pairs, f_ref, hi_ref, lo_ref, centre_ref):
    sub = subs_of((rows, width))
    for q in range(pairs):
        for h in range(2):
            mean = jnp.zeros((rows, width), F32)
            for y in range(rows):
                at = ((q * 2 + h) * rows + y) * members
                v = f_ref[pl.ds(at, members), :]
                m = jnp.sum(v, axis=0, keepdims=True) / members
                mean = jnp.where(sub == y, m, mean)
                a = v - m
                hi = a.astype(BF16)
                to = (q, pl.ds(y * members, members), pl.ds(h * width, width))
                hi_ref[to] = hi
                lo_ref[to] = (a - hi.astype(F32)).astype(BF16)
            centre_ref[pl.ds((q * 2 + h) * rows, rows), :] = mean


def anomalies(f, members, levels, rows, width, pairs=2):
    shape = (levels // 2, rows * members, 2 * width)
    block = (pairs, rows * members, 2 * width)
    return pl.pallas_call(
        functools.partial(spread_kernel, members, rows, width, pairs),
        name="anomalies",
        grid=(levels // 2 // pairs,),
        out_shape=(jax.ShapeDtypeStruct(shape, BF16), jax.ShapeDtypeStruct(shape, BF16),
                   jax.ShapeDtypeStruct((levels * rows, width), F32)),
        in_specs=[pl.BlockSpec((pairs * 2 * rows * members, width), lambda i: (i, 0))],
        out_specs=[pl.BlockSpec(block, lambda i: (i, 0, 0)), pl.BlockSpec(block, lambda i: (i, 0, 0)),
                   pl.BlockSpec((pairs * 2 * rows, width), lambda i: (i, 0))],
        cost_estimate=pl.CostEstimate(flops=8_000_000, bytes_accessed=8_000_000, transcendentals=0),
    )(f)


def moments_kernel(members, blocks_dev, block, n_parts, *refs):
    parts, (obs_ref, var_ref, prior_ref, innov_ref, packed_ref) = refs[:n_parts], refs[n_parts:]
    scaled, both = [], []
    for b in range(blocks_dev):
        at = pl.ds(b * members, members)
        total = parts[0][at, :]
        for part in parts[1:]:
            total = total + part[at, :]
        prior_ref[:, pl.ds(b * block, block)] = total
        mean = jnp.sum(total, axis=0, keepdims=True) / members
        dev = total - mean
        var = var_ref[pl.ds(b, 1), :]
        misfit = obs_ref[pl.ds(b, 1), :] - mean
        innov_ref[pl.ds(b, 1), :] = misfit / jnp.sqrt(var)
        scaled.append(dev / var)
        both.append(jnp.concatenate([dev, jnp.broadcast_to(misfit, (SUB, block))], axis=0))
    left = jnp.concatenate(scaled, axis=1)
    right = jnp.concatenate(both, axis=1)
    g = lax.dot_general(left, right, (((1,), (1,)), ((), ())), precision=lax.Precision.HIGHEST,
                        preferred_element_type=F32)
    wide = jnp.concatenate([g, jnp.zeros((members, 128 - g.shape[1]), F32)], axis=1)
    lane = lanes_of((SUB, 128))
    packed = jnp.zeros((SUB, 128), F32)
    groups = members // SUB
    start = 0
    for i in range(groups):
        v = wide[i * SUB:(i + 1) * SUB]
        stop = start + SUB * (i + 1)
        moved = pltpu.roll(v, start, 1) if start else v
        packed = jnp.where((lane >= start) & (lane < stop), moved, packed)
        start = stop
    for i in range(groups):
        v = wide[i * SUB:(i + 1) * SUB]
        packed = jnp.where(lane == start + i, pltpu.roll(v, start + i - members, 1), packed)
    packed_ref[...] = packed


def moments(parts, obs, var, members, blocks_dev, block):
    whole = pl.BlockSpec(memory_space=VMEM)
    return pl.pallas_call(
        functools.partial(moments_kernel, members, blocks_dev, block, len(parts)),
        name="moments",
        out_shape=(jax.ShapeDtypeStruct((members, blocks_dev * block), F32),
                   jax.ShapeDtypeStruct((blocks_dev, block), F32),
                   jax.ShapeDtypeStruct((SUB, 128), F32)),
        in_specs=[whole] * (len(parts) + 2),
        out_specs=[whole] * 3,
        cost_estimate=pl.CostEstimate(flops=4_000_000, bytes_accessed=400_000, transcendentals=0),
    )(*parts, obs, var)


def weights(gathered, members, devices):
    groups = members // SUB
    lane = lanes_of((SUB, 128))
    sub = subs_of((SUB, 128))
    total = gathered[pl.ds(0, SUB), :]
    for d in range(1, devices):
        total = total + gathered[pl.ds(d * SUB, SUB), :]
    lower, start = [], 0
    for i in range(groups):
        v = pltpu.roll(total, (128 - start) % 128, 1) if start else total
        lower.append(jnp.where(lane < SUB * (i + 1), v, 0.0))
        start += SUB * (i + 1)
    upper = jnp.transpose(jnp.concatenate(lower, axis=0))
    upper = upper[:members]
    upper = jnp.concatenate([upper, jnp.zeros((members, 128 - members), F32)], axis=1)
    rows = []
    for i in range(groups):
        a = jnp.where(lane < SUB * (i + 1), lower[i], upper[i * SUB:(i + 1) * SUB])
        a = jnp.where(lane < members, a, 0.0)
        a = a + jnp.where(lane == sub + SUB * i, members - 1.0, 0.0)
        a = jnp.where(lane == members + sub + SUB * i, 1.0, a)
        pull = pltpu.roll(total, (2 * members - start - i) % 128, 1)
        rows.append(jnp.where(lane == 2 * members, pull, a))
    for k in range(members):
        i0, s = divmod(k, SUB)
        pivot_row = jnp.broadcast_to(rows[i0][s:s + 1, :], (SUB, 128))
        pivot = jnp.broadcast_to(pivot_row[:, k:k + 1], (SUB, 128))
        ratio = pivot_row / pivot
        for i in range(i0, groups):
            if i == i0 and s == SUB - 1:
                continue
            factor = jnp.broadcast_to(rows[i][:, k:k + 1], (SUB, 128))
            if i == i0:
                factor = jnp.where(sub > s, factor, 0.0)
            rows[i] = rows[i] - factor * ratio
    mean_weight = jnp.zeros((SUB, 128), F32)
    for i in range(groups):
        pivot = jnp.sum(jnp.where(lane == sub + SUB * i, rows[i], 0.0), axis=1, keepdims=True)
        rows[i] = rows[i] / jnp.sqrt(pivot)
        mean_weight = mean_weight + rows[i] * rows[i][:, 2 * members:2 * members + 1]
    mean_weight = jnp.sum(mean_weight, axis=0, keepdims=True)
    return [mean_weight + math.sqrt(members - 1.0) * r for r in rows]


def update_kernel(dims, devices, pairs, gathered, hi_ref, lo_ref, centre_ref, out_ref, mat_hi, mat_lo):
    members, levels, rows, width = dims
    size = rows * members

    @pl.when(pl.program_id(0) == 0)
    def _():
        lane = lanes_of((rows, 128))
        sub = subs_of((rows, 128))
        copies = 128 // members
        made = weights(gathered, members, devices)
        for i, r in enumerate(made):
            r = jnp.where(lane < members, pltpu.roll(r, 128 - members, 1), 0.0)
            tiled = r
            for q in range(1, copies):
                tiled = tiled + pltpu.roll(r, q * members, 1)
            for s in range(0, SUB, 2):
                b = i * SUB + s
                for h in range(size // 128):
                    keep = (lane // members) + h * copies == sub
                    two = [jnp.where(keep, jnp.broadcast_to(tiled[t:t + 1], (rows, 128)), 0.0) for t in (s, s + 1)]
                    m = jnp.concatenate(two, axis=0)
                    big = m.astype(BF16)
                    to = (pl.ds(b * rows, 2 * rows), pl.ds(h * 128, 128))
                    mat_hi[to] = big
                    mat_lo[to] = (m - big.astype(F32)).astype(BF16)

    for q in range(pairs):
        hi, lo = hi_ref[q], lo_ref[q]
        big = mat_hi[...]
        dot = functools.partial(jnp.dot, preferred_element_type=F32)
        acc = dot(big, hi) + dot(big, lo) + dot(mat_lo[...], hi)
        for h in range(2):
            centre = centre_ref[pl.ds((q * 2 + h) * rows, rows), :]
            part = acc[:, h * width:(h + 1) * width].reshape(members, rows, width)
            out_ref[:, q * 2 + h] = part + centre[None]


def update(gathered, hi, lo, centre, dims, devices, pairs=2):
    members, levels, rows, width = dims
    block = (pairs, rows * members, 2 * width)
    return pl.pallas_call(
        functools.partial(update_kernel, dims, devices, pairs),
        name="update",
        grid=(levels // 2 // pairs,),
        out_shape=jax.ShapeDtypeStruct(dims, F32),
        in_specs=[pl.BlockSpec(gathered.shape, lambda i: (0, 0)),
                  pl.BlockSpec(block, lambda i: (i, 0, 0)), pl.BlockSpec(block, lambda i: (i, 0, 0)),
                  pl.BlockSpec((pairs * 2 * rows, width), lambda i: (i, 0))],
        out_specs=pl.BlockSpec((members, pairs * 2, rows, width), lambda i: (0, i, 0, 0)),
        scratch_shapes=[VMEM((rows * members, rows * members), BF16)] * 2,
        cost_estimate=pl.CostEstimate(flops=2_000_000_000, bytes_accessed=8_000_000, transcendentals=0),
    )(gathered, hi, lo, centre)


def per_device(sample_deviations, east_courant, north_courant, production, loss_rate, entry_count, entry_row,
               entry_block, path_weight, observed, obs_var):
    dims = members, levels, rows, width = sample_deviations.shape
    lat_size, lon_size = lax.axis_size("lat"), lax.axis_size("lon")
    block = path_weight.shape[2]
    blocks_dev = observed.shape[0] // block
    step = width // levels
    ring = lambda n, s: [(i, (i + s) % n) for i in range(n)]
    up = [(i, i + 1) for i in range(lat_size - 1)]
    down = [(j, i) for i, j in up]

    fields = [f.reshape(levels * rows, width) for f in (east_courant, north_courant, production, loss_rate)]
    to_north, to_south, edge = pack(sample_deviations, fields)
    below = lax.ppermute(to_north, "lat", up)
    above = lax.ppermute(to_south, "lat", down)
    west = lax.ppermute(edge, "lon", ring(lon_size, 1))
    east = lax.ppermute(edge, "lon", ring(lon_size, lon_size - 1))
    from_west = ((jnp.arange(width) + 2) % step < 2)[None, :]
    top = slice((rows - 1) * members, rows * members)
    corner_s = lax.ppermute(jnp.where(from_west, west[top], east[top]), "lat", up)
    corner_n = lax.ppermute(jnp.where(from_west, west[:members], east[:members]), "lat", down)

    mine = lax.axis_index("lat")
    slot_of = ((entry_block // blocks_dev - mine) % lat_size) * blocks_dev + entry_block % blocks_dev
    f, *sums = forecast(sample_deviations, fields, below, above, edge, west, east, corner_s, corner_n, path_weight,
                        slot_of, entry_row, entry_count, lat_size, blocks_dev)
    got = [sums[0]] + [lax.ppermute(sums[s], "lat", ring(lat_size, s)) for s in range(1, lat_size)]
    hi, lo, centre = anomalies(f, members, levels, rows, width)
    prior, innovation, packed = moments(got, observed.reshape(blocks_dev, block), obs_var.reshape(blocks_dev, block),
                                        members, blocks_dev, block)
    devices = lat_size * lon_size
    spread_out = jnp.broadcast_to(packed[None], (devices, SUB, 128)).reshape(devices * SUB, 128)
    gathered = lax.all_to_all(spread_out, ("lon", "lat"), 0, 0, tiled=True)
    updated = update(gathered, hi, lo, centre, dims, devices)
    return updated, prior, innovation.reshape(observed.shape)


def solution(mesh):
    tile = P(None, "lat", "lon")
    owned = P(("lon", "lat"))
    in_specs = (P(None, None, "lat", "lon"), tile, tile, tile, tile, owned, owned, owned,
                P(("lon", "lat"), None, None), owned, owned)
    out_specs = (P(None, None, "lat", "lon"), P(None, ("lon", "lat")), owned)
    return jax.shard_map(per_device, mesh=mesh, in_specs=in_specs, out_specs=out_specs, check_vma=False)
```

time: 202 us -> 94.8 us (0.47)
  Pallas kernels: 0 us -> 53.1 us
  local copies, waits for them, and re-layouts: 54.5 us -> 4.61 us
  blocking collectives: 39.5 us -> 0 us
  other arithmetic: 36.8 us -> 0.54 us
  between operations: 14.9 us -> 1.44 us
  matrix products: 12.5 us -> 0 us
  waiting for transfers between devices: 23.6 us -> 11.9 us
  starting transfers between devices: 19.7 us -> 22.4 us
    pallas_call x0 -> x5, Pallas kernels: none -> 53.1 us  [the longest x1 25.5 us: forecast(): pl.pallas_call(functools.partial(forecast_kernel, x.shape, per, lat_size,...]
    psum x1 -> x0, blocking collectives: 39.5 us -> none  [per_device(): gram_sum, pull_sum = lax.psum((gram_sum, pull_sum), ('lon', 'lat'))]
    slice x6 -> x0, local copies, waits for them, and re-layouts: 27.8 us -> none  [the longest x5 24 us: extended(): last = lax.slice_in_dim(x, length - width, length, axis=dim)]
    reduce_scatter x1 -> x0, waiting for transfers between devices: 23.5 us -> none  [per_device(): lax.psum_scatter(summed, 'lat', scatter_dimension=1, tiled=True)]
    reduce_sum x2 -> x0, other arithmetic: 15.8 us -> none  [the longest x1 15 us: per_device(): centre = jnp.mean(raveled_grid_vector, axis=0)]
    ppermute x4 -> x0, local copies, waits for them, and re-layouts: 15.3 us -> none  [the longest x2 7.66 us: extended(): after = lax.ppermute(initial, axis, down)]
    add x2 -> x1, other arithmetic: 12.7 us -> 0.53 us  [per_device(): (entry_block // blocks_dev - mine) % lat_size * blocks_dev]
    dot_general x5 -> x0, matrix products: 11.9 us -> none  [the longest x1 8.28 us: per_device(): jnp.dot(transform.T, anomalies, precision=highest)]
  transfers between devices with their start and end apart: 9 -> 10, of which waited for: 1 -> 5; matrix products, arithmetic and copies ran while one was open for 19% -> 1% of each run, Pallas kernels for 0% -> 7%
where the time goes in v1:
time: 94.8 us; the launch traced here: 94.1 us
  Pallas kernels  53.1 us (56%)
  starting transfers between devices  22.4 us (24%)
  waiting for transfers between devices  11.9 us (13%)
  local copies, waits for them, and re-layouts  4.61 us (5%)
  between operations  1.44 us (2%)
    pallas_call x1, Pallas kernels, forecast(): pl.pallas_call(functools.partial(forecast_kernel, x.shape, per, lat_size,...  25.5 us
    pallas_call x1, Pallas kernels, update(): pl.pallas_call(functools.partial(update_kernel, dims, devices, pairs), na...  12.2 us
    pallas_call x1, Pallas kernels, anomalies(): pl.pallas_call(functools.partial(spread_kernel, members, rows, width, pai...  7.04 us
    pallas_call x1, Pallas kernels, pack(): pl.pallas_call(functools.partial(pack_kernel, x.shape, chunks), name='pac...  6.59 us
    ppermute x3, starting transfers between devices, per_device(): lax.ppermute(sums[s], 'lat', ring(lat_size, s))  5.97 us
    ppermute x1, starting transfers between devices, per_device(): east = lax.ppermute(edge, 'lon', ring(lon_size, lon_size - 1))  5.43 us
    ppermute x1, waiting for transfers between devices, per_device(): west = lax.ppermute(edge, 'lon', ring(lon_size, 1))  5.35 us
    ppermute x1, starting transfers between devices, per_device(): lax.ppermute(jnp.where(from_west, west[top], east[top]), 'lat', up)  3.44 us
  transfers between devices with their start and end apart: 10, of which 5 were waited for; matrix products, arithmetic and copies ran while one was open for 1% of the time, Pallas kernels for 7%

profile of v1, /device:TPU:0, one launch (start us, length us, event | category | flops | bytes accessed | tf_op | source)
XLA Modules:
  0.0 94.1 jit_solution(2067289801009139576)
XLA Ops:
  0.6 6.6 %pack_halos.1 = (f32[2176,128]{1,0:T(8,128)}, f32[2176,128]{1,0:T(8,128)}, f32[288,128]{1,0:T(8,128)}) custom-call(f32[32,32,8,128]{3,2,1,0:T(8,128)} %x_ref.1, f32[256,128]{1,0:T(8,128)} %bitcast.8, f32[256,128]{1,0:T(8,128)} %bitcast.10, f32[256,128]{1,0:T(8,128)} %bitcast.12, f32[256,128]{1,0:T(8,128)} %bitcast.14), custom_call_target="tpu_custom_call" | custom-call | flops 4000000 | bytes 8000000 | tf_op jit(solution)/shard_map/pack_halos/pallas_call | solution.py:107
  7.2 2.5 %collective-permute-start = (f32[2176,128]{1,0:T(8,128)}, f32[2176,128]{1,0:T(8,128)S(1)}, u32[]{:S(2)}, u32[]{:S(2)}) collective-permute-start(f32[2176,128]{1,0:T(8,128)} %get-tuple-element.17), channel_id=1, source_target_pairs={{0,1},{1,2},{2,3},{4,5},{5,6},{6,7},{8,9},{9,10},{10,11},{12,13},{... | collective-permute-start | bytes 3342344 | tf_op jit(solution)/shard_map/ppermute | solution.py:512
  9.7 1.3 %collective-permute-start.1 = (f32[2176,128]{1,0:T(8,128)}, f32[2176,128]{1,0:T(8,128)S(1)}, u32[]{:S(2)}, u32[]{:S(2)}) collective-permute-start(f32[2176,128]{1,0:T(8,128)} %get-tuple-element.18), channel_id=1, source_target_pairs={{1,0},{2,1},{3,2},{5,4},{6,5},{7,6},{9,8},{10,9},{11,10},{13,12},{... | collective-permute-start | bytes 3342344 | tf_op jit(solution)/shard_map/ppermute | solution.py:513
  11.0 5.4 %collective-permute-start.3 = (f32[288,128]{1,0:T(8,128)}, f32[288,128]{1,0:T(8,128)S(1)}, u32[]{:S(2)}, u32[]{:S(2)}) collective-permute-start(f32[288,128]{1,0:T(8,128)} %get-tuple-element.19.edge), channel_id=1, source_target_pairs={{0,28},{4,0},{8,4},{12,8},{16,12},{20,16},{24,20},{28,24},{1,29},{... | collective-permute-start | bytes 442376 | tf_op jit(solution)/shard_map/ppermute | solution.py:515
  16.5 3.2 %collective-permute-done.3.east = f32[288,128]{1,0:T(8,128)S(1)} collective-permute-done((f32[288,128]{1,0:T(8,128)}, f32[288,128]{1,0:T(8,128)S(1)}, u32[]{:S(2)}, u32[]{:S(2)}) %collective-permute-start.3) | collective-permute-done | bytes 147488 | tf_op jit(solution)/shard_map/ppermute | solution.py:515
  19.6 5.4 %collective-permute-done.2.west = f32[288,128]{1,0:T(8,128)S(1)} collective-permute-done((f32[288,128]{1,0:T(8,128)}, f32[288,128]{1,0:T(8,128)S(1)}, u32[]{:S(2)}, u32[]{:S(2)}) %collective-permute-start.2) | collective-permute-done | bytes 147488 | tf_op jit(solution)/shard_map/ppermute | solution.py:514
  25.0 1.3 %collective-permute-start.5 = (f32[32,128]{1,0:T(8,128)S(1)}, f32[32,128]{1,0:T(8,128)S(1)}, u32[]{:S(2)}, u32[]{:S(2)}) collective-permute-start(f32[32,128]{1,0:T(8,128)S(1)} %get-tuple-element.31), channel_id=1, source_target_pairs={{1,0},{2,1},{3,2},{5,4},{6,5},{7,6},{9,8},{10,9},{11,10},{13,12},{... | collective-permute-start | bytes 49160 | tf_op jit(solution)/shard_map/ppermute | solution.py:519
  26.3 3.4 %collective-permute-start.4 = (f32[32,128]{1,0:T(8,128)S(1)}, f32[32,128]{1,0:T(8,128)S(1)}, u32[]{:S(2)}, u32[]{:S(2)}) collective-permute-start(f32[32,128]{1,0:T(8,128)S(1)} %get-tuple-element.32), channel_id=1, source_target_pairs={{0,1},{1,2},{2,3},{4,5},{5,6},{6,7},{8,9},{9,10},{10,11},{12,13},{... | collective-permute-start | bytes 49160 | tf_op jit(solution)/shard_map/ppermute | solution.py:518
  29.8 0.5 fusion.slot_of
  32.0 1.0 %copy-done.1 = f32[2176,128]{1,0:T(8,128)} copy-done((f32[2176,128]{1,0:T(8,128)}, f32[2176,128]{1,0:T(8,128)S(1)}, u32[]{:S(2)}) %copy-start.1) | copy-done | bytes 1114136
  33.0 25.5 %forecast_rays.1 = (f32[8192,128]{1,0:T(8,128)}, f32[128,128]{1,0:T(8,128)}, f32[128,128]{1,0:T(8,128)}, f32[128,128]{1,0:T(8,128)}, f32[128,128]{1,0:T(8,128)}) custom-call(s32[48]{0:T(128)} %fusion.slot_of, s32[48]{0:T(128)} %row_of.1, s32[1]{0:T(128)S(6)} %copy.14.count, f32[32,32,8,128]{3,2,1,0:T(8,128)} %x_ref.1, f32[2176,128]{1,0:T(8,128)} %copy-done, ...), custom_call_target="tpu_custom_call" | custom-call | flops 60000000 | bytes 12000000 | tf_op jit(solution)/shard_map/forecast_rays/pallas_call | solution.py:284
  58.5 2.7 %collective-permute-start.6 = (f32[128,128]{1,0:T(8,128)}, f32[128,128]{1,0:T(8,128)S(1)}, u32[]{:S(2)}, u32[]{:S(2)}) collective-permute-start(f32[128,128]{1,0:T(8,128)} %get-tuple-element.21), channel_id=1, source_target_pairs={{0,1},{1,2},{2,3},{3,0},{4,5},{5,6},{6,7},{7,4},{8,9},{9,10},{10,1... | collective-permute-start | bytes 196616 | tf_op jit(solution)/shard_map/ppermute | solution.py:525
  61.2 1.9 %collective-permute-start.7 = (f32[128,128]{1,0:T(8,128)}, f32[128,128]{1,0:T(8,128)S(1)}, u32[]{:S(2)}, u32[]{:S(2)}) collective-permute-start(f32[128,128]{1,0:T(8,128)} %get-tuple-element.22), channel_id=1, source_target_pairs={{0,2},{1,3},{2,0},{3,1},{4,6},{5,7},{6,4},{7,5},{8,10},{9,11},{10,... | collective-permute-start | bytes 196616 | tf_op jit(solution)/shard_map/ppermute | solution.py:525
  63.0 1.4 %collective-permute-start.8 = (f32[128,128]{1,0:T(8,128)}, f32[128,128]{1,0:T(8,128)S(1)}, u32[]{:S(2)}, u32[]{:S(2)}) collective-permute-start(f32[128,128]{1,0:T(8,128)} %get-tuple-element.23), channel_id=1, source_target_pairs={{0,3},{1,0},{2,1},{3,2},{4,7},{5,4},{6,5},{7,6},{8,11},{9,8},{10,9... | collective-permute-start | bytes 196616 | tf_op jit(solution)/shard_map/ppermute | solution.py:525
  64.4 1.4 %collective-permute-done.7.refs_2_ = f32[128,128]{1,0:T(8,128)S(1)} collective-permute-done((f32[128,128]{1,0:T(8,128)}, f32[128,128]{1,0:T(8,128)S(1)}, u32[]{:S(2)}, u32[]{:S(2)}) %collective-permute-start.7) | collective-permute-done | bytes 65568 | tf_op jit(solution)/shard_map/ppermute | solution.py:525
  65.8 0.8 collective-permute-done.8.refs_3_
  66.7 0.6 copy-done.7
  67.3 1.8 %moments.1 = (f32[32,512]{1,0:T(8,128)}, f32[4,128]{1,0:T(4,128)}, f32[8,128]{1,0:T(8,128)}) custom-call(f32[128,128]{1,0:T(8,128)} %get-tuple-element.20.refs_0_, f32[128,128]{1,0:T(8,128)} %copy-done.5, f32[128,128]{1,0:T(8,128)} %copy-done.6, f32[128,128]{1,0:T(8,128)} %copy-done.7, f32[4,128]{1,0:T(4,128)} %bitcast.17, f32[4,128]{1,0:T(4,128)} %bitcast.18), custom_call_target="tpu_custom_call" | custom-call | flops 4000000 | bytes 400000 | tf_op jit(solution)/shard_map/moments/pallas_call | solution.py:389
  69.1 1.3 %broadcast_in_dim.21 = f32[32,8,128]{2,1,0:T(8,128)} broadcast(f32[8,128]{1,0:T(8,128)} %get-tuple-element.24), dimensions={1,2} | broadcast | bytes 135168 | tf_op jit(solution)/shard_map/broadcast_in_dim | solution.py:530
  70.4 2.6 %all-to-all-start = ((f32[32,8,128]{2,1,0:T(8,128)}), f32[32,8,128]{2,1,0:T(8,128)S(1)}, u32[]{:S(2)}, u32[]{:S(2)}) async-start(f32[32,8,128]{2,1,0:T(8,128)} %broadcast_in_dim.21), calls=%async_computation | async-start | bytes 262144 | tf_op jit(solution)/shard_map/all_to_all | solution.py:531
  73.0 7.0 %anomalies.1 = (bf16[16,256,256]{2,1,0:T(8,128)(2,1)}, bf16[16,256,256]{2,1,0:T(8,128)(2,1)}, f32[256,128]{1,0:T(8,128)}) custom-call(f32[8192,128]{1,0:T(8,128)} %get-tuple-element.25.f_ref), custom_call_target="tpu_custom_call" | custom-call | flops 8000000 | bytes 8000000 | tf_op jit(solution)/shard_map/anomalies/pallas_call | solution.py:337
  80.0 1.2 %all-to-all-done = f32[32,8,128]{2,1,0:T(8,128)S(1)} async-done(((f32[32,8,128]{2,1,0:T(8,128)}), f32[32,8,128]{2,1,0:T(8,128)S(1)}, u32[]{:S(2)}, u32[]{:S(2)}) %all-to-all-start) | async-done | bytes 131104 | tf_op jit(solution)/shard_map/all_to_all | solution.py:531
  81.2 0.7 copy-done.2
  81.9 12.2 %update.1 = f32[32,32,8,128]{3,2,1,0:T(8,128)} custom-call(f32[256,128]{1,0:T(8,128)} %bitcast.16, bf16[16,256,256]{2,1,0:T(8,128)(2,1)} %get-tuple-element.26.hi_ref, bf16[16,256,256]{2,1,0:T(8,128)(2,1)} %get-tuple-element.27.lo_ref, f32[256,128]{1,0:T(8,128)} %get-tuple-element.28.centre_ref), custom_call_target="tpu_custom_call" | custom-call | flops 2000000000 | bytes 8000000 | tf_op jit(solution)/shard_map/update/pallas_call | solution.py:485
  (27 shorter events, 1.0 us)
Async XLA Ops:
  0.6 29.1 %copy-start.10 = (s32[48]{0:T(128)S(1)}, s32[48]{0:T(128)}, u32[]{:S(2)}) copy-start(s32[48]{0:T(128)} %param.18) | copy-start | bytes 580
  7.2 23.7 %collective-permute-start = (f32[2176,128]{1,0:T(8,128)}, f32[2176,128]{1,0:T(8,128)S(1)}, u32[]{:S(2)}, u32[]{:S(2)}) collective-permute-start(f32[2176,128]{1,0:T(8,128)} %get-tuple-element.17), channel_id=1, source_target_pairs={{0,1},{1,2},{2,3},{4,5},{5,6},{6,7},{8,9},{9,10},{10,11},{12,13},{... | collective-permute-start | bytes 3342344 | tf_op jit(solution)/shard_map/ppermute | solution.py:512
  9.7 21.3 %collective-permute-start.1 = (f32[2176,128]{1,0:T(8,128)}, f32[2176,128]{1,0:T(8,128)S(1)}, u32[]{:S(2)}, u32[]{:S(2)}) collective-permute-start(f32[2176,128]{1,0:T(8,128)} %get-tuple-element.18), channel_id=1, source_target_pairs={{1,0},{2,1},{3,2},{5,4},{6,5},{7,6},{9,8},{10,9},{11,10},{13,12},{... | collective-permute-start | bytes 3342344 | tf_op jit(solution)/shard_map/ppermute | solution.py:513
  11.0 8.6 %collective-permute-start.3 = (f32[288,128]{1,0:T(8,128)}, f32[288,128]{1,0:T(8,128)S(1)}, u32[]{:S(2)}, u32[]{:S(2)}) collective-permute-start(f32[288,128]{1,0:T(8,128)} %get-tuple-element.19.edge), channel_id=1, source_target_pairs={{0,28},{4,0},{8,4},{12,8},{16,12},{20,16},{24,20},{28,24},{1,29},{... | collective-permute-start | bytes 442376 | tf_op jit(solution)/shard_map/ppermute | solution.py:515
  16.4 8.5 %collective-permute-start.2 = (f32[288,128]{1,0:T(8,128)}, f32[288,128]{1,0:T(8,128)S(1)}, u32[]{:S(2)}, u32[]{:S(2)}) collective-permute-start(f32[288,128]{1,0:T(8,128)} %get-tuple-element.19.edge), channel_id=1, source_target_pairs={{0,4},{4,8},{8,12},{12,16},{16,20},{20,24},{24,28},{28,0},{1,5},{5... | collective-permute-start | bytes 442376 | tf_op jit(solution)/shard_map/ppermute | solution.py:514
  19.6 11.4 %copy-start.3 = (f32[288,128]{1,0:T(8,128)}, f32[288,128]{1,0:T(8,128)S(1)}, u32[]{:S(2)}) copy-start(f32[288,128]{1,0:T(8,128)S(1)} %collective-permute-done.3.east) | copy-start | bytes 442372
  25.0 6.0 %copy-start.4 = (f32[288,128]{1,0:T(8,128)}, f32[288,128]{1,0:T(8,128)S(1)}, u32[]{:S(2)}) copy-start(f32[288,128]{1,0:T(8,128)S(1)} %collective-permute-done.2.west) | copy-start | bytes 442372
  25.0 5.9 %collective-permute-start.5 = (f32[32,128]{1,0:T(8,128)S(1)}, f32[32,128]{1,0:T(8,128)S(1)}, u32[]{:S(2)}, u32[]{:S(2)}) collective-permute-start(f32[32,128]{1,0:T(8,128)S(1)} %get-tuple-element.31), channel_id=1, source_target_pairs={{1,0},{2,1},{3,2},{5,4},{6,5},{7,6},{9,8},{10,9},{11,10},{13,12},{... | collective-permute-start | bytes 49160 | tf_op jit(solution)/shard_map/ppermute | solution.py:519
  26.3 4.7 %collective-permute-start.4 = (f32[32,128]{1,0:T(8,128)S(1)}, f32[32,128]{1,0:T(8,128)S(1)}, u32[]{:S(2)}, u32[]{:S(2)}) collective-permute-start(f32[32,128]{1,0:T(8,128)S(1)} %get-tuple-element.32), channel_id=1, source_target_pairs={{0,1},{1,2},{2,3},{4,5},{5,6},{6,7},{8,9},{9,10},{10,11},{12,13},{... | collective-permute-start | bytes 49160 | tf_op jit(solution)/shard_map/ppermute | solution.py:518
  30.9 0.6 copy-start.8
  31.0 0.6 copy-start.9
  31.0 1.0 %copy-start = (f32[2176,128]{1,0:T(8,128)}, f32[2176,128]{1,0:T(8,128)S(1)}, u32[]{:S(2)}) copy-start(f32[2176,128]{1,0:T(8,128)S(1)} %collective-permute-done.below_ref.belowc_ref) | copy-start | bytes 3342340
  32.0 1.0 %copy-start.1 = (f32[2176,128]{1,0:T(8,128)}, f32[2176,128]{1,0:T(8,128)S(1)}, u32[]{:S(2)}) copy-start(f32[2176,128]{1,0:T(8,128)S(1)} %collective-permute-done.1.above_ref.abovec_ref) | copy-start | bytes 3342340
  58.5 6.0 %collective-permute-start.6 = (f32[128,128]{1,0:T(8,128)}, f32[128,128]{1,0:T(8,128)S(1)}, u32[]{:S(2)}, u32[]{:S(2)}) collective-permute-start(f32[128,128]{1,0:T(8,128)} %get-tuple-element.21), channel_id=1, source_target_pairs={{0,1},{1,2},{2,3},{3,0},{4,5},{5,6},{6,7},{7,4},{8,9},{9,10},{10,1... | collective-permute-start | bytes 196616 | tf_op jit(solution)/shard_map/ppermute | solution.py:525
  61.2 4.7 %collective-permute-start.7 = (f32[128,128]{1,0:T(8,128)}, f32[128,128]{1,0:T(8,128)S(1)}, u32[]{:S(2)}, u32[]{:S(2)}) collective-permute-start(f32[128,128]{1,0:T(8,128)} %get-tuple-element.22), channel_id=1, source_target_pairs={{0,2},{1,3},{2,0},{3,1},{4,6},{5,7},{6,4},{7,5},{8,10},{9,11},{10,... | collective-permute-start | bytes 196616 | tf_op jit(solution)/shard_map/ppermute | solution.py:525
  63.0 3.6 %collective-permute-start.8 = (f32[128,128]{1,0:T(8,128)}, f32[128,128]{1,0:T(8,128)S(1)}, u32[]{:S(2)}, u32[]{:S(2)}) collective-permute-start(f32[128,128]{1,0:T(8,128)} %get-tuple-element.23), channel_id=1, source_target_pairs={{0,3},{1,0},{2,1},{3,2},{4,7},{5,4},{6,5},{7,6},{8,11},{9,8},{10,9... | collective-permute-start | bytes 196616 | tf_op jit(solution)/shard_map/ppermute | solution.py:525
  64.4 2.2 %copy-start.5 = (f32[128,128]{1,0:T(8,128)}, f32[128,128]{1,0:T(8,128)S(1)}, u32[]{:S(2)}) copy-start(f32[128,128]{1,0:T(8,128)S(1)} %collective-permute-done.6.refs_1_) | copy-start | bytes 196612
  65.8 0.8 copy-start.6
  66.6 0.6 copy-start.7
  70.4 10.8 %all-to-all-start = ((f32[32,8,128]{2,1,0:T(8,128)}), f32[32,8,128]{2,1,0:T(8,128)S(1)}, u32[]{:S(2)}, u32[]{:S(2)}) async-start(f32[32,8,128]{2,1,0:T(8,128)} %broadcast_in_dim.21), calls=%async_computation | async-start | bytes 262144 | tf_op jit(solution)/shard_map/all_to_all | solution.py:531
  81.2 0.7 copy-start.2

commit v2 on v1

v2 whole, which is shorter than its diff:
```python
import functools
import math

import jax
import jax.numpy as jnp
from jax import lax
from jax.experimental import pallas as pl
from jax.experimental.pallas import tpu as pltpu
from jax.sharding import PartitionSpec as P


SUB = 8
F32 = jnp.float32
BF16 = jnp.bfloat16
VMEM = pltpu.VMEM
SMEM = pltpu.SMEM


def lanes_of(shape):
    return lax.broadcasted_iota(jnp.int32, shape, 1)


def subs_of(shape):
    return lax.broadcasted_iota(jnp.int32, shape, 0)


def grant(mib, flops, moved):
    return dict(
        compiler_params=pltpu.CompilerParams(vmem_limit_bytes=mib * 1024 * 1024),
        cost_estimate=pl.CostEstimate(flops=flops, bytes_accessed=moved, transcendentals=0),
    )


def near(*arrays):
    return [pltpu.with_memory_space_constraint(a, pltpu.VMEM) for a in arrays]


def far(*arrays):
    return [pltpu.with_memory_space_constraint(a, pltpu.HBM) for a in arrays]


IN_VMEM = pl.BlockSpec(memory_space=VMEM)
IN_SMEM = pl.BlockSpec(memory_space=SMEM)
IN_HBM = pl.BlockSpec(memory_space=pltpu.HBM)


def pack_kernel(dims, chunks, x_hbm, e_hbm, n_hbm, p_hbm, d_hbm, state, north, south, edge, fields,
                in_sem, field_sem, tail_sem):
    members, levels, rows, width = dims
    per = levels // chunks
    step = width // levels
    field_refs = (e_hbm, n_hbm, p_hbm, d_hbm)
    state_rows = 2 * levels * members

    def load(l, y):
        return pltpu.make_async_copy(x_hbm.at[:, l, y], state.at[l * rows + y], in_sem.at[l // per])

    def load_field(f):
        return pltpu.make_async_copy(field_refs[f], fields.at[f], field_sem.at[f])

    for f in range(4):
        load_field(f).start()
    for l in range(levels):
        for y in range(rows):
            load(l, y).start()
    lane = lanes_of((SUB, width))
    level_of = ((lane + 2) // step) % levels
    edge[...] = jnp.zeros_like(edge)
    for f in range(4):
        load_field(f).wait()
        acc = jnp.zeros((SUB, width), F32)
        for l in range(levels):
            acc = jnp.where(level_of == l, pltpu.roll(fields[f, l], (step * l) % width, 1), acc)
        edge[pl.ds(rows * members + f * rows, rows), :] = acc
        at = pl.ds(state_rows + f * levels, levels)
        pltpu.make_async_copy(fields.at[f, :, rows - 1], north.at[at], tail_sem.at[0, f]).start()
        pltpu.make_async_copy(fields.at[f, :, 0], south.at[at], tail_sem.at[1, f]).start()
    for c in range(chunks):
        first = c * per
        for l in range(first, first + per):
            for y in range(rows):
                load(l, y).wait()
        for l in range(first, first + per):
            for r in range(2):
                at = pl.ds((l * 2 + r) * members, members)
                south[at, :] = state[l * rows + r]
                north[at, :] = state[l * rows + rows - 2 + r]
        for y in range(rows):
            for g in range(members // SUB):
                at = pl.ds(y * members + g * SUB, SUB)
                acc = edge[at, :]
                for l in range(first, first + per):
                    v = state[l * rows + y, pl.ds(g * SUB, SUB), :]
                    acc = jnp.where(level_of == l, pltpu.roll(v, (step * l) % width, 1), acc)
                edge[at, :] = acc
    for f in range(4):
        at = pl.ds(state_rows + f * levels, levels)
        pltpu.make_async_copy(fields.at[f, :, rows - 1], north.at[at], tail_sem.at[0, f]).wait()
        pltpu.make_async_copy(fields.at[f, :, 0], south.at[at], tail_sem.at[1, f]).wait()


def pack(x, fields, chunks=4):
    members, levels, rows, width = x.shape
    halo = 2 * levels * members + 4 * levels
    edge = rows * members + 4 * rows
    return pl.pallas_call(
        functools.partial(pack_kernel, x.shape, chunks),
        name="pack_halos",
        out_shape=(
            VMEM((levels * rows, members, width), F32),
            VMEM((halo, width), F32),
            VMEM((halo, width), F32),
            VMEM((edge, width), F32),
            VMEM((4, levels, rows, width), F32),
        ),
        in_specs=[IN_HBM] * 5,
        out_specs=[IN_VMEM] * 5,
        scratch_shapes=[
            pltpu.SemaphoreType.DMA((chunks,)),
            pltpu.SemaphoreType.DMA((4,)),
            pltpu.SemaphoreType.DMA((2, 4)),
        ],
        **grant(8, 4_000_000, 8_000_000),
    )(*far(x, *fields))


def stencil(e, n, p, d):
    keep = 1.0 - d
    ep, em = jnp.maximum(e, 0.0), jnp.minimum(e, 0.0)
    np_, nm = jnp.maximum(n, 0.0), jnp.minimum(n, 0.0)
    return (
        keep * (1.0 - ep + em - np_ + nm),
        keep * ep,
        -(keep * em),
        keep * np_,
        -(keep * nm),
        p,
    )


def sided(side, turn, v, width):
    lane = lanes_of(v.shape)
    values = pltpu.roll(side, turn, 1)
    w = pltpu.roll(jnp.where(lane == width - 1, values, v), 1, 1)
    e = pltpu.roll(jnp.where(lane == 0, values, v), width - 1, 1)
    return w, e


def advance(mid, low, high, side, turn, c, width):
    c0, cw, ce, cs, cn, p = c
    out = []
    for g, v in enumerate(mid):
        w, e = sided(side[g], turn, v, width)
        total = (c0 * v + cw * w) + (ce * e + p)
        if low is not None:
            total = total + cs * low[g]
        if high is not None:
            total = total + cn * high[g]
        out.append(total)
    return out


def spread(ref, k, row):
    return ref[k, pl.ds(row, SUB, stride=0), :]


def interior_kernel(dims, state, fields, edge, west, east, pw_hbm,
                    inner, part, content, coef, halo1, strip, pw, halo, pw_sem):
    members, levels, rows, width = dims
    fetch = pltpu.make_async_copy(pw_hbm, pw, pw_sem)
    fetch.start()
    groups = members // SUB
    step = width // levels
    from_west = ((lanes_of((SUB, width)) + 2) % step) < 2
    merged = []
    for f in range(4):
        at = pl.ds(rows * members + f * rows, rows)
        merged.append(jnp.where(from_west, west[at, :], east[at, :]))
    for k, c in enumerate(stencil(*merged)):
        strip[k] = c
    for y in range(rows):
        for g in range(groups):
            at = pl.ds(y * members + g * SUB, SUB)
            halo[at, :] = jnp.where(from_west, west[at, :], east[at, :])
    for y in range(rows):
        c0, cw, ce, cs, cn, p = [spread(strip, k, y) for k in range(6)]
        for g in range(groups):
            at = pl.ds(y * members + g * SUB, SUB)
            own, aw, ae = edge[at, :], west[at, :], east[at, :]
            side_w = jnp.where(from_west, pltpu.roll(aw, 1, 1), pltpu.roll(own, 1, 1))
            side_e = jnp.where(from_west, pltpu.roll(own, width - 1, 1), pltpu.roll(ae, width - 1, 1))
            total = (c0 * halo[at, :] + cw * side_w) + (ce * side_e + p)
            if y > 0:
                total = total + cs * halo[pl.ds((y - 1) * members + g * SUB, SUB), :]
            if y < rows - 1:
                total = total + cn * halo[pl.ds((y + 1) * members + g * SUB, SUB), :]
            halo1[at, :] = total
    content[...] = jnp.zeros_like(content)

    def level(l, carry):
        turn = (width - step * l) % width
        base = pl.multiple_of(l * rows, rows)
        got = stencil(*[fields[f, l] for f in range(4)])
        for k, c in enumerate(got):
            coef[k, pl.ds(base, rows), :] = c

        def load(ref, row):
            return [ref[row, pl.ds(g * SUB, SUB), :] for g in range(groups)]

        def sides(ref, y):
            return [ref[pl.ds(y * members + g * SUB, SUB), :] for g in range(groups)]

        def store(ref, row, values):
            for g in range(groups):
                ref[row, pl.ds(g * SUB, SUB), :] = values[g]

        before, now = None, load(state, base)
        older, old, older_c = None, None, None
        for y in range(rows):
            after = load(state, base + y + 1) if y < rows - 1 else None
            c = [spread(coef, k, base + y) for k in range(6)]
            new = advance(now, before, after, sides(halo, y), turn, c, width)
            if y in (0, 1, rows - 2, rows - 1):
                store(part, l * 6 + {0: 0, 1: 1, rows - 2: 2, rows - 1: 3}[y], new)
            y2 = y - 1
            if y2 >= 1:
                done = advance(old, older if y2 > 1 else None, new if y2 < rows - 2 else None,
                               sides(halo1, y2), turn, older_c, width)
                if y2 == 1:
                    store(part, l * 6 + 4, done)
                elif y2 == rows - 2:
                    store(part, l * 6 + 5, done)
                else:
                    store(inner, l * (rows - 4) + y2 - 2, done)
                    for g in range(groups):
                        content[pl.ds((y2 - 2) * members + g * SUB, SUB), :] += done[g]
            older, old, older_c = old, new, c
            before, now = now, after
        return carry

    lax.fori_loop(0, levels, level, 0)
    fetch.wait()


def interior(dims, state, fields, edge, west, east, pw):
    members, levels, rows, width = dims
    shapes = (
        (levels * (rows - 4), members, width),
        (levels * 6, members, width),
        ((rows - 4) * members, width),
        (6, levels * rows, width),
        (rows * members, width),
        (6, rows, width),
    )
    return pl.pallas_call(
        functools.partial(interior_kernel, dims),
        name="interior",
        out_shape=[VMEM(s, F32) for s in shapes] + [VMEM(pw.shape, BF16)],
        in_specs=[IN_VMEM] * 5 + [IN_HBM],
        out_specs=[IN_VMEM] * 7,
        scratch_shapes=[VMEM((rows * members, width), F32), pltpu.SemaphoreType.DMA],
        **grant(8, 60_000_000, 12_000_000),
    )(*near(state, fields, edge, west, east), *far(pw))


def boundary_kernel(dims, lat_size, slots, blocks_dev, block_of, row_of, count,
                    state, part, inner_content, coef, halo1, strip, pw, corner_s, corner_n, below, above,
                    outer, *rest):
    members, levels, rows, width = dims
    outs, (low_coef, high_coef, content, content16, rays, ends) = rest[:lat_size], rest[lat_size:]
    groups = members // SUB
    step = width // levels
    tail = 2 * levels * members
    for source, target in ((below, low_coef), (above, high_coef)):
        got = [source[pl.ds(tail + f * levels, levels), :] for f in range(4)]
        for k, c in enumerate(stencil(*got)):
            target[k] = c
    for i, (y, k, corner) in enumerate(((0, 3, corner_s), (rows - 1, 4, corner_n))):
        c = spread(strip, k, y)
        for g in range(groups):
            at = pl.ds(g * SUB, SUB)
            ends[i, at, :] = halo1[pl.ds(y * members + g * SUB, SUB), :] + c * corner[at, :]
    edge_rows = (0, 1, rows - 2, rows - 1)
    for y in edge_rows:
        at = pl.ds(y * members, members)
        content[at, :] = jnp.zeros((members, width), F32)
    content[pl.ds(2 * members, (rows - 4) * members), :] = inner_content[...]

    def level(l, carry):
        turn = (width - step * l) % width
        base = pl.multiple_of(l * rows, rows)

        def halo_row(ref, r):
            start = pl.multiple_of((l * 2 + r) * members, members)
            return [ref[pl.ds(start + g * SUB, SUB), :] for g in range(groups)]

        def load(ref, row):
            return [ref[row, pl.ds(g * SUB, SUB), :] for g in range(groups)]

        def side(ref):
            return [ref[pl.ds(g * SUB, SUB), :] for g in range(groups)]

        def add(partial, c, values):
            return [q + c * v for q, v in zip(partial, values)]

        south1, north1 = halo_row(below, 1), halo_row(above, 0)
        lower = advance(south1, halo_row(below, 0), load(state, base), side(corner_s), turn,
                        [spread(low_coef, k, l) for k in range(6)], width)
        upper = advance(north1, load(state, base + rows - 1), halo_row(above, 1), side(corner_n), turn,
                        [spread(high_coef, k, l) for k in range(6)], width)
        c_first = [spread(coef, k, base) for k in range(6)]
        c_last = [spread(coef, k, base + rows - 1) for k in range(6)]
        first = add(load(part, l * 6), c_first[3], south1)
        last = add(load(part, l * 6 + 3), c_last[4], north1)
        done = (
            advance(first, lower, load(part, l * 6 + 1), side(ends.at[0]), turn, c_first, width),
            add(load(part, l * 6 + 4), spread(coef, 3, base + 1), first),
            add(load(part, l * 6 + 5), spread(coef, 4, base + rows - 2), last),
            advance(last, load(part, l * 6 + 2), upper, side(ends.at[1]), turn, c_last, width),
        )
        for i, y in enumerate(edge_rows):
            for g in range(groups):
                content[pl.ds(y * members + g * SUB, SUB), :] += done[i][g]
                outer[l * 4 + i, pl.ds(g * SUB, SUB), :] = done[i][g]
        return carry

    lax.fori_loop(0, levels, level, 0)
    content16[...] = (content[...] / math.sqrt(levels)).astype(BF16)
    rays[...] = jnp.zeros_like(rays)
    live = count[0]
    mine = lax.axis_index("lat")
    for k in range(slots):
        picked = content16[pl.ds(pl.multiple_of(row_of[k] * members, members), members), :]
        partial = jnp.dot(picked, pw[k], preferred_element_type=F32)
        partial = jnp.where(k < live, partial, 0.0)
        owner = lax.rem(block_of[k] // blocks_dev - mine + lat_size, lat_size)
        place = owner * blocks_dev + lax.rem(block_of[k], blocks_dev)
        at = pl.ds(pl.multiple_of(place * members, members), members)
        rays[at, :] += partial
    size = blocks_dev * members
    for s in range(lat_size):
        outs[s][...] = rays[pl.ds(s * size, size), :]


def boundary(dims, state, inside, corner_s, corner_n, below, above, block_of, row_of, count, lat_size, blocks_dev):
    members, levels, rows, width = dims
    slots, _, block = inside[-1].shape
    size = blocks_dev * members
    return pl.pallas_call(
        functools.partial(boundary_kernel, dims, lat_size, slots, blocks_dev),
        name="boundary_rays",
        out_shape=[VMEM((levels * 4, members, width), F32)] + [VMEM((size, block), F32)] * lat_size,
        in_specs=[IN_SMEM] * 3 + [IN_VMEM] * 11,
        out_specs=[IN_VMEM] * (1 + lat_size),
        scratch_shapes=[
            VMEM((6, levels, width), F32),
            VMEM((6, levels, width), F32),
            VMEM((rows * members, width), F32),
            VMEM((rows * members, width), BF16),
            VMEM((lat_size * size, block), F32),
            VMEM((2, members, width), F32),
        ],
        **grant(8, 30_000_000, 12_000_000),
    )(block_of, row_of, count, *near(state, *inside, corner_s, corner_n, below, above))


def spread_kernel(dims, inner, outer, hi_ref, lo_hbm, centre_ref, lo_ref, sem):
    members, levels, rows, width = dims
    sub = subs_of((rows, width))
    edge_rows = {0: 0, 1: 1, rows - 2: 2, rows - 1: 3}

    def pair(q, carry):
        for h in range(2):
            l = q * 2 + h
            mean = jnp.zeros((rows, width), F32)
            for y in range(rows):
                v = outer[l * 4 + edge_rows[y]] if y in edge_rows else inner[l * (rows - 4) + y - 2]
                m = jnp.sum(v, axis=0, keepdims=True) / members
                mean = jnp.where(sub == y, m, mean)
                a = v - m
                hi = a.astype(BF16)
                to = (q, pl.ds(y * members, members), pl.ds(h * width, width))
                hi_ref[to] = hi
                lo_ref[to] = (a - hi.astype(F32)).astype(BF16)
            centre_ref[pl.ds(pl.multiple_of(l * rows, rows), rows), :] = mean
        pltpu.make_async_copy(lo_ref.at[q], lo_hbm.at[q], sem.at[q]).start()
        return carry

    def finish(q, carry):
        pltpu.make_async_copy(lo_ref.at[q], lo_hbm.at[q], sem.at[q]).wait()
        return carry

    lax.fori_loop(0, levels // 2, pair, 0)
    lax.fori_loop(0, levels // 2, finish, 0)


def anomalies(dims, inner, outer):
    members, levels, rows, width = dims
    shape = (levels // 2, rows * members, 2 * width)
    return pl.pallas_call(
        functools.partial(spread_kernel, dims),
        name="anomalies",
        out_shape=(VMEM(shape, BF16), pltpu.HBM(shape, BF16), VMEM((levels * rows, width), F32)),
        in_specs=[IN_VMEM] * 2,
        out_specs=[IN_VMEM, IN_HBM, IN_VMEM],
        scratch_shapes=[VMEM(shape, BF16), pltpu.SemaphoreType.DMA((levels // 2,))],
        **grant(8, 8_000_000, 8_000_000),
    )(*near(inner, outer))


def moments_kernel(members, blocks_dev, block, n_parts, devices, *refs):
    parts, (obs_ref, var_ref, _, prior_ref, innov_ref, packed_ref) = refs[:n_parts], refs[n_parts:]
    scaled, both = [], []
    for b in range(blocks_dev):
        at = pl.ds(b * members, members)
        total = parts[0][at, :]
        for part in parts[1:]:
            total = total + part[at, :]
        prior_ref[:, pl.ds(b * block, block)] = total
        mean = jnp.sum(total, axis=0, keepdims=True) / members
        dev = total - mean
        var = var_ref[pl.ds(b, 1), :]
        misfit = obs_ref[pl.ds(b, 1), :] - mean
        innov_ref[pl.ds(b, 1), :] = misfit / jnp.sqrt(var)
        scaled.append(dev / var)
        both.append(jnp.concatenate([dev, jnp.broadcast_to(misfit, (SUB, block))], axis=0))
    left = jnp.concatenate(scaled, axis=1)
    right = jnp.concatenate(both, axis=1)
    g = lax.dot_general(left, right, (((1,), (1,)), ((), ())), precision=lax.Precision.HIGHEST,
                        preferred_element_type=F32)
    wide = jnp.concatenate([g, jnp.zeros((members, 128 - g.shape[1]), F32)], axis=1)
    lane = lanes_of((SUB, 128))
    packed = jnp.zeros((SUB, 128), F32)
    groups = members // SUB
    start = 0
    for i in range(groups):
        v = wide[i * SUB:(i + 1) * SUB]
        stop = start + SUB * (i + 1)
        moved = pltpu.roll(v, start, 1) if start else v
        packed = jnp.where((lane >= start) & (lane < stop), moved, packed)
        start = stop
    for i in range(groups):
        v = wide[i * SUB:(i + 1) * SUB]
        packed = jnp.where(lane == start + i, pltpu.roll(v, start + i - members, 1), packed)
    for device in range(devices):
        packed_ref[pl.ds(device * SUB, SUB), :] = packed


def moments(parts, obs, var, after, members, blocks_dev, block, devices):
    return pl.pallas_call(
        functools.partial(moments_kernel, members, blocks_dev, block, len(parts), devices),
        name="moments",
        out_shape=(jax.ShapeDtypeStruct((members, blocks_dev * block), F32),
                   jax.ShapeDtypeStruct((blocks_dev, block), F32),
                   VMEM((devices * SUB, 128), F32)),
        in_specs=[IN_VMEM] * (len(parts) + 3),
        out_specs=[IN_VMEM] * 3,
        **grant(8, 4_000_000, 400_000),
    )(*near(*parts), obs, var, *near(after))


def weights(gathered, members, devices):
    groups = members // SUB
    lane = lanes_of((SUB, 128))
    sub = subs_of((SUB, 128))
    total = gathered[pl.ds(0, SUB), :]
    for d in range(1, devices):
        total = total + gathered[pl.ds(d * SUB, SUB), :]
    lower, start = [], 0
    for i in range(groups):
        v = pltpu.roll(total, (128 - start) % 128, 1) if start else total
        lower.append(jnp.where(lane < SUB * (i + 1), v, 0.0))
        start += SUB * (i + 1)
    upper = jnp.transpose(jnp.concatenate(lower, axis=0))
    upper = upper[:members]
    upper = jnp.concatenate([upper, jnp.zeros((members, 128 - members), F32)], axis=1)
    rows = []
    for i in range(groups):
        a = jnp.where(lane < SUB * (i + 1), lower[i], upper[i * SUB:(i + 1) * SUB])
        a = jnp.where(lane < members, a, 0.0)
        a = a + jnp.where(lane == sub + SUB * i, members - 1.0, 0.0)
        a = jnp.where(lane == members + sub + SUB * i, 1.0, a)
        pull = pltpu.roll(total, (2 * members - start - i) % 128, 1)
        rows.append(jnp.where(lane == 2 * members, pull, a))
    for k in range(members):
        i0, s = divmod(k, SUB)
        pivot_row = jnp.broadcast_to(rows[i0][s:s + 1, :], (SUB, 128))
        pivot = jnp.broadcast_to(pivot_row[:, k:k + 1], (SUB, 128))
        ratio = pivot_row / pivot
        for i in range(i0, groups):
            if i == i0 and s == SUB - 1:
                continue
            factor = jnp.broadcast_to(rows[i][:, k:k + 1], (SUB, 128))
            if i == i0:
                factor = jnp.where(sub > s, factor, 0.0)
            rows[i] = rows[i] - factor * ratio
    mean_weight = jnp.zeros((SUB, 128), F32)
    for i in range(groups):
        pivot = jnp.sum(jnp.where(lane == sub + SUB * i, rows[i], 0.0), axis=1, keepdims=True)
        rows[i] = rows[i] / jnp.sqrt(pivot)
        mean_weight = mean_weight + rows[i] * rows[i][:, 2 * members:2 * members + 1]
    mean_weight = jnp.sum(mean_weight, axis=0, keepdims=True)
    return [mean_weight + math.sqrt(members - 1.0) * r for r in rows]


def update_kernel(dims, devices, gathered, hi_ref, centre_ref, lo_hbm, out_hbm, mat_hi, mat_lo, done, lo_ref, sem, lo_sem):
    members, levels, rows, width = dims
    fetch = pltpu.make_async_copy(lo_hbm, lo_ref, lo_sem)
    fetch.start()
    size = rows * members
    lane = lanes_of((rows, 128))
    sub = subs_of((rows, 128))
    copies = 128 // members
    made = weights(gathered, members, devices)
    for i, r in enumerate(made):
        r = jnp.where(lane < members, pltpu.roll(r, 128 - members, 1), 0.0)
        tiled = r
        for q in range(1, copies):
            tiled = tiled + pltpu.roll(r, q * members, 1)
        for s in range(0, SUB, 2):
            b = i * SUB + s
            for h in range(size // 128):
                keep = (lane // members) + h * copies == sub
                two = [jnp.where(keep, jnp.broadcast_to(tiled[t:t + 1], (rows, 128)), 0.0) for t in (s, s + 1)]
                m = jnp.concatenate(two, axis=0)
                big = m.astype(BF16)
                to = (pl.ds(b * rows, 2 * rows), pl.ds(h * 128, 128))
                mat_hi[to] = big
                mat_lo[to] = (m - big.astype(F32)).astype(BF16)

    fetch.wait()

    def copy(q):
        part = pl.ds(q * 2, 2)
        return pltpu.make_async_copy(done.at[:, part], out_hbm.at[:, part], sem.at[q])

    def pair(q, carry):
        dot = functools.partial(jnp.dot, preferred_element_type=F32)
        hi = hi_ref[q]
        acc = dot(mat_hi[...], hi) + dot(mat_hi[...], lo_ref[q]) + dot(mat_lo[...], hi)
        for h in range(2):
            l = q * 2 + h
            centre = centre_ref[pl.ds(pl.multiple_of(l * rows, rows), rows), :]
            done[:, l] = acc[:, h * width:(h + 1) * width].reshape(members, rows, width) + centre[None]
        copy(q).start()
        return carry

    lax.fori_loop(0, levels // 2, pair, 0)

    def finish(q, carry):
        copy(q).wait()
        return carry

    lax.fori_loop(0, levels // 2, finish, 0)


def update(gathered, hi, lo, centre, dims, devices):
    members, levels, rows, _ = dims
    return pl.pallas_call(
        functools.partial(update_kernel, dims, devices),
        name="update",
        out_shape=jax.ShapeDtypeStruct(dims, F32),
        in_specs=[IN_VMEM] * 3 + [IN_HBM],
        out_specs=IN_HBM,
        scratch_shapes=[VMEM((rows * members, rows * members), BF16)] * 2
        + [VMEM(dims, F32), VMEM(lo.shape, BF16), pltpu.SemaphoreType.DMA((levels // 2,)), pltpu.SemaphoreType.DMA],
        **grant(12, 2_000_000_000, 8_000_000),
    )(*near(gathered, hi, centre), *far(lo))


def per_device(sample_deviations, east_courant, north_courant, production, loss_rate, entry_count, entry_row,
               entry_block, path_weight, observed, obs_var):
    dims = members, levels, rows, width = sample_deviations.shape
    lat_size, lon_size = lax.axis_size("lat"), lax.axis_size("lon")
    block = path_weight.shape[2]
    blocks_dev = observed.shape[0] // block
    step = width // levels
    ring = lambda n, s: [(i, (i + s) % n) for i in range(n)]
    up = [(i, i + 1) for i in range(lat_size - 1)]
    down = [(j, i) for i, j in up]

    fields = (east_courant, north_courant, production, loss_rate)
    state, to_north, to_south, edge, local = pack(sample_deviations, fields)
    west = lax.ppermute(edge, "lon", ring(lon_size, 1))
    east = lax.ppermute(edge, "lon", ring(lon_size, lon_size - 1))
    below = lax.ppermute(to_north, "lat", up)
    above = lax.ppermute(to_south, "lat", down)
    from_west = ((jnp.arange(width) + 2) % step < 2)[None, :]
    top = slice((rows - 1) * members, rows * members)
    corner_s = lax.ppermute(jnp.where(from_west, west[top], east[top]), "lat", up)
    corner_n = lax.ppermute(jnp.where(from_west, west[:members], east[:members]), "lat", down)

    inner, *inside = interior(dims, state, local, edge, west, east, path_weight)
    outer, *sums = boundary(dims, state, inside, corner_s, corner_n, below, above,
                            entry_block, entry_row, entry_count, lat_size, blocks_dev)
    got = [sums[0]] + [lax.ppermute(sums[s], "lat", ring(lat_size, s)) for s in range(1, lat_size)]
    hi, lo, centre = anomalies(dims, inner, outer)
    devices = lat_size * lon_size
    prior, innovation, packed = moments(got, observed.reshape(blocks_dev, block), obs_var.reshape(blocks_dev, block),
                                        centre, members, blocks_dev, block, devices)
    gathered = lax.all_to_all(packed, ("lon", "lat"), 0, 0, tiled=True)
    updated = update(gathered, hi, lo, centre, dims, devices)
    return updated, prior, innovation.reshape(observed.shape)


def solution(mesh):
    tile = P(None, "lat", "lon")
    owned = P(("lon", "lat"))
    in_specs = (P(None, None, "lat", "lon"), tile, tile, tile, tile, owned, owned, owned,
                P(("lon", "lat"), None, None), owned, owned)
    out_specs = (P(None, None, "lat", "lon"), P(None, ("lon", "lat")), owned)
    return jax.shard_map(per_device, mesh=mesh, in_specs=in_specs, out_specs=out_specs, check_vma=False)
```

time: 94.8 us -> 73.4 us (0.77)
  Pallas kernels: 53.1 us -> 34.5 us
  blocking collectives: 0 us -> 9.89 us
  local copies, waits for them, and re-layouts: 4.61 us -> 0.02 us
  starting transfers between devices: 22.4 us -> 18.5 us
  waiting for transfers between devices: 11.9 us -> 8.83 us
    pallas_call x3 -> x4, Pallas kernels: 44.7 us -> 29 us  [the longest x1 10.2 us: interior(): pl.pallas_call(functools.partial(interior_kernel, dims), name='interior',...]
    all_to_all x0 -> x1, blocking collectives: none -> 9.89 us  [per_device(): gathered = lax.all_to_all(packed, ('lon', 'lat'), 0, 0, tiled=True)]
    unnamed x22 -> x8, local copies, waits for them, and re-layouts: 3.26 us -> 0.02 us
    all_to_all x1 -> x0, starting transfers between devices: 2.56 us -> none  [per_device(): gathered = lax.all_to_all(spread_out, ('lon', 'lat'), 0, 0, tiled=True)]
    ppermute x3, waiting for transfers between devices: 2.22 us -> 0.5 us  [per_device(): lax.ppermute(sums[s], 'lat', ring(lat_size, s))]
    pallas_call x1, Pallas kernels: 6.59 us -> 4.88 us  [pack(): pl.pallas_call(functools.partial(pack_kernel, x.shape, chunks), name='pac...]
    ppermute x3, starting transfers between devices: 5.97 us -> 4.56 us  [per_device(): lax.ppermute(sums[s], 'lat', ring(lat_size, s))]
    broadcast_in_dim x1 -> x0, local copies, waits for them, and re-layouts: 1.35 us -> none  [per_device(): jnp.broadcast_to(packed[None], (devices, SUB, 128))]
  transfers between devices with their start and end apart: 10 -> 9, of which waited for: 5 -> 3; matrix products, arithmetic and copies ran while one was open for 1% -> 0% of each run, Pallas kernels for 7% -> 17%
where the time goes in v2:
time: 73.4 us; the launch traced here: 73.2 us
  Pallas kernels  34.5 us (47%)
  starting transfers between devices  18.5 us (25%)
  blocking collectives  9.89 us (13%)
  waiting for transfers between devices  8.83 us (12%)
  between operations  1.42 us (2%)
    pallas_call x1, Pallas kernels, interior(): pl.pallas_call(functools.partial(interior_kernel, dims), name='interior',...  10.2 us
    all_to_all x1, blocking collectives, per_device(): gathered = lax.all_to_all(packed, ('lon', 'lat'), 0, 0, tiled=True)  9.89 us
    pallas_call x1, Pallas kernels, update(): pl.pallas_call(functools.partial(update_kernel, dims, devices), name='upd...  9.58 us
    pallas_call x1, Pallas kernels, boundary(): pl.pallas_call(functools.partial(boundary_kernel, dims, lat_size, slots,...  7 us
    ppermute x1, waiting for transfers between devices, per_device(): west = lax.ppermute(edge, 'lon', ring(lon_size, 1))  5.46 us
    ppermute x1, starting transfers between devices, per_device(): east = lax.ppermute(edge, 'lon', ring(lon_size, lon_size - 1))  5.43 us
    pallas_call x1, Pallas kernels, pack(): pl.pallas_call(functools.partial(pack_kernel, x.shape, chunks), name='pac...  4.88 us
    ppermute x3, starting transfers between devices, per_device(): lax.ppermute(sums[s], 'lat', ring(lat_size, s))  4.56 us
  transfers between devices with their start and end apart: 9, of which 3 were waited for; matrix products, arithmetic and copies ran while one was open for 0% of the time, Pallas kernels for 17%

profile of v2, /device:TPU:0, one launch (start us, length us, event | category | flops | bytes accessed | tf_op | source)
XLA Modules:
  0.0 73.2 jit_solution(16508009094520633709)
XLA Ops:
  0.6 4.9 %pack_halos.1 = (f32[256,32,128]{2,1,0:T(8,128)S(1)}, f32[2176,128]{1,0:T(8,128)S(1)}, f32[2176,128]{1,0:T(8,128)S(1)}, f32[288,128]{1,0:T(8,128)S(1)}, f32[4,32,8,128]{3,2,1,0:T(8,128)S(1)}) custom-call(f32[32,32,8,128]{3,2,1,0:T(8,128)} %x_hbm.1, f32[32,8,128]{2,1,0:T(8,128)} %e_hbm.1, f32[32,8,128]{2,1,0:T(8,128)} %n_hbm.1, f32[32,8,128]{2,1,0:T(8,128)} %p_hbm.1, ...), custom_call_target="tpu_custom_call" | custom-call | flops 4000000 | bytes 8000000 | tf_op jit(solution)/shard_map/pack_halos/pallas_call | solution.py:106
  5.5 2.5 %collective-permute-start.4 = (f32[2176,128]{1,0:T(8,128)S(1)}, f32[2176,128]{1,0:T(8,128)S(1)}, u32[]{:S(2)}, u32[]{:S(2)}) collective-permute-start(f32[2176,128]{1,0:T(8,128)S(1)} %get-tuple-element.35), channel_id=1, source_target_pairs={{0,1},{1,2},{2,3},{4,5},{5,6},{6,7},{8,9},{9,10},{10,11},{12,13},{... | collective-permute-start | bytes 3342344 | tf_op jit(solution)/shard_map/ppermute | solution.py:586
  8.0 1.3 %collective-permute-start.5 = (f32[2176,128]{1,0:T(8,128)S(1)}, f32[2176,128]{1,0:T(8,128)S(1)}, u32[]{:S(2)}, u32[]{:S(2)}) collective-permute-start(f32[2176,128]{1,0:T(8,128)S(1)} %get-tuple-element.36), channel_id=1, source_target_pairs={{1,0},{2,1},{3,2},{5,4},{6,5},{7,6},{9,8},{10,9},{11,10},{13,12},{... | collective-permute-start | bytes 3342344 | tf_op jit(solution)/shard_map/ppermute | solution.py:587
  9.3 5.4 %collective-permute-start.1 = (f32[288,128]{1,0:T(8,128)S(1)}, f32[288,128]{1,0:T(8,128)S(1)}, u32[]{:S(2)}, u32[]{:S(2)}) collective-permute-start(f32[288,128]{1,0:T(8,128)S(1)} %get-tuple-element.28.edge), channel_id=1, source_target_pairs={{0,28},{4,0},{8,4},{12,8},{16,12},{20,16},{24,20},{28,24},{1,29},{... | collective-permute-start | bytes 442376 | tf_op jit(solution)/shard_map/ppermute | solution.py:585
  14.7 0.0 collective-permute-start
  14.7 2.9 %collective-permute-done.1.east = f32[288,128]{1,0:T(8,128)S(1)} collective-permute-done((f32[288,128]{1,0:T(8,128)S(1)}, f32[288,128]{1,0:T(8,128)S(1)}, u32[]{:S(2)}, u32[]{:S(2)}) %collective-permute-start.1) | collective-permute-done | bytes 147488 | tf_op jit(solution)/shard_map/ppermute | solution.py:585
  17.6 5.5 %collective-permute-done.west = f32[288,128]{1,0:T(8,128)S(1)} collective-permute-done((f32[288,128]{1,0:T(8,128)S(1)}, f32[288,128]{1,0:T(8,128)S(1)}, u32[]{:S(2)}, u32[]{:S(2)}) %collective-permute-start) | collective-permute-done | bytes 147488 | tf_op jit(solution)/shard_map/ppermute | solution.py:584
  23.1 1.3 %collective-permute-start.3 = (f32[32,128]{1,0:T(8,128)S(1)}, f32[32,128]{1,0:T(8,128)S(1)}, u32[]{:S(2)}, u32[]{:S(2)}) collective-permute-start(f32[32,128]{1,0:T(8,128)S(1)} %get-tuple-element.49), channel_id=1, source_target_pairs={{1,0},{2,1},{3,2},{5,4},{6,5},{7,6},{9,8},{10,9},{11,10},{13,12},{... | collective-permute-start | bytes 49160 | tf_op jit(solution)/shard_map/ppermute | solution.py:591
  24.4 3.4 %collective-permute-start.2 = (f32[32,128]{1,0:T(8,128)S(1)}, f32[32,128]{1,0:T(8,128)S(1)}, u32[]{:S(2)}, u32[]{:S(2)}) collective-permute-start(f32[32,128]{1,0:T(8,128)S(1)} %get-tuple-element.50), channel_id=1, source_target_pairs={{0,1},{1,2},{2,3},{4,5},{5,6},{6,7},{8,9},{9,10},{10,11},{12,13},{... | collective-permute-start | bytes 49160 | tf_op jit(solution)/shard_map/ppermute | solution.py:590
  28.4 0.0 copy-start.2
  28.5 0.0 copy-start.3
  28.5 10.2 %interior.1 = (f32[128,32,128]{2,1,0:T(8,128)S(1)}, f32[192,32,128]{2,1,0:T(8,128)S(1)}, f32[128,128]{1,0:T(8,128)S(1)}, f32[6,256,128]{2,1,0:T(8,128)S(1)}, f32...) custom-call(f32[256,32,128]{2,1,0:T(8,128)S(1)} %get-tuple-element.26.state, ...), custom_call_target="tpu_custom_call" | custom-call | flops 60000000 | bytes 12000000 | tf_op jit(solution)/shard_map/interior/pallas_call | solution.py:255
  38.7 0.0 collective-permute-done.3.corner_n
  38.8 0.0 collective-permute-done.5.above
  38.8 7.0 %boundary_rays.1 = (f32[128,32,128]{2,1,0:T(8,128)S(1)}, f32[128,128]{1,0:T(8,128)S(1)}, f32[128,128]{1,0:T(8,128)S(1)}, f32[128,128]{1,0:T(8,128)S(1)}, f32[128,128]{1,0:T(8,128)S(1)}) custom-call(s32[48]{0:T(128)S(1)} %copy-done.2, s32[48]{0:T(128)S(1)} %copy-done.3, s32[1]{0:T(128)S(6)} %copy.14.count, f32[256,32,128]{2,1,0:T(8,128)S(1)} %get-tuple-element.26.state, ...), custom_call_target="tpu_custom_call" | custom-call | flops 30000000 | bytes 12000000 | tf_op jit(solution)/shard_map/boundary_rays/pallas_call | solution.py:349
  45.8 2.7 %collective-permute-start.6 = (f32[128,128]{1,0:T(8,128)S(1)}, f32[128,128]{1,0:T(8,128)S(1)}, u32[]{:S(2)}, u32[]{:S(2)}) collective-permute-start(f32[128,128]{1,0:T(8,128)S(1)} %get-tuple-element.38), channel_id=1, source_target_pairs={{0,1},{1,2},{2,3},{3,0},{4,5},{5,6},{6,7},{7,4},{8,9},{9,10},{10,1... | collective-permute-start | bytes 196616 | tf_op jit(solution)/shard_map/ppermute | solution.py:596
  48.5 0.5 collective-permute-start.7
  49.0 1.4 %collective-permute-start.8 = (f32[128,128]{1,0:T(8,128)S(1)}, f32[128,128]{1,0:T(8,128)S(1)}, u32[]{:S(2)}, u32[]{:S(2)}) collective-permute-start(f32[128,128]{1,0:T(8,128)S(1)} %get-tuple-element.40), channel_id=1, source_target_pairs={{0,3},{1,0},{2,1},{3,2},{4,7},{5,4},{6,5},{7,6},{8,11},{9,8},{10,9... | collective-permute-start | bytes 196616 | tf_op jit(solution)/shard_map/ppermute | solution.py:596
  50.4 2.1 %anomalies.1 = (bf16[16,256,256]{2,1,0:T(8,128)(2,1)S(1)}, bf16[16,256,256]{2,1,0:T(8,128)(2,1)}, f32[256,128]{1,0:T(8,128)S(1)}) custom-call(f32[128,32,128]{2,1,0:T(8,128)S(1)} %get-tuple-element.41.inner, f32[128,32,128]{2,1,0:T(8,128)S(1)} %get-tuple-element.42.outer), custom_call_target="tpu_custom_call" | custom-call | flops 8000000 | bytes 8000000 | tf_op jit(solution)/shard_map/anomalies/pallas_call | solution.py:400
  52.5 0.0 collective-permute-done.6.refs_1_
  52.5 0.5 collective-permute-done.7.refs_2_
  53.0 0.7 moments.1
  53.7 9.9 %all_to_all.11 = f32[32,8,128]{2,1,0:T(8,128)S(1)} all-to-all(f32[32,8,128]{2,1,0:T(8,128)S(1)} %bitcast.6), channel_id=1, replica_groups=mesh['lon'=8,'lat'=4] {'lon','lat'}, dimensions={0} | all-to-all | bytes 262144 | tf_op jit(solution)/shard_map/all_to_all | solution.py:601
  63.6 9.6 %update.1 = f32[32,32,8,128]{3,2,1,0:T(8,128)} custom-call(f32[256,128]{1,0:T(8,128)S(1)} %bitcast.5, bf16[16,256,256]{2,1,0:T(8,128)(2,1)S(1)} %get-tuple-element.45.hi_ref, f32[256,128]{1,0:T(8,128)S(1)} %get-tuple-element.43.refs_6_.centre_ref, bf16[16,256,256]{2,1,0:T(8,128)(2,1)} %get-tuple-element.46.lo_hbm), custom_call_target="tpu_custom_call" | custom-call | flops 2000000000 | bytes 8000000 | tf_op jit(solution)/shard_map/update/pallas_call | solution.py:559
  (11 shorter events, 0.0 us)
Async XLA Ops:
  5.5 33.2 %collective-permute-start.4 = (f32[2176,128]{1,0:T(8,128)S(1)}, f32[2176,128]{1,0:T(8,128)S(1)}, u32[]{:S(2)}, u32[]{:S(2)}) collective-permute-start(f32[2176,128]{1,0:T(8,128)S(1)} %get-tuple-element.35), channel_id=1, source_target_pairs={{0,1},{1,2},{2,3},{4,5},{5,6},{6,7},{8,9},{9,10},{10,11},{12,13},{... | collective-permute-start | bytes 3342344 | tf_op jit(solution)/shard_map/ppermute | solution.py:586
  8.0 30.8 %collective-permute-start.5 = (f32[2176,128]{1,0:T(8,128)S(1)}, f32[2176,128]{1,0:T(8,128)S(1)}, u32[]{:S(2)}, u32[]{:S(2)}) collective-permute-start(f32[2176,128]{1,0:T(8,128)S(1)} %get-tuple-element.36), channel_id=1, source_target_pairs={{1,0},{2,1},{3,2},{5,4},{6,5},{7,6},{9,8},{10,9},{11,10},{13,12},{... | collective-permute-start | bytes 3342344 | tf_op jit(solution)/shard_map/ppermute | solution.py:587
  9.3 8.3 %collective-permute-start.1 = (f32[288,128]{1,0:T(8,128)S(1)}, f32[288,128]{1,0:T(8,128)S(1)}, u32[]{:S(2)}, u32[]{:S(2)}) collective-permute-start(f32[288,128]{1,0:T(8,128)S(1)} %get-tuple-element.28.edge), channel_id=1, source_target_pairs={{0,28},{4,0},{8,4},{12,8},{16,12},{20,16},{24,20},{28,24},{1,29},{... | collective-permute-start | bytes 442376 | tf_op jit(solution)/shard_map/ppermute | solution.py:585
  14.7 8.3 %collective-permute-start = (f32[288,128]{1,0:T(8,128)S(1)}, f32[288,128]{1,0:T(8,128)S(1)}, u32[]{:S(2)}, u32[]{:S(2)}) collective-permute-start(f32[288,128]{1,0:T(8,128)S(1)} %get-tuple-element.28.edge), channel_id=1, source_target_pairs={{0,4},{4,8},{8,12},{12,16},{16,20},{20,24},{24,28},{28,0},{1,5},{5... | collective-permute-start | bytes 442376 | tf_op jit(solution)/shard_map/ppermute | solution.py:584
  23.1 15.7 %collective-permute-start.3 = (f32[32,128]{1,0:T(8,128)S(1)}, f32[32,128]{1,0:T(8,128)S(1)}, u32[]{:S(2)}, u32[]{:S(2)}) collective-permute-start(f32[32,128]{1,0:T(8,128)S(1)} %get-tuple-element.49), channel_id=1, source_target_pairs={{1,0},{2,1},{3,2},{5,4},{6,5},{7,6},{9,8},{10,9},{11,10},{13,12},{... | collective-permute-start | bytes 49160 | tf_op jit(solution)/shard_map/ppermute | solution.py:591
  24.4 14.4 %collective-permute-start.2 = (f32[32,128]{1,0:T(8,128)S(1)}, f32[32,128]{1,0:T(8,128)S(1)}, u32[]{:S(2)}, u32[]{:S(2)}) collective-permute-start(f32[32,128]{1,0:T(8,128)S(1)} %get-tuple-element.50), channel_id=1, source_target_pairs={{0,1},{1,2},{2,3},{4,5},{5,6},{6,7},{8,9},{9,10},{10,11},{12,13},{... | collective-permute-start | bytes 49160 | tf_op jit(solution)/shard_map/ppermute | solution.py:590
  28.4 10.3 %copy-start.2 = (s32[48]{0:T(128)S(1)}, s32[48]{0:T(128)}, u32[]{:S(2)}) copy-start(s32[48]{0:T(128)} %block_of.1) | copy-start | bytes 580
  28.5 10.3 %copy-start.3 = (s32[48]{0:T(128)S(1)}, s32[48]{0:T(128)}, u32[]{:S(2)}) copy-start(s32[48]{0:T(128)} %row_of.1) | copy-start | bytes 580
  45.8 6.7 %collective-permute-start.6 = (f32[128,128]{1,0:T(8,128)S(1)}, f32[128,128]{1,0:T(8,128)S(1)}, u32[]{:S(2)}, u32[]{:S(2)}) collective-permute-start(f32[128,128]{1,0:T(8,128)S(1)} %get-tuple-element.38), channel_id=1, source_target_pairs={{0,1},{1,2},{2,3},{3,0},{4,5},{5,6},{6,7},{7,4},{8,9},{9,10},{10,1... | collective-permute-start | bytes 196616 | tf_op jit(solution)/shard_map/ppermute | solution.py:596
  48.5 4.5 %collective-permute-start.7 = (f32[128,128]{1,0:T(8,128)S(1)}, f32[128,128]{1,0:T(8,128)S(1)}, u32[]{:S(2)}, u32[]{:S(2)}) collective-permute-start(f32[128,128]{1,0:T(8,128)S(1)} %get-tuple-element.39), channel_id=1, source_target_pairs={{0,2},{1,3},{2,0},{3,1},{4,6},{5,7},{6,4},{7,5},{8,10},{9,11},{10,... | collective-permute-start | bytes 196616 | tf_op jit(solution)/shard_map/ppermute | solution.py:596
  49.0 4.0 %collective-permute-start.8 = (f32[128,128]{1,0:T(8,128)S(1)}, f32[128,128]{1,0:T(8,128)S(1)}, u32[]{:S(2)}, u32[]{:S(2)}) collective-permute-start(f32[128,128]{1,0:T(8,128)S(1)} %get-tuple-element.40), channel_id=1, source_target_pairs={{0,3},{1,0},{2,1},{3,2},{4,7},{5,4},{6,5},{7,6},{8,11},{9,8},{10,9... | collective-permute-start | bytes 196616 | tf_op jit(solution)/shard_map/ppermute | solution.py:596
  50.4 2.7 %copy-start = (f32[512]{0:T(512)S(1)}, f32[512]{0:T(512)}, u32[]{:S(2)}) copy-start(f32[512]{0:T(512)} %param.20) | copy-start | bytes 6148
  50.4 2.7 %copy-start.1 = (f32[512]{0:T(512)S(1)}, f32[512]{0:T(512)}, u32[]{:S(2)}) copy-start(f32[512]{0:T(512)} %param.21) | copy-start | bytes 6148

commit v3 on v2

--- a/solution.py
+++ b/solution.py
@@ -44,8 +44,12 @@
 IN_HBM = pl.BlockSpec(memory_space=pltpu.HBM)
 
 
-def pack_kernel(dims, chunks, x_hbm, e_hbm, n_hbm, p_hbm, d_hbm, state, north, south, edge, fields,
-                in_sem, field_sem, tail_sem):
+def west_lanes(width, step):
+    return ((lanes_of((SUB, width)) + 2) % step) < 2
+
+
+def pack_kernel(dims, chunks, x_hbm, e_hbm, n_hbm, p_hbm, d_hbm, state, north, south, edge, to_east, to_west,
+                fields, in_sem, field_sem):
     members, levels, rows, width = dims
     per = levels // chunks
     step = width // levels
@@ -72,9 +76,10 @@
         for l in range(levels):
             acc = jnp.where(level_of == l, pltpu.roll(fields[f, l], (step * l) % width, 1), acc)
         edge[pl.ds(rows * members + f * rows, rows), :] = acc
-        at = pl.ds(state_rows + f * levels, levels)
-        pltpu.make_async_copy(fields.at[f, :, rows - 1], north.at[at], tail_sem.at[0, f]).start()
-        pltpu.make_async_copy(fields.at[f, :, 0], south.at[at], tail_sem.at[1, f]).start()
+        for l in range(levels):
+            at = pl.ds(state_rows + l * 4 + f, 1)
+            north[at, :] = fields[f, l, rows - 1:rows]
+            south[at, :] = fields[f, l, 0:1]
     for c in range(chunks):
         first = c * per
         for l in range(first, first + per):
@@ -93,10 +98,15 @@
                     v = state[l * rows + y, pl.ds(g * SUB, SUB), :]
                     acc = jnp.where(level_of == l, pltpu.roll(v, (step * l) % width, 1), acc)
                 edge[at, :] = acc
-    for f in range(4):
-        at = pl.ds(state_rows + f * levels, levels)
-        pltpu.make_async_copy(fields.at[f, :, rows - 1], north.at[at], tail_sem.at[0, f]).wait()
-        pltpu.make_async_copy(fields.at[f, :, 0], south.at[at], tail_sem.at[1, f]).wait()
+    from_west = west_lanes(width, step)
+    tiles = [(y * members + g * SUB, (y + 1) * members + g * SUB, (y // 2) * members + g * SUB)
+             for y in range(0, rows, 2) for g in range(members // SUB)]
+    start = rows * members
+    tiles += [(start + f * rows, start + (f + 1) * rows, start // 2 + (f // 2) * rows) for f in (0, 2)]
+    for even, odd, to in tiles:
+        a, b = edge[pl.ds(even, SUB), :], edge[pl.ds(odd, SUB), :]
+        to_east[pl.ds(to, SUB), :] = jnp.where(from_west, a, pltpu.roll(b, width - 2, 1))
+        to_west[pl.ds(to, SUB), :] = jnp.where(from_west, pltpu.roll(b, 2, 1), a)
 
 
 def pack(x, fields, chunks=4):
@@ -111,14 +121,15 @@
             VMEM((halo, width), F32),
             VMEM((halo, width), F32),
             VMEM((edge, width), F32),
+            VMEM((edge // 2, width), F32),
+            VMEM((edge // 2, width), F32),
             VMEM((4, levels, rows, width), F32),
         ),
         in_specs=[IN_HBM] * 5,
-        out_specs=[IN_VMEM] * 5,
+        out_specs=[IN_VMEM] * 7,
         scratch_shapes=[
             pltpu.SemaphoreType.DMA((chunks,)),
             pltpu.SemaphoreType.DMA((4,)),
-            pltpu.SemaphoreType.DMA((2, 4)),
         ],
         **grant(8, 4_000_000, 8_000_000),
     )(*far(x, *fields))
@@ -138,20 +149,18 @@
     )
 
 
-def sided(side, turn, v, width):
-    lane = lanes_of(v.shape)
-    values = pltpu.roll(side, turn, 1)
-    w = pltpu.roll(jnp.where(lane == width - 1, values, v), 1, 1)
-    e = pltpu.roll(jnp.where(lane == 0, values, v), width - 1, 1)
-    return w, e
-
-
-def advance(mid, low, high, side, turn, c, width):
+def closed(c):
+    lane = lanes_of(c[1].shape)
+    width = c[1].shape[1]
+    c0, cw, ce, cs, cn, p = c
+    return c0, jnp.where(lane == 0, 0.0, cw), jnp.where(lane == width - 1, 0.0, ce), cs, cn, p
+
+
+def advance(mid, low, high, c):
     c0, cw, ce, cs, cn, p = c
     out = []
     for g, v in enumerate(mid):
-        w, e = sided(side[g], turn, v, width)
-        total = (c0 * v + cw * w) + (ce * e + p)
+        total = (c0 * v + cw * pltpu.roll(v, 1, 1)) + (ce * pltpu.roll(v, v.shape[1] - 1, 1) + p)
         if low is not None:
             total = total + cs * low[g]
         if high is not None:
@@ -160,55 +169,141 @@
     return out
 
 
-def spread(ref, k, row):
-    return ref[k, pl.ds(row, SUB, stride=0), :]
-
-
-def interior_kernel(dims, state, fields, edge, west, east, pw_hbm,
-                    inner, part, content, coef, halo1, strip, pw, halo, pw_sem):
-    members, levels, rows, width = dims
+def spread(tile, row):
+    return jnp.broadcast_to(tile[row:row + 1], (SUB, tile.shape[1]))
+
+
+def open_strip(packed, base, odd, back, width):
+    tile = packed[pl.ds(base, SUB), :]
+    return pltpu.roll(tile, back % width, 1) if odd else tile
+
+
+def corners_kernel(dims, edge, west, east, first_out, last_out):
+    members, levels, rows, width = dims
+    from_west = west_lanes(width, width // levels)
+    for g in range(members // SUB):
+        at = pl.ds(g * SUB, SUB)
+        base = (rows // 2 - 1) * members + g * SUB
+        first_out[at, :] = jnp.where(from_west, west[at, :], east[at, :])
+        last_out[at, :] = jnp.where(from_west, open_strip(west, base, True, 2, width),
+                                    open_strip(east, base, True, -2, width))
+    start = rows * members
+    sub = subs_of((SUB, width))
+    for out, y in ((first_out, 0), (last_out, rows - 1)):
+        picked = jnp.zeros((SUB, width), F32)
+        for f in range(4):
+            picked = jnp.where(sub == f, spread(edge[pl.ds(start + f * rows, rows), :], y), picked)
+        out[pl.ds(members, SUB), :] = picked
+
+
+def corners(dims, edge, west, east):
+    members, _, _, width = dims
+    shape = (members + SUB, width)
+    return pl.pallas_call(
+        functools.partial(corners_kernel, dims),
+        name="corners",
+        out_shape=[VMEM(shape, F32)] * 2,
+        in_specs=[IN_VMEM] * 3,
+        out_specs=[IN_VMEM] * 2,
+        **grant(8, 100_000, 400_000),
+    )(*near(edge, west, east))
+
+
+def columns_kernel(dims, edge, west, east, corner_s, corner_n, fix, fix_sum, halo, change, halo1):
+    members, levels, rows, width = dims
+    groups = members // SUB
+    step = width // levels
+    lane = lanes_of((SUB, width))
+    kind = lane % step
+    from_west = west_lanes(width, step)
+    is_first, is_last = kind == 0, kind == step - 1
+    start = rows * members
+    outside = []
+    for f in range(4):
+        base = start // 2 + (f // 2) * rows
+        outside.append(jnp.where(from_west, open_strip(west, base, f % 2, 2, width),
+                                 open_strip(east, base, f % 2, -2, width)))
+    outside = stencil(*outside)
+    own = stencil(*[edge[pl.ds(start + f * rows, rows), :] for f in range(4)])
+
+    def change_of(values, cw, ce):
+        entering = jnp.where(is_first, cw * pltpu.roll(values, 1, 1), 0.0)
+        return jnp.where(is_last, ce * pltpu.roll(values, width - 1, 1), entering)
+
+    for y in range(-1, rows + 1):
+        if y < 0 or y >= rows:
+            source = corner_s if y < 0 else corner_n
+            fields = source[pl.ds(members, SUB), :]
+            c = stencil(*[spread(fields, f) for f in range(4)])
+            cw, ce = c[1], c[2]
+        else:
+            cw, ce = spread(own[1], y), spread(own[2], y)
+        for g in range(groups):
+            at = pl.ds((y + 1) * members + g * SUB, SUB)
+            if y < 0 or y >= rows:
+                values = source[pl.ds(g * SUB, SUB), :]
+            else:
+                base = (y // 2) * members + g * SUB
+                values = jnp.where(from_west, open_strip(west, base, y % 2, 2, width),
+                                   open_strip(east, base, y % 2, -2, width))
+            halo[at, :] = values
+            change[at, :] = change_of(values, cw, ce)
+    for y in range(rows):
+        c0, cw, ce, cs, cn, p = [spread(t, y) for t in outside]
+        k0, kw, ke, ks, kn, _ = [spread(t, y) for t in own]
+        for g in range(groups):
+            at = pl.ds(y * members + g * SUB, SUB)
+            low, mid, high = [pl.ds((y + d) * members + g * SUB, SUB) for d in range(3)]
+            base = (y // 2) * members + g * SUB
+            inner = edge[at, :]
+            aw = open_strip(west, base, y % 2, 2, width)
+            ae = open_strip(east, base, y % 2, -2, width)
+            side_w = jnp.where(from_west, pltpu.roll(aw, 1, 1), pltpu.roll(inner, 1, 1))
+            side_e = jnp.where(from_west, pltpu.roll(inner, width - 1, 1), pltpu.roll(ae, width - 1, 1))
+            beyond = (c0 * halo[mid, :] + cw * side_w) + (ce * side_e + cs * halo[low, :]) + (cn * halo[high, :] + p)
+            moved = change[mid, :]
+            total = k0 * moved + ks * change[low, :] + kn * change[high, :] + change_of(beyond, kw, ke)
+            total = jnp.where(kind == 1, kw * pltpu.roll(moved, 1, 1), total)
+            total = jnp.where(kind == 2, ke * pltpu.roll(moved, width - 1, 1), total)
+            fix[at, :] = total
+            shift = step
+            while shift < width:
+                total = total + pltpu.roll(total, shift, 1)
+                shift *= 2
+            fix_sum[at, :] = jnp.where((lane < 2) | (lane >= width - 2), total, 0.0)
+
+
+def columns(dims, edge, west, east, corner_s, corner_n):
+    members, levels, rows, width = dims
+    if width != 4 * levels:
+        raise ValueError("strip width")
+    shape = (rows * members, width)
+    return pl.pallas_call(
+        functools.partial(columns_kernel, dims),
+        name="columns",
+        out_shape=[VMEM(shape, F32)] * 2,
+        in_specs=[IN_VMEM] * 5,
+        out_specs=[IN_VMEM] * 2,
+        scratch_shapes=[VMEM(((rows + 2) * members, width), F32)] * 2 + [VMEM(shape, F32)],
+        **grant(8, 2_000_000, 1_000_000),
+    )(*near(edge, west, east, corner_s, corner_n))
+
+
+def interior_kernel(dims, state, fields, pw_hbm, inner, part, content, coef, pw, pw_sem):
+    members, levels, rows, _ = dims
+    groups = members // SUB
     fetch = pltpu.make_async_copy(pw_hbm, pw, pw_sem)
     fetch.start()
-    groups = members // SUB
-    step = width // levels
-    from_west = ((lanes_of((SUB, width)) + 2) % step) < 2
-    merged = []
-    for f in range(4):
-        at = pl.ds(rows * members + f * rows, rows)
-        merged.append(jnp.where(from_west, west[at, :], east[at, :]))
-    for k, c in enumerate(stencil(*merged)):
-        strip[k] = c
-    for y in range(rows):
-        for g in range(groups):
-            at = pl.ds(y * members + g * SUB, SUB)
-            halo[at, :] = jnp.where(from_west, west[at, :], east[at, :])
-    for y in range(rows):
-        c0, cw, ce, cs, cn, p = [spread(strip, k, y) for k in range(6)]
-        for g in range(groups):
-            at = pl.ds(y * members + g * SUB, SUB)
-            own, aw, ae = edge[at, :], west[at, :], east[at, :]
-            side_w = jnp.where(from_west, pltpu.roll(aw, 1, 1), pltpu.roll(own, 1, 1))
-            side_e = jnp.where(from_west, pltpu.roll(own, width - 1, 1), pltpu.roll(ae, width - 1, 1))
-            total = (c0 * halo[at, :] + cw * side_w) + (ce * side_e + p)
-            if y > 0:
-                total = total + cs * halo[pl.ds((y - 1) * members + g * SUB, SUB), :]
-            if y < rows - 1:
-                total = total + cn * halo[pl.ds((y + 1) * members + g * SUB, SUB), :]
-            halo1[at, :] = total
     content[...] = jnp.zeros_like(content)
 
     def level(l, carry):
-        turn = (width - step * l) % width
         base = pl.multiple_of(l * rows, rows)
-        got = stencil(*[fields[f, l] for f in range(4)])
+        got = closed(stencil(*[fields[f, l] for f in range(4)]))
         for k, c in enumerate(got):
-            coef[k, pl.ds(base, rows), :] = c
+            coef[l, k] = c
 
         def load(ref, row):
             return [ref[row, pl.ds(g * SUB, SUB), :] for g in range(groups)]
-
-        def sides(ref, y):
-            return [ref[pl.ds(y * members + g * SUB, SUB), :] for g in range(groups)]
 
         def store(ref, row, values):
             for g in range(groups):
@@ -218,14 +313,13 @@
         older, old, older_c = None, None, None
         for y in range(rows):
             after = load(state, base + y + 1) if y < rows - 1 else None
-            c = [spread(coef, k, base + y) for k in range(6)]
-            new = advance(now, before, after, sides(halo, y), turn, c, width)
+            c = [spread(t, y) for t in got]
+            new = advance(now, before, after, c)
             if y in (0, 1, rows - 2, rows - 1):
                 store(part, l * 6 + {0: 0, 1: 1, rows - 2: 2, rows - 1: 3}[y], new)
             y2 = y - 1
             if y2 >= 1:
-                done = advance(old, older if y2 > 1 else None, new if y2 < rows - 2 else None,
-                               sides(halo1, y2), turn, older_c, width)
+                done = advance(old, older if y2 > 1 else None, new if y2 < rows - 2 else None, older_c)
                 if y2 == 1:
                     store(part, l * 6 + 4, done)
                 elif y2 == rows - 2:
@@ -242,89 +336,80 @@
     fetch.wait()
 
 
-def interior(dims, state, fields, edge, west, east, pw):
+def interior(dims, state, fields, pw):
     members, levels, rows, width = dims
     shapes = (
         (levels * (rows - 4), members, width),
         (levels * 6, members, width),
         ((rows - 4) * members, width),
-        (6, levels * rows, width),
-        (rows * members, width),
-        (6, rows, width),
+        (levels, 6, rows, width),
     )
     return pl.pallas_call(
         functools.partial(interior_kernel, dims),
         name="interior",
         out_shape=[VMEM(s, F32) for s in shapes] + [VMEM(pw.shape, BF16)],
-        in_specs=[IN_VMEM] * 5 + [IN_HBM],
-        out_specs=[IN_VMEM] * 7,
-        scratch_shapes=[VMEM((rows * members, width), F32), pltpu.SemaphoreType.DMA],
+        in_specs=[IN_VMEM] * 2 + [IN_HBM],
+        out_specs=[IN_VMEM] * 5,
+        scratch_shapes=[pltpu.SemaphoreType.DMA],
         **grant(8, 60_000_000, 12_000_000),
-    )(*near(state, fields, edge, west, east), *far(pw))
+    )(*near(state, fields), *far(pw))
 
 
 def boundary_kernel(dims, lat_size, slots, blocks_dev, block_of, row_of, count,
-                    state, part, inner_content, coef, halo1, strip, pw, corner_s, corner_n, below, above,
-                    outer, *rest):
-    members, levels, rows, width = dims
-    outs, (low_coef, high_coef, content, content16, rays, ends) = rest[:lat_size], rest[lat_size:]
+                    state, part, inner_content, coef, pw, fix_sum, below, above, outer, *rest):
+    members, levels, rows, _ = dims
+    outs, (content, content16, rays) = rest[:lat_size], rest[lat_size:]
     groups = members // SUB
-    step = width // levels
     tail = 2 * levels * members
-    for source, target in ((below, low_coef), (above, high_coef)):
-        got = [source[pl.ds(tail + f * levels, levels), :] for f in range(4)]
-        for k, c in enumerate(stencil(*got)):
-            target[k] = c
-    for i, (y, k, corner) in enumerate(((0, 3, corner_s), (rows - 1, 4, corner_n))):
-        c = spread(strip, k, y)
-        for g in range(groups):
-            at = pl.ds(g * SUB, SUB)
-            ends[i, at, :] = halo1[pl.ds(y * members + g * SUB, SUB), :] + c * corner[at, :]
     edge_rows = (0, 1, rows - 2, rows - 1)
     for y in edge_rows:
         at = pl.ds(y * members, members)
-        content[at, :] = jnp.zeros((members, width), F32)
-    content[pl.ds(2 * members, (rows - 4) * members), :] = inner_content[...]
-
-    def level(l, carry):
-        turn = (width - step * l) % width
+        content[at, :] = fix_sum[at, :]
+    middle = pl.ds(2 * members, (rows - 4) * members)
+    content[middle, :] = inner_content[...] + fix_sum[middle, :]
+
+    def level(l, half):
         base = pl.multiple_of(l * rows, rows)
 
         def halo_row(ref, r):
             start = pl.multiple_of((l * 2 + r) * members, members)
             return [ref[pl.ds(start + g * SUB, SUB), :] for g in range(groups)]
 
+        def halo_coefs(ref):
+            values = ref[pl.ds(pl.multiple_of(tail + (l - half) * 4, SUB), SUB), :]
+            return closed(stencil(*[spread(values, half * 4 + f) for f in range(4)]))
+
         def load(ref, row):
             return [ref[row, pl.ds(g * SUB, SUB), :] for g in range(groups)]
 
-        def side(ref):
-            return [ref[pl.ds(g * SUB, SUB), :] for g in range(groups)]
-
         def add(partial, c, values):
             return [q + c * v for q, v in zip(partial, values)]
 
         south1, north1 = halo_row(below, 1), halo_row(above, 0)
-        lower = advance(south1, halo_row(below, 0), load(state, base), side(corner_s), turn,
-                        [spread(low_coef, k, l) for k in range(6)], width)
-        upper = advance(north1, load(state, base + rows - 1), halo_row(above, 1), side(corner_n), turn,
-                        [spread(high_coef, k, l) for k in range(6)], width)
-        c_first = [spread(coef, k, base) for k in range(6)]
-        c_last = [spread(coef, k, base + rows - 1) for k in range(6)]
+        lower = advance(south1, halo_row(below, 0), load(state, base), halo_coefs(below))
+        upper = advance(north1, load(state, base + rows - 1), halo_row(above, 1), halo_coefs(above))
+        tiles = [coef[l, k] for k in range(6)]
+        c_first = [spread(t, 0) for t in tiles]
+        c_last = [spread(t, rows - 1) for t in tiles]
         first = add(load(part, l * 6), c_first[3], south1)
         last = add(load(part, l * 6 + 3), c_last[4], north1)
         done = (
-            advance(first, lower, load(part, l * 6 + 1), side(ends.at[0]), turn, c_first, width),
-            add(load(part, l * 6 + 4), spread(coef, 3, base + 1), first),
-            add(load(part, l * 6 + 5), spread(coef, 4, base + rows - 2), last),
-            advance(last, load(part, l * 6 + 2), upper, side(ends.at[1]), turn, c_last, width),
+            advance(first, lower, load(part, l * 6 + 1), c_first),
+            add(load(part, l * 6 + 4), spread(tiles[3], 1), first),
+            add(load(part, l * 6 + 5), spread(tiles[4], rows - 2), last),
+            advance(last, load(part, l * 6 + 2), upper, c_last),
         )
         for i, y in enumerate(edge_rows):
             for g in range(groups):
                 content[pl.ds(y * members + g * SUB, SUB), :] += done[i][g]
                 outer[l * 4 + i, pl.ds(g * SUB, SUB), :] = done[i][g]
+
+    def two_levels(q, carry):
+        for half in range(2):
+            level(q * 2 + half, half)
         return carry
 
-    lax.fori_loop(0, levels, level, 0)
+    lax.fori_loop(0, levels // 2, two_levels, 0)
     content16[...] = (content[...] / math.sqrt(levels)).astype(BF16)
     rays[...] = jnp.zeros_like(rays)
     live = count[0]
@@ -333,8 +418,8 @@
         picked = content16[pl.ds(pl.multiple_of(row_of[k] * members, members), members), :]
         partial = jnp.dot(picked, pw[k], preferred_element_type=F32)
         partial = jnp.where(k < live, partial, 0.0)
-        owner = lax.rem(block_of[k] // blocks_dev - mine + lat_size, lat_size)
-        place = owner * blocks_dev + lax.rem(block_of[k], blocks_dev)
+        place = block_of[k] - mine * blocks_dev
+        place = jnp.where(place < 0, place + lat_size * blocks_dev, place)
         at = pl.ds(pl.multiple_of(place * members, members), members)
         rays[at, :] += partial
     size = blocks_dev * members
@@ -342,7 +427,7 @@
         outs[s][...] = rays[pl.ds(s * size, size), :]
 
 
-def boundary(dims, state, inside, corner_s, corner_n, below, above, block_of, row_of, count, lat_size, blocks_dev):
+def boundary(dims, state, inside, fix_sum, below, above, block_of, row_of, count, lat_size, blocks_dev):
     members, levels, rows, width = dims
     slots, _, block = inside[-1].shape
     size = blocks_dev * members
@@ -350,23 +435,22 @@
         functools.partial(boundary_kernel, dims, lat_size, slots, blocks_dev),
         name="boundary_rays",
         out_shape=[VMEM((levels * 4, members, width), F32)] + [VMEM((size, block), F32)] * lat_size,
-        in_specs=[IN_SMEM] * 3 + [IN_VMEM] * 11,
+        in_specs=[IN_SMEM] * 3 + [IN_VMEM] * 8,
         out_specs=[IN_VMEM] * (1 + lat_size),
         scratch_shapes=[
-            VMEM((6, levels, width), F32),
-            VMEM((6, levels, width), F32),
             VMEM((rows * members, width), F32),
             VMEM((rows * members, width), BF16),
             VMEM((lat_size * size, block), F32),
-            VMEM((2, members, width), F32),
         ],
         **grant(8, 30_000_000, 12_000_000),
-    )(block_of, row_of, count, *near(state, *inside, corner_s, corner_n, below, above))
-
-
-def spread_kernel(dims, inner, outer, hi_ref, lo_hbm, centre_ref, lo_ref, sem):
+    )(block_of, row_of, count, *near(state, *inside, fix_sum, below, above))
+
+
+def spread_kernel(dims, inner, outer, fix, hi_ref, lo_hbm, centre_ref, lo_ref, sem):
     members, levels, rows, width = dims
     sub = subs_of((rows, width))
+    lane = lanes_of((members, width))
+    near_edge = (lane < 2) | (lane >= width - 2)
     edge_rows = {0: 0, 1: 1, rows - 2: 2, rows - 1: 3}
 
     def pair(q, carry):
@@ -375,6 +459,8 @@
             mean = jnp.zeros((rows, width), F32)
             for y in range(rows):
                 v = outer[l * 4 + edge_rows[y]] if y in edge_rows else inner[l * (rows - 4) + y - 2]
+                turned = pltpu.roll(fix[pl.ds(y * members, members), :], (width - (width // levels) * l) % width, 1)
+                v = v + jnp.where(near_edge, turned, 0.0)
                 m = jnp.sum(v, axis=0, keepdims=True) / members
                 mean = jnp.where(sub == y, m, mean)
                 a = v - m
@@ -394,18 +480,18 @@
     lax.fori_loop(0, levels // 2, finish, 0)
 
 
-def anomalies(dims, inner, outer):
+def anomalies(dims, inner, outer, fix):
     members, levels, rows, width = dims
     shape = (levels // 2, rows * members, 2 * width)
     return pl.pallas_call(
         functools.partial(spread_kernel, dims),
         name="anomalies",
         out_shape=(VMEM(shape, BF16), pltpu.HBM(shape, BF16), VMEM((levels * rows, width), F32)),
-        in_specs=[IN_VMEM] * 2,
+        in_specs=[IN_VMEM] * 3,
         out_specs=[IN_VMEM, IN_HBM, IN_VMEM],
         scratch_shapes=[VMEM(shape, BF16), pltpu.SemaphoreType.DMA((levels // 2,))],
         **grant(8, 8_000_000, 8_000_000),
-    )(*near(inner, outer))
+    )(*near(inner, outer, fix))
 
 
 def moments_kernel(members, blocks_dev, block, n_parts, devices, *refs):
@@ -574,27 +660,25 @@
     lat_size, lon_size = lax.axis_size("lat"), lax.axis_size("lon")
     block = path_weight.shape[2]
     blocks_dev = observed.shape[0] // block
-    step = width // levels
     ring = lambda n, s: [(i, (i + s) % n) for i in range(n)]
     up = [(i, i + 1) for i in range(lat_size - 1)]
     down = [(j, i) for i, j in up]
 
     fields = (east_courant, north_courant, production, loss_rate)
-    state, to_north, to_south, edge, local = pack(sample_deviations, fields)
-    west = lax.ppermute(edge, "lon", ring(lon_size, 1))
-    east = lax.ppermute(edge, "lon", ring(lon_size, lon_size - 1))
+    state, to_north, to_south, edge, to_east, to_west, local = pack(sample_deviations, fields)
+    west = lax.ppermute(to_east, "lon", ring(lon_size, 1))
+    east = lax.ppermute(to_west, "lon", ring(lon_size, lon_size - 1))
     below = lax.ppermute(to_north, "lat", up)
     above = lax.ppermute(to_south, "lat", down)
-    from_west = ((jnp.arange(width) + 2) % step < 2)[None, :]
-    top = slice((rows - 1) * members, rows * members)
-    corner_s = lax.ppermute(jnp.where(from_west, west[top], east[top]), "lat", up)
-    corner_n = lax.ppermute(jnp.where(from_west, west[:members], east[:members]), "lat", down)
-
-    inner, *inside = interior(dims, state, local, edge, west, east, path_weight)
-    outer, *sums = boundary(dims, state, inside, corner_s, corner_n, below, above,
+    inner, *inside = interior(dims, state, local, path_weight)
+    first, last = corners(dims, edge, west, east)
+    corner_s = lax.ppermute(last, "lat", up)
+    corner_n = lax.ppermute(first, "lat", down)
+    fix, fix_sum = columns(dims, edge, west, east, corner_s, corner_n)
+    outer, *sums = boundary(dims, state, inside, fix_sum, below, above,
                             entry_block, entry_row, entry_count, lat_size, blocks_dev)
     got = [sums[0]] + [lax.ppermute(sums[s], "lat", ring(lat_size, s)) for s in range(1, lat_size)]
-    hi, lo, centre = anomalies(dims, inner, outer)
+    hi, lo, centre = anomalies(dims, inner, outer, fix)
     devices = lat_size * lon_size
     prior, innovation, packed = moments(got, observed.reshape(blocks_dev, block), obs_var.reshape(blocks_dev, block),
                                         centre, members, blocks_dev, block, devices)

time: 73.4 us -> 70.6 us (0.962)
  waiting for transfers between devices: 8.83 us -> 2.36 us
  blocking collectives: 9.89 us -> 13.1 us
  starting transfers between devices: 18.5 us -> 20.4 us
  Pallas kernels: 34.5 us -> 33.1 us
    ppermute x4, waiting for transfers between devices: 8.33 us -> 2.35 us  [the longest x1 2.34 us: per_device(): west = lax.ppermute(to_east, 'lon', ring(lon_size, 1))]
    pallas_call x0 -> x2, Pallas kernels: none -> 3.67 us  [the longest x1 3.59 us: columns(): pl.pallas_call(functools.partial(columns_kernel, dims), name='columns', o...]
    pallas_call x1, Pallas kernels: 7 us -> 3.46 us  [boundary(): pl.pallas_call(functools.partial(boundary_kernel, dims, lat_size, slots,...]
    pallas_call x1, Pallas kernels: 10.2 us -> 6.89 us  [interior(): pl.pallas_call(functools.partial(interior_kernel, dims), name='interior',...]
    all_to_all x1, blocking collectives: 9.89 us -> 13.1 us  [per_device(): gathered = lax.all_to_all(packed, ('lon', 'lat'), 0, 0, tiled=True)]
    ppermute x3, starting transfers between devices: 4.56 us -> 6.53 us  [per_device(): lax.ppermute(sums[s], 'lat', ring(lat_size, s))]
    pallas_call x1, Pallas kernels: 2.13 us -> 3.91 us  [anomalies(): pl.pallas_call(functools.partial(spread_kernel, dims), name='anomalies',...]
  transfers between devices with their start and end apart: 9 -> 9, of which waited for: 3 -> 1; matrix products, arithmetic and copies ran while one was open for 0% -> 0% of each run, Pallas kernels for 17% -> 21%
where the time goes in v3:
time: 70.6 us; the launch traced here: 70.4 us
  Pallas kernels  33.1 us (47%)
  starting transfers between devices  20.4 us (29%)
  blocking collectives  13.1 us (19%)
  waiting for transfers between devices  2.36 us (3%)
  between operations  1.45 us (2%)
    all_to_all x1, blocking collectives, per_device(): gathered = lax.all_to_all(packed, ('lon', 'lat'), 0, 0, tiled=True)  13.1 us
    pallas_call x1, Pallas kernels, update(): pl.pallas_call(functools.partial(update_kernel, dims, devices), name='upd...  9.6 us
    pallas_call x1, Pallas kernels, interior(): pl.pallas_call(functools.partial(interior_kernel, dims), name='interior',...  6.89 us
    ppermute x3, starting transfers between devices, per_device(): lax.ppermute(sums[s], 'lat', ring(lat_size, s))  6.53 us
    pallas_call x1, Pallas kernels, pack(): pl.pallas_call(functools.partial(pack_kernel, x.shape, chunks), name='pac...  4.86 us
    pallas_call x1, Pallas kernels, anomalies(): pl.pallas_call(functools.partial(spread_kernel, dims), name='anomalies',...  3.91 us
    pallas_call x1, Pallas kernels, columns(): pl.pallas_call(functools.partial(columns_kernel, dims), name='columns', o...  3.59 us
    pallas_call x1, Pallas kernels, boundary(): pl.pallas_call(functools.partial(boundary_kernel, dims, lat_size, slots,...  3.46 us
  transfers between devices with their start and end apart: 9, of which 1 were waited for; matrix products, arithmetic and copies ran while one was open for 0% of the time, Pallas kernels for 21%

profile of v3, /device:TPU:0, one launch (start us, length us, event | category | flops | bytes accessed | tf_op | source)
XLA Modules:
  0.0 70.4 jit_solution(11526424772665672150)
XLA Ops:
  0.6 4.9 %pack_halos.1 = (f32[256,32,128]{2,1,0:T(8,128)S(1)}, f32[2176,128]{1,0:T(8,128)S(1)}, f32[2176,128]{1,0:T(8,128)S(1)}, f32[288,128]{1,0:T(8,128)S(1)}, f32[144,...) custom-call(f32[32,32,8,128]{3,2,1,0:T(8,128)} %x_hbm.1, f32[32,8,128]{2,1,0:T(8,128)} %e_hbm.1, ...), custom_call_target="tpu_custom_call" | custom-call | flops 4000000 | bytes 8000000 | tf_op jit(solution)/shard_map/pack_halos/pallas_call | solution.py:116
  5.5 2.5 %collective-permute-start.4 = (f32[2176,128]{1,0:T(8,128)S(1)}, f32[2176,128]{1,0:T(8,128)S(1)}, u32[]{:S(2)}, u32[]{:S(2)}) collective-permute-start(f32[2176,128]{1,0:T(8,128)S(1)} %get-tuple-element.42), channel_id=1, source_target_pairs={{0,1},{1,2},{2,3},{4,5},{5,6},{6,7},{8,9},{9,10},{10,11},{12,13},{... | collective-permute-start | bytes 3342344 | tf_op jit(solution)/shard_map/ppermute | solution.py:671
  8.0 1.3 %collective-permute-start.5 = (f32[2176,128]{1,0:T(8,128)S(1)}, f32[2176,128]{1,0:T(8,128)S(1)}, u32[]{:S(2)}, u32[]{:S(2)}) collective-permute-start(f32[2176,128]{1,0:T(8,128)S(1)} %get-tuple-element.43), channel_id=1, source_target_pairs={{1,0},{2,1},{3,2},{5,4},{6,5},{7,6},{9,8},{10,9},{11,10},{13,12},{... | collective-permute-start | bytes 3342344 | tf_op jit(solution)/shard_map/ppermute | solution.py:672
  9.3 2.4 %collective-permute-start = (f32[144,128]{1,0:T(8,128)S(1)}, f32[144,128]{1,0:T(8,128)S(1)}, u32[]{:S(2)}, u32[]{:S(2)}) collective-permute-start(f32[144,128]{1,0:T(8,128)S(1)} %get-tuple-element.37), channel_id=1, source_target_pairs={{0,4},{4,8},{8,12},{12,16},{16,20},{20,24},{24,28},{28,0},{1,5},{5... | collective-permute-start | bytes 221192 | tf_op jit(solution)/shard_map/ppermute | solution.py:669
  11.7 3.1 %collective-permute-start.1 = (f32[144,128]{1,0:T(8,128)S(1)}, f32[144,128]{1,0:T(8,128)S(1)}, u32[]{:S(2)}, u32[]{:S(2)}) collective-permute-start(f32[144,128]{1,0:T(8,128)S(1)} %get-tuple-element.38), channel_id=1, source_target_pairs={{0,28},{4,0},{8,4},{12,8},{16,12},{20,16},{24,20},{28,24},{1,29},{... | collective-permute-start | bytes 221192 | tf_op jit(solution)/shard_map/ppermute | solution.py:670
  14.8 2.3 %collective-permute-done.west = f32[144,128]{1,0:T(8,128)S(1)} collective-permute-done((f32[144,128]{1,0:T(8,128)S(1)}, f32[144,128]{1,0:T(8,128)S(1)}, u32[]{:S(2)}, u32[]{:S(2)}) %collective-permute-start) | collective-permute-done | bytes 73760 | tf_op jit(solution)/shard_map/ppermute | solution.py:669
  17.1 0.0 collective-permute-done.1.east
  17.1 0.1 corners.1
  17.2 3.3 %collective-permute-start.2 = (f32[40,128]{1,0:T(8,128)S(1)}, f32[40,128]{1,0:T(8,128)S(1)}, u32[]{:S(2)}, u32[]{:S(2)}) collective-permute-start(f32[40,128]{1,0:T(8,128)S(1)} %get-tuple-element.39), channel_id=1, source_target_pairs={{0,1},{1,2},{2,3},{4,5},{5,6},{6,7},{8,9},{9,10},{10,11},{12,13},{... | collective-permute-start | bytes 61448 | tf_op jit(solution)/shard_map/ppermute | solution.py:675
  20.5 1.3 %collective-permute-start.3 = (f32[40,128]{1,0:T(8,128)S(1)}, f32[40,128]{1,0:T(8,128)S(1)}, u32[]{:S(2)}, u32[]{:S(2)}) collective-permute-start(f32[40,128]{1,0:T(8,128)S(1)} %get-tuple-element.40), channel_id=1, source_target_pairs={{1,0},{2,1},{3,2},{5,4},{6,5},{7,6},{9,8},{10,9},{11,10},{13,12},{... | collective-permute-start | bytes 61448 | tf_op jit(solution)/shard_map/ppermute | solution.py:676
  22.4 0.0 copy-start.2
  22.4 0.0 copy-start.3
  22.5 6.9 %interior.1 = (f32[128,32,128]{2,1,0:T(8,128)S(1)}, f32[192,32,128]{2,1,0:T(8,128)S(1)}, f32[128,128]{1,0:T(8,128)S(1)}, f32[32,6,8,128]{3,2,1,0:T(8,128)S(1)}, bf16[48,128,128]{2,1,0:T(8,128)(2,1)S(1)}) custom-call(f32[256,32,128]{2,1,0:T(8,128)S(1)} %get-tuple-element.30.state, f32[4,32,8,128]{3,2,1,0:T(8,128)S(1)} %get-tuple-element.31.fields, ...), custom_call_target="tpu_custom_call" | custom-call | flops 60000000 | bytes 12000000 | tf_op jit(solution)/shard_map/interior/pallas_call | solution.py:347
  29.4 0.0 collective-permute-done.2.corner_s
  29.4 3.6 %columns.1 = (f32[256,128]{1,0:T(8,128)S(1)}, f32[256,128]{1,0:T(8,128)S(1)}) custom-call(f32[288,128]{1,0:T(8,128)S(1)} %get-tuple-element.36.edge, f32[144,128]{1,0:T(8,128)S(1)} %collective-permute-done.west, f32[144,128]{1,0:T(8,128)S(1)} %collective-permute-done.1.east, f32[40,128]{1,0:T(8,128)S(1)} %collective-permute-done.2.corner_s, ...), custom_call_target="tpu_custom_call" | custom-call | flops 2000000 | bytes 1000000 | tf_op jit(solution)/shard_map/columns/pallas_call | solution.py:281
  33.0 0.0 collective-permute-done.4.below
  33.0 3.5 %boundary_rays.1 = (f32[128,32,128]{2,1,0:T(8,128)S(1)}, f32[128,128]{1,0:T(8,128)S(1)}, f32[128,128]{1,0:T(8,128)S(1)}, f32[128,128]{1,0:T(8,128)S(1)}, f32[128,128]{1,0:T(8,128)S(1)}) custom-call(s32[48]{0:T(128)S(1)} %copy-done.2, s32[48]{0:T(128)S(1)} %copy-done.3, s32[1]{0:T(128)S(6)} %copy.14.count, f32[256,32,128]{2,1,0:T(8,128)S(1)} %get-tuple-element.30.state, ...), custom_call_target="tpu_custom_call" | custom-call | flops 30000000 | bytes 12000000 | tf_op jit(solution)/shard_map/boundary_rays/pallas_call | solution.py:434
  36.5 3.4 %collective-permute-start.6 = (f32[128,128]{1,0:T(8,128)S(1)}, f32[128,128]{1,0:T(8,128)S(1)}, u32[]{:S(2)}, u32[]{:S(2)}) collective-permute-start(f32[128,128]{1,0:T(8,128)S(1)} %get-tuple-element.45), channel_id=1, source_target_pairs={{0,1},{1,2},{2,3},{3,0},{4,5},{5,6},{6,7},{7,4},{8,9},{9,10},{10,1... | collective-permute-start | bytes 196616 | tf_op jit(solution)/shard_map/ppermute | solution.py:680
  39.9 1.7 %collective-permute-start.7 = (f32[128,128]{1,0:T(8,128)S(1)}, f32[128,128]{1,0:T(8,128)S(1)}, u32[]{:S(2)}, u32[]{:S(2)}) collective-permute-start(f32[128,128]{1,0:T(8,128)S(1)} %get-tuple-element.46), channel_id=1, source_target_pairs={{0,2},{1,3},{2,0},{3,1},{4,6},{5,7},{6,4},{7,5},{8,10},{9,11},{10,... | collective-permute-start | bytes 196616 | tf_op jit(solution)/shard_map/ppermute | solution.py:680
  41.6 1.4 %collective-permute-start.8 = (f32[128,128]{1,0:T(8,128)S(1)}, f32[128,128]{1,0:T(8,128)S(1)}, u32[]{:S(2)}, u32[]{:S(2)}) collective-permute-start(f32[128,128]{1,0:T(8,128)S(1)} %get-tuple-element.47), channel_id=1, source_target_pairs={{0,3},{1,0},{2,1},{3,2},{4,7},{5,4},{6,5},{7,6},{8,11},{9,8},{10,9... | collective-permute-start | bytes 196616 | tf_op jit(solution)/shard_map/ppermute | solution.py:680
  43.0 3.9 %anomalies.1 = (bf16[16,256,256]{2,1,0:T(8,128)(2,1)S(1)}, bf16[16,256,256]{2,1,0:T(8,128)(2,1)}, f32[256,128]{1,0:T(8,128)S(1)}) custom-call(f32[128,32,128]{2,1,0:T(8,128)S(1)} %get-tuple-element.48.inner, f32[128,32,128]{2,1,0:T(8,128)S(1)} %get-tuple-element.49.outer, f32[256,128]{1,0:T(8,128)S(1)} %get-tuple-element.50.fix), custom_call_target="tpu_custom_call" | custom-call | flops 8000000 | bytes 8000000 | tf_op jit(solution)/shard_map/anomalies/pallas_call | solution.py:486
  47.0 0.7 moments.1
  47.7 13.1 %all_to_all.11 = f32[32,8,128]{2,1,0:T(8,128)S(1)} all-to-all(f32[32,8,128]{2,1,0:T(8,128)S(1)} %bitcast.6), channel_id=1, replica_groups=mesh['lon'=8,'lat'=4] {'lon','lat'}, dimensions={0} | all-to-all | bytes 262144 | tf_op jit(solution)/shard_map/all_to_all | solution.py:685
  60.8 9.6 %update.1 = f32[32,32,8,128]{3,2,1,0:T(8,128)} custom-call(f32[256,128]{1,0:T(8,128)S(1)} %bitcast.5, bf16[16,256,256]{2,1,0:T(8,128)(2,1)S(1)} %get-tuple-element.53.hi_ref, f32[256,128]{1,0:T(8,128)S(1)} %get-tuple-element.51.refs_6_.centre_ref, bf16[16,256,256]{2,1,0:T(8,128)(2,1)} %get-tuple-element.54.lo_hbm), custom_call_target="tpu_custom_call" | custom-call | flops 2000000000 | bytes 8000000 | tf_op jit(solution)/shard_map/update/pallas_call | solution.py:645
  (11 shorter events, 0.0 us)
Async XLA Ops:
  5.5 27.5 %collective-permute-start.4 = (f32[2176,128]{1,0:T(8,128)S(1)}, f32[2176,128]{1,0:T(8,128)S(1)}, u32[]{:S(2)}, u32[]{:S(2)}) collective-permute-start(f32[2176,128]{1,0:T(8,128)S(1)} %get-tuple-element.42), channel_id=1, source_target_pairs={{0,1},{1,2},{2,3},{4,5},{5,6},{6,7},{8,9},{9,10},{10,11},{12,13},{... | collective-permute-start | bytes 3342344 | tf_op jit(solution)/shard_map/ppermute | solution.py:671
  8.0 25.0 %collective-permute-start.5 = (f32[2176,128]{1,0:T(8,128)S(1)}, f32[2176,128]{1,0:T(8,128)S(1)}, u32[]{:S(2)}, u32[]{:S(2)}) collective-permute-start(f32[2176,128]{1,0:T(8,128)S(1)} %get-tuple-element.43), channel_id=1, source_target_pairs={{1,0},{2,1},{3,2},{5,4},{6,5},{7,6},{9,8},{10,9},{11,10},{13,12},{... | collective-permute-start | bytes 3342344 | tf_op jit(solution)/shard_map/ppermute | solution.py:672
  9.3 7.8 %collective-permute-start = (f32[144,128]{1,0:T(8,128)S(1)}, f32[144,128]{1,0:T(8,128)S(1)}, u32[]{:S(2)}, u32[]{:S(2)}) collective-permute-start(f32[144,128]{1,0:T(8,128)S(1)} %get-tuple-element.37), channel_id=1, source_target_pairs={{0,4},{4,8},{8,12},{12,16},{16,20},{20,24},{24,28},{28,0},{1,5},{5... | collective-permute-start | bytes 221192 | tf_op jit(solution)/shard_map/ppermute | solution.py:669
  11.7 5.5 %collective-permute-start.1 = (f32[144,128]{1,0:T(8,128)S(1)}, f32[144,128]{1,0:T(8,128)S(1)}, u32[]{:S(2)}, u32[]{:S(2)}) collective-permute-start(f32[144,128]{1,0:T(8,128)S(1)} %get-tuple-element.38), channel_id=1, source_target_pairs={{0,28},{4,0},{8,4},{12,8},{16,12},{20,16},{24,20},{28,24},{1,29},{... | collective-permute-start | bytes 221192 | tf_op jit(solution)/shard_map/ppermute | solution.py:670
  17.2 12.2 %collective-permute-start.2 = (f32[40,128]{1,0:T(8,128)S(1)}, f32[40,128]{1,0:T(8,128)S(1)}, u32[]{:S(2)}, u32[]{:S(2)}) collective-permute-start(f32[40,128]{1,0:T(8,128)S(1)} %get-tuple-element.39), channel_id=1, source_target_pairs={{0,1},{1,2},{2,3},{4,5},{5,6},{6,7},{8,9},{9,10},{10,11},{12,13},{... | collective-permute-start | bytes 61448 | tf_op jit(solution)/shard_map/ppermute | solution.py:675
  20.5 8.9 %collective-permute-start.3 = (f32[40,128]{1,0:T(8,128)S(1)}, f32[40,128]{1,0:T(8,128)S(1)}, u32[]{:S(2)}, u32[]{:S(2)}) collective-permute-start(f32[40,128]{1,0:T(8,128)S(1)} %get-tuple-element.40), channel_id=1, source_target_pairs={{1,0},{2,1},{3,2},{5,4},{6,5},{7,6},{9,8},{10,9},{11,10},{13,12},{... | collective-permute-start | bytes 61448 | tf_op jit(solution)/shard_map/ppermute | solution.py:676
  22.4 10.6 %copy-start.2 = (s32[48]{0:T(128)S(1)}, s32[48]{0:T(128)}, u32[]{:S(2)}) copy-start(s32[48]{0:T(128)} %block_of.1) | copy-start | bytes 580
  22.4 10.6 %copy-start.3 = (s32[48]{0:T(128)S(1)}, s32[48]{0:T(128)}, u32[]{:S(2)}) copy-start(s32[48]{0:T(128)} %row_of.1) | copy-start | bytes 580
  36.5 10.5 %collective-permute-start.6 = (f32[128,128]{1,0:T(8,128)S(1)}, f32[128,128]{1,0:T(8,128)S(1)}, u32[]{:S(2)}, u32[]{:S(2)}) collective-permute-start(f32[128,128]{1,0:T(8,128)S(1)} %get-tuple-element.45), channel_id=1, source_target_pairs={{0,1},{1,2},{2,3},{3,0},{4,5},{5,6},{6,7},{7,4},{8,9},{9,10},{10,1... | collective-permute-start | bytes 196616 | tf_op jit(solution)/shard_map/ppermute | solution.py:680
  39.9 7.0 %collective-permute-start.7 = (f32[128,128]{1,0:T(8,128)S(1)}, f32[128,128]{1,0:T(8,128)S(1)}, u32[]{:S(2)}, u32[]{:S(2)}) collective-permute-start(f32[128,128]{1,0:T(8,128)S(1)} %get-tuple-element.46), channel_id=1, source_target_pairs={{0,2},{1,3},{2,0},{3,1},{4,6},{5,7},{6,4},{7,5},{8,10},{9,11},{10,... | collective-permute-start | bytes 196616 | tf_op jit(solution)/shard_map/ppermute | solution.py:680
  41.6 5.3 %collective-permute-start.8 = (f32[128,128]{1,0:T(8,128)S(1)}, f32[128,128]{1,0:T(8,128)S(1)}, u32[]{:S(2)}, u32[]{:S(2)}) collective-permute-start(f32[128,128]{1,0:T(8,128)S(1)} %get-tuple-element.47), channel_id=1, source_target_pairs={{0,3},{1,0},{2,1},{3,2},{4,7},{5,4},{6,5},{7,6},{8,11},{9,8},{10,9... | collective-permute-start | bytes 196616 | tf_op jit(solution)/shard_map/ppermute | solution.py:680
  43.0 4.0 %copy-start = (f32[512]{0:T(512)S(1)}, f32[512]{0:T(512)}, u32[]{:S(2)}) copy-start(f32[512]{0:T(512)} %param.20) | copy-start | bytes 6148
  43.0 4.0 %copy-start.1 = (f32[512]{0:T(512)S(1)}, f32[512]{0:T(512)}, u32[]{:S(2)}) copy-start(f32[512]{0:T(512)} %param.21) | copy-start | bytes 6148

commit v4 on v3

--- a/solution.py
+++ b/solution.py
@@ -209,14 +209,29 @@
     )(*near(edge, west, east))
 
 
-def columns_kernel(dims, edge, west, east, corner_s, corner_n, fix, fix_sum, halo, change, halo1):
+def change_of(values, cw, ce, step):
+    width = values.shape[1]
+    kind = lanes_of(values.shape) % step
+    entering = jnp.where(kind == 0, cw * pltpu.roll(values, 1, 1), 0.0)
+    return jnp.where(kind == step - 1, ce * pltpu.roll(values, width - 1, 1), entering)
+
+
+def level_sums(tiles, step):
+    width = tiles[0].shape[1]
+    lane = lanes_of(tiles[0].shape)
+    shift = step
+    while shift < width:
+        tiles = [t + pltpu.roll(t, shift, 1) for t in tiles]
+        shift *= 2
+    return [jnp.where((lane < 2) | (lane >= width - 2), t, 0.0) for t in tiles]
+
+
+def columns_kernel(dims, edge, west, east, fix, fix_sum, side):
     members, levels, rows, width = dims
     groups = members // SUB
     step = width // levels
-    lane = lanes_of((SUB, width))
-    kind = lane % step
+    kind = lanes_of((SUB, width)) % step
     from_west = west_lanes(width, step)
-    is_first, is_last = kind == 0, kind == step - 1
     start = rows * members
     outside = []
     for f in range(4):
@@ -225,55 +240,47 @@
                                  open_strip(east, base, f % 2, -2, width)))
     outside = stencil(*outside)
     own = stencil(*[edge[pl.ds(start + f * rows, rows), :] for f in range(4)])
-
-    def change_of(values, cw, ce):
-        entering = jnp.where(is_first, cw * pltpu.roll(values, 1, 1), 0.0)
-        return jnp.where(is_last, ce * pltpu.roll(values, width - 1, 1), entering)
-
-    for y in range(-1, rows + 1):
-        if y < 0 or y >= rows:
-            source = corner_s if y < 0 else corner_n
-            fields = source[pl.ds(members, SUB), :]
-            c = stencil(*[spread(fields, f) for f in range(4)])
-            cw, ce = c[1], c[2]
-        else:
-            cw, ce = spread(own[1], y), spread(own[2], y)
-        for g in range(groups):
-            at = pl.ds((y + 1) * members + g * SUB, SUB)
-            if y < 0 or y >= rows:
-                values = source[pl.ds(g * SUB, SUB), :]
-            else:
-                base = (y // 2) * members + g * SUB
-                values = jnp.where(from_west, open_strip(west, base, y % 2, 2, width),
-                                   open_strip(east, base, y % 2, -2, width))
-            halo[at, :] = values
-            change[at, :] = change_of(values, cw, ce)
-    for y in range(rows):
-        c0, cw, ce, cs, cn, p = [spread(t, y) for t in outside]
-        k0, kw, ke, ks, kn, _ = [spread(t, y) for t in own]
-        for g in range(groups):
-            at = pl.ds(y * members + g * SUB, SUB)
-            low, mid, high = [pl.ds((y + d) * members + g * SUB, SUB) for d in range(3)]
+    all_tiles = []
+    for g in range(groups):
+        halo, change, side_w, side_e = [], [], [], []
+        for y in range(rows):
             base = (y // 2) * members + g * SUB
-            inner = edge[at, :]
             aw = open_strip(west, base, y % 2, 2, width)
             ae = open_strip(east, base, y % 2, -2, width)
-            side_w = jnp.where(from_west, pltpu.roll(aw, 1, 1), pltpu.roll(inner, 1, 1))
-            side_e = jnp.where(from_west, pltpu.roll(inner, width - 1, 1), pltpu.roll(ae, width - 1, 1))
-            beyond = (c0 * halo[mid, :] + cw * side_w) + (ce * side_e + cs * halo[low, :]) + (cn * halo[high, :] + p)
-            moved = change[mid, :]
-            total = k0 * moved + ks * change[low, :] + kn * change[high, :] + change_of(beyond, kw, ke)
-            total = jnp.where(kind == 1, kw * pltpu.roll(moved, 1, 1), total)
-            total = jnp.where(kind == 2, ke * pltpu.roll(moved, width - 1, 1), total)
-            fix[at, :] = total
-            shift = step
-            while shift < width:
-                total = total + pltpu.roll(total, shift, 1)
-                shift *= 2
-            fix_sum[at, :] = jnp.where((lane < 2) | (lane >= width - 2), total, 0.0)
-
-
-def columns(dims, edge, west, east, corner_s, corner_n):
+            inner = edge[pl.ds(y * members + g * SUB, SUB), :]
+            halo.append(jnp.where(from_west, aw, ae))
+            change.append(change_of(halo[-1], spread(own[1], y), spread(own[2], y), step))
+            side_w.append(pltpu.roll(jnp.where(kind == step - 1, inner, aw), 1, 1))
+            side_e.append(pltpu.roll(jnp.where(kind == 0, inner, ae), width - 1, 1))
+        for y in range(rows):
+            c0, cw, ce, cs, cn, p = [spread(t, y) for t in outside]
+            k0, kw, ke, ks, kn, _ = [spread(t, y) for t in own]
+            beyond = (c0 * halo[y] + cw * side_w[y]) + (ce * side_e[y] + p)
+            total = k0 * change[y]
+            if y > 0:
+                beyond = beyond + cs * halo[y - 1]
+                total = total + ks * change[y - 1]
+            if y < rows - 1:
+                beyond = beyond + cn * halo[y + 1]
+                total = total + kn * change[y + 1]
+            total = total + change_of(beyond, kw, ke, step)
+            total = jnp.where(kind == 1, kw * pltpu.roll(change[y], 1, 1), total)
+            total = jnp.where(kind == 2, ke * pltpu.roll(change[y], width - 1, 1), total)
+            all_tiles.append(total)
+    at = 0
+    for y, own_side, far_side in ((0, own[3], outside[3]), (rows - 1, own[4], outside[4])):
+        for t in (own_side, own[1], own[2], far_side):
+            side[at] = spread(t, y)
+            at += 1
+    sums = level_sums(all_tiles, step)
+    for g in range(groups):
+        for y in range(rows):
+            to = pl.ds(y * members + g * SUB, SUB)
+            fix[to, :] = all_tiles[g * rows + y]
+            fix_sum[to, :] = sums[g * rows + y]
+
+
+def columns(dims, edge, west, east):
     members, levels, rows, width = dims
     if width != 4 * levels:
         raise ValueError("strip width")
@@ -281,12 +288,11 @@
     return pl.pallas_call(
         functools.partial(columns_kernel, dims),
         name="columns",
-        out_shape=[VMEM(shape, F32)] * 2,
-        in_specs=[IN_VMEM] * 5,
-        out_specs=[IN_VMEM] * 2,
-        scratch_shapes=[VMEM(((rows + 2) * members, width), F32)] * 2 + [VMEM(shape, F32)],
+        out_shape=[VMEM(shape, F32)] * 2 + [VMEM((8, SUB, width), F32)],
+        in_specs=[IN_VMEM] * 3,
+        out_specs=[IN_VMEM] * 3,
         **grant(8, 2_000_000, 1_000_000),
-    )(*near(edge, west, east, corner_s, corner_n))
+    )(*near(edge, west, east))
 
 
 def interior_kernel(dims, state, fields, pw_hbm, inner, part, content, coef, pw, pw_sem):
@@ -356,13 +362,29 @@
 
 
 def boundary_kernel(dims, lat_size, slots, blocks_dev, block_of, row_of, count,
-                    state, part, inner_content, coef, pw, fix_sum, below, above, outer, *rest):
-    members, levels, rows, _ = dims
-    outs, (content, content16, rays) = rest[:lat_size], rest[lat_size:]
+                    state, part, inner_content, coef, pw, fix, fix_sum, side, corner_s, corner_n, below, above,
+                    outer_hbm, fix_ends, *rest):
+    members, levels, rows, width = dims
+    outs, (content, content16, rays, outer, outer_sem) = rest[:lat_size], rest[lat_size:]
     groups = members // SUB
     tail = 2 * levels * members
     edge_rows = (0, 1, rows - 2, rows - 1)
-    for y in edge_rows:
+    step = width // levels
+    extras = []
+    for i, (y, corner) in enumerate(((0, corner_s), (rows - 1, corner_n))):
+        fields = corner[pl.ds(members, SUB), :]
+        c = stencil(*[spread(fields, f) for f in range(4)])
+        ks, kw, ke, cs = [side[4 * i + d] for d in range(4)]
+        for g in range(groups):
+            values = corner[pl.ds(g * SUB, SUB), :]
+            extra = ks * change_of(values, c[1], c[2], step) + change_of(cs * values, kw, ke, step)
+            extras.append((i, y, g, extra))
+    sums = level_sums([e[-1] for e in extras], step)
+    for (i, y, g, extra), total in zip(extras, sums):
+        at = pl.ds(y * members + g * SUB, SUB)
+        fix_ends[pl.ds(i * members + g * SUB, SUB), :] = fix[at, :] + extra
+        content[at, :] = fix_sum[at, :] + total
+    for y in (1, rows - 2):
         at = pl.ds(y * members, members)
         content[at, :] = fix_sum[at, :]
     middle = pl.ds(2 * members, (rows - 4) * members)
@@ -404,9 +426,14 @@
                 content[pl.ds(y * members + g * SUB, SUB), :] += done[i][g]
                 outer[l * 4 + i, pl.ds(g * SUB, SUB), :] = done[i][g]
 
+    def put(q):
+        part = pl.ds(q * 8, 8)
+        return pltpu.make_async_copy(outer.at[part], outer_hbm.at[part], outer_sem.at[q])
+
     def two_levels(q, carry):
         for half in range(2):
             level(q * 2 + half, half)
+        put(q).start()
         return carry
 
     lax.fori_loop(0, levels // 2, two_levels, 0)
@@ -425,42 +452,67 @@
     size = blocks_dev * members
     for s in range(lat_size):
         outs[s][...] = rays[pl.ds(s * size, size), :]
-
-
-def boundary(dims, state, inside, fix_sum, below, above, block_of, row_of, count, lat_size, blocks_dev):
+    for q in range(levels // 2):
+        put(q).wait()
+
+
+def boundary(dims, state, inside, sides, corner_s, corner_n, below, above, block_of, row_of, count, lat_size, blocks_dev):
     members, levels, rows, width = dims
     slots, _, block = inside[-1].shape
     size = blocks_dev * members
     return pl.pallas_call(
         functools.partial(boundary_kernel, dims, lat_size, slots, blocks_dev),
         name="boundary_rays",
-        out_shape=[VMEM((levels * 4, members, width), F32)] + [VMEM((size, block), F32)] * lat_size,
-        in_specs=[IN_SMEM] * 3 + [IN_VMEM] * 8,
-        out_specs=[IN_VMEM] * (1 + lat_size),
+        out_shape=[pltpu.HBM((levels * 4, members, width), F32), VMEM((2 * members, width), F32)]
+        + [VMEM((size, block), F32)] * lat_size,
+        in_specs=[IN_SMEM] * 3 + [IN_VMEM] * 12,
+        out_specs=[IN_HBM] + [IN_VMEM] * (1 + lat_size),
         scratch_shapes=[
             VMEM((rows * members, width), F32),
             VMEM((rows * members, width), BF16),
             VMEM((lat_size * size, block), F32),
+            VMEM((levels * 4, members, width), F32),
+            pltpu.SemaphoreType.DMA((levels // 2,)),
         ],
         **grant(8, 30_000_000, 12_000_000),
-    )(block_of, row_of, count, *near(state, *inside, fix_sum, below, above))
-
-
-def spread_kernel(dims, inner, outer, fix, hi_ref, lo_hbm, centre_ref, lo_ref, sem):
+    )(block_of, row_of, count, *near(state, *inside, *sides, corner_s, corner_n, below, above))
+
+
+def spread_kernel(dims, inner, fix, fix_ends, outer_hbm, hi_hbm, lo_hbm, centre_ref,
+                  outer, hi_ref, lo_ref, outer_sem, hi_sem, lo_sem):
     members, levels, rows, width = dims
     sub = subs_of((rows, width))
     lane = lanes_of((members, width))
     near_edge = (lane < 2) | (lane >= width - 2)
     edge_rows = {0: 0, 1: 1, rows - 2: 2, rows - 1: 3}
 
+    def get(q):
+        part = pl.ds(q * 8, 8)
+        return pltpu.make_async_copy(outer_hbm.at[part], outer.at[part], outer_sem.at[q])
+
+    def put_hi(q):
+        return pltpu.make_async_copy(hi_ref.at[q], hi_hbm.at[q], hi_sem.at[q])
+
+    def put_lo(q):
+        return pltpu.make_async_copy(lo_ref.at[q], lo_hbm.at[q], lo_sem.at[q])
+
+    def begin(q, carry):
+        get(q).start()
+        return carry
+
     def pair(q, carry):
+        get(q).wait()
         for h in range(2):
             l = q * 2 + h
+            turn = (width - (width // levels) * l) % width
             mean = jnp.zeros((rows, width), F32)
             for y in range(rows):
                 v = outer[l * 4 + edge_rows[y]] if y in edge_rows else inner[l * (rows - 4) + y - 2]
-                turned = pltpu.roll(fix[pl.ds(y * members, members), :], (width - (width // levels) * l) % width, 1)
-                v = v + jnp.where(near_edge, turned, 0.0)
+                if y in (0, rows - 1):
+                    add = fix_ends[pl.ds((0 if y == 0 else 1) * members, members), :]
+                else:
+                    add = fix[pl.ds(y * members, members), :]
+                v = v + jnp.where(near_edge, pltpu.roll(add, turn, 1), 0.0)
                 m = jnp.sum(v, axis=0, keepdims=True) / members
                 mean = jnp.where(sub == y, m, mean)
                 a = v - m
@@ -469,33 +521,37 @@
                 hi_ref[to] = hi
                 lo_ref[to] = (a - hi.astype(F32)).astype(BF16)
             centre_ref[pl.ds(pl.multiple_of(l * rows, rows), rows), :] = mean
-        pltpu.make_async_copy(lo_ref.at[q], lo_hbm.at[q], sem.at[q]).start()
+        put_hi(q).start()
+        put_lo(q).start()
         return carry
 
     def finish(q, carry):
-        pltpu.make_async_copy(lo_ref.at[q], lo_hbm.at[q], sem.at[q]).wait()
+        put_hi(q).wait()
+        put_lo(q).wait()
         return carry
 
+    lax.fori_loop(0, levels // 2, begin, 0)
     lax.fori_loop(0, levels // 2, pair, 0)
     lax.fori_loop(0, levels // 2, finish, 0)
 
 
-def anomalies(dims, inner, outer, fix):
+def anomalies(dims, inner, outer, fix, fix_ends):
     members, levels, rows, width = dims
     shape = (levels // 2, rows * members, 2 * width)
     return pl.pallas_call(
         functools.partial(spread_kernel, dims),
         name="anomalies",
-        out_shape=(VMEM(shape, BF16), pltpu.HBM(shape, BF16), VMEM((levels * rows, width), F32)),
-        in_specs=[IN_VMEM] * 3,
-        out_specs=[IN_VMEM, IN_HBM, IN_VMEM],
-        scratch_shapes=[VMEM(shape, BF16), pltpu.SemaphoreType.DMA((levels // 2,))],
-        **grant(8, 8_000_000, 8_000_000),
-    )(*near(inner, outer, fix))
+        out_shape=(pltpu.HBM(shape, BF16), pltpu.HBM(shape, BF16), VMEM((levels * rows, width), F32)),
+        in_specs=[IN_VMEM] * 3 + [IN_HBM],
+        out_specs=[IN_HBM] * 2 + [IN_VMEM],
+        scratch_shapes=[VMEM(outer.shape, F32), VMEM(shape, BF16), VMEM(shape, BF16)]
+        + [pltpu.SemaphoreType.DMA((levels // 2,))] * 3,
+        **grant(12, 8_000_000, 8_000_000),
+    )(*near(inner, fix, fix_ends), *far(outer))
 
 
 def moments_kernel(members, blocks_dev, block, n_parts, devices, *refs):
-    parts, (obs_ref, var_ref, _, prior_ref, innov_ref, packed_ref) = refs[:n_parts], refs[n_parts:]
+    parts, (obs_ref, var_ref, prior_ref, innov_ref, packed_ref) = refs[:n_parts], refs[n_parts:]
     scaled, both = [], []
     for b in range(blocks_dev):
         at = pl.ds(b * members, members)
@@ -532,17 +588,17 @@
         packed_ref[pl.ds(device * SUB, SUB), :] = packed
 
 
-def moments(parts, obs, var, after, members, blocks_dev, block, devices):
+def moments(parts, obs, var, members, blocks_dev, block, devices):
     return pl.pallas_call(
         functools.partial(moments_kernel, members, blocks_dev, block, len(parts), devices),
         name="moments",
         out_shape=(jax.ShapeDtypeStruct((members, blocks_dev * block), F32),
                    jax.ShapeDtypeStruct((blocks_dev, block), F32),
                    VMEM((devices * SUB, 128), F32)),
-        in_specs=[IN_VMEM] * (len(parts) + 3),
+        in_specs=[IN_VMEM] * (len(parts) + 2),
         out_specs=[IN_VMEM] * 3,
         **grant(8, 4_000_000, 400_000),
-    )(*near(*parts), obs, var, *near(after))
+    )(*near(*parts), obs, var)
 
 
 def weights(gathered, members, devices):
@@ -568,18 +624,25 @@
         a = jnp.where(lane == members + sub + SUB * i, 1.0, a)
         pull = pltpu.roll(total, (2 * members - start - i) % 128, 1)
         rows.append(jnp.where(lane == 2 * members, pull, a))
-    for k in range(members):
+    for k in range(0, members, 2):
         i0, s = divmod(k, SUB)
-        pivot_row = jnp.broadcast_to(rows[i0][s:s + 1, :], (SUB, 128))
-        pivot = jnp.broadcast_to(pivot_row[:, k:k + 1], (SUB, 128))
-        ratio = pivot_row / pivot
+        f0 = [jnp.broadcast_to(r[:, k:k + 1], (SUB, 128)) for r in rows]
+        f1 = [jnp.broadcast_to(r[:, k + 1:k + 2], (SUB, 128)) for r in rows]
+        row0, row1 = spread(rows[i0], s), spread(rows[i0], s + 1)
+        a, b, d = spread(f0[i0], s), spread(f1[i0], s), spread(f1[i0], s + 1)
+        inv = 1.0 / a
+        slope = b * inv
+        low = row1 - slope * row0
+        ratio0 = row0 * inv
+        ratio1 = low * (1.0 / (d - slope * b))
         for i in range(i0, groups):
-            if i == i0 and s == SUB - 1:
-                continue
-            factor = jnp.broadcast_to(rows[i][:, k:k + 1], (SUB, 128))
+            g1 = f1[i] - slope * f0[i]
+            change = f0[i] * ratio0
+            second = g1 * ratio1
             if i == i0:
-                factor = jnp.where(sub > s, factor, 0.0)
-            rows[i] = rows[i] - factor * ratio
+                change = jnp.where(sub > s, change, 0.0)
+                second = jnp.where(sub > s + 1, second, 0.0)
+            rows[i] = rows[i] - change - second
     mean_weight = jnp.zeros((SUB, 128), F32)
     for i in range(groups):
         pivot = jnp.sum(jnp.where(lane == sub + SUB * i, rows[i], 0.0), axis=1, keepdims=True)
@@ -589,10 +652,17 @@
     return [mean_weight + math.sqrt(members - 1.0) * r for r in rows]
 
 
-def update_kernel(dims, devices, gathered, hi_ref, centre_ref, lo_hbm, out_hbm, mat_hi, mat_lo, done, lo_ref, sem, lo_sem):
-    members, levels, rows, width = dims
-    fetch = pltpu.make_async_copy(lo_hbm, lo_ref, lo_sem)
-    fetch.start()
+def update_kernel(dims, devices, gathered, centre_ref, hi_hbm, lo_hbm, out_hbm, mat_hi, mat_lo, done, hi_ref, lo_ref, sem, part_sem):
+    members, levels, rows, width = dims
+    half = levels // 4
+
+    def get(source, target, part, k):
+        at = pl.ds(part * half, half)
+        return pltpu.make_async_copy(source.at[at], target.at[at], part_sem.at[k, part])
+
+    for part in range(2):
+        get(hi_hbm, hi_ref, part, 0).start()
+        get(lo_hbm, lo_ref, part, 1).start()
     size = rows * members
     lane = lanes_of((rows, 128))
     sub = subs_of((rows, 128))
@@ -614,8 +684,6 @@
                 mat_hi[to] = big
                 mat_lo[to] = (m - big.astype(F32)).astype(BF16)
 
-    fetch.wait()
-
     def copy(q):
         part = pl.ds(q * 2, 2)
         return pltpu.make_async_copy(done.at[:, part], out_hbm.at[:, part], sem.at[q])
@@ -631,7 +699,10 @@
         copy(q).start()
         return carry
 
-    lax.fori_loop(0, levels // 2, pair, 0)
+    for part in range(2):
+        get(hi_hbm, hi_ref, part, 0).wait()
+        get(lo_hbm, lo_ref, part, 1).wait()
+        lax.fori_loop(part * half, (part + 1) * half, pair, 0, unroll=4)
 
     def finish(q, carry):
         copy(q).wait()
@@ -646,12 +717,13 @@
         functools.partial(update_kernel, dims, devices),
         name="update",
         out_shape=jax.ShapeDtypeStruct(dims, F32),
-        in_specs=[IN_VMEM] * 3 + [IN_HBM],
+        in_specs=[IN_VMEM] * 2 + [IN_HBM] * 2,
         out_specs=IN_HBM,
         scratch_shapes=[VMEM((rows * members, rows * members), BF16)] * 2
-        + [VMEM(dims, F32), VMEM(lo.shape, BF16), pltpu.SemaphoreType.DMA((levels // 2,)), pltpu.SemaphoreType.DMA],
-        **grant(12, 2_000_000_000, 8_000_000),
-    )(*near(gathered, hi, centre), *far(lo))
+        + [VMEM(dims, F32), VMEM(lo.shape, BF16), VMEM(lo.shape, BF16), pltpu.SemaphoreType.DMA((levels // 2,)),
+           pltpu.SemaphoreType.DMA((2, 2))],
+        **grant(14, 2_000_000_000, 8_000_000),
+    )(*near(gathered, centre), *far(hi, lo))
 
 
 def per_device(sample_deviations, east_courant, north_courant, production, loss_rate, entry_count, entry_row,
@@ -674,14 +746,14 @@
     first, last = corners(dims, edge, west, east)
     corner_s = lax.ppermute(last, "lat", up)
     corner_n = lax.ppermute(first, "lat", down)
-    fix, fix_sum = columns(dims, edge, west, east, corner_s, corner_n)
-    outer, *sums = boundary(dims, state, inside, fix_sum, below, above,
+    sides = columns(dims, edge, west, east)
+    outer, fix_ends, *sums = boundary(dims, state, inside, sides, corner_s, corner_n, below, above,
                             entry_block, entry_row, entry_count, lat_size, blocks_dev)
     got = [sums[0]] + [lax.ppermute(sums[s], "lat", ring(lat_size, s)) for s in range(1, lat_size)]
-    hi, lo, centre = anomalies(dims, inner, outer, fix)
+    hi, lo, centre = anomalies(dims, inner, outer, sides[0], fix_ends)
     devices = lat_size * lon_size
     prior, innovation, packed = moments(got, observed.reshape(blocks_dev, block), obs_var.reshape(blocks_dev, block),
-                                        centre, members, blocks_dev, block, devices)
+                                        members, blocks_dev, block, devices)
     gathered = lax.all_to_all(packed, ("lon", "lat"), 0, 0, tiled=True)
     updated = update(gathered, hi, lo, centre, dims, devices)
     return updated, prior, innovation.reshape(observed.shape)

time: 70.6 us -> 65.7 us (0.931)
  blocking collectives: 13.1 us -> 0 us
  starting transfers between devices: 20.4 us -> 26.7 us
  waiting for transfers between devices: 2.36 us -> 7.32 us
  Pallas kernels: 33.1 us -> 29.9 us
    all_to_all x1 -> x0, blocking collectives: 13.1 us -> none  [per_device(): gathered = lax.all_to_all(packed, ('lon', 'lat'), 0, 0, tiled=True)]
    all_to_all x0 -> x1, starting transfers between devices: none -> 6.37 us  [per_device(): gathered = lax.all_to_all(packed, ('lon', 'lat'), 0, 0, tiled=True)]
    all_to_all x0 -> x1, waiting for transfers between devices: none -> 3.06 us  [per_device(): gathered = lax.all_to_all(packed, ('lon', 'lat'), 0, 0, tiled=True)]
    pallas_call x1, Pallas kernels: 9.6 us -> 6.69 us  [update(): pl.pallas_call(functools.partial(update_kernel, dims, devices), name='upd...]
    pallas_call x1, Pallas kernels: 3.59 us -> 1.24 us  [columns(): pl.pallas_call(functools.partial(columns_kernel, dims), name='columns', o...]
    ppermute x3, waiting for transfers between devices: 0.01 us -> 1.9 us  [per_device(): lax.ppermute(sums[s], 'lat', ring(lat_size, s))]
    pallas_call x1, Pallas kernels: 3.91 us -> 5.14 us  [anomalies(): pl.pallas_call(functools.partial(spread_kernel, dims), name='anomalies',...]
  transfers between devices with their start and end apart: 9 -> 10, of which waited for: 1 -> 4; matrix products, arithmetic and copies ran while one was open for 0% -> 0% of each run, Pallas kernels for 21% -> 20%
where the time goes in v4:
time: 65.7 us; the launch traced here: 65.5 us
  Pallas kernels  29.9 us (46%)
  starting transfers between devices  26.7 us (41%)
  waiting for transfers between devices  7.32 us (11%)
  between operations  1.44 us (2%)
    pallas_call x1, Pallas kernels, interior(): pl.pallas_call(functools.partial(interior_kernel, dims), name='interior',...  6.89 us
    pallas_call x1, Pallas kernels, update(): pl.pallas_call(functools.partial(update_kernel, dims, devices), name='upd...  6.69 us
    ppermute x3, starting transfers between devices, per_device(): lax.ppermute(sums[s], 'lat', ring(lat_size, s))  6.53 us
    all_to_all x1, starting transfers between devices, per_device(): gathered = lax.all_to_all(packed, ('lon', 'lat'), 0, 0, tiled=True)  6.37 us
    pallas_call x1, Pallas kernels, anomalies(): pl.pallas_call(functools.partial(spread_kernel, dims), name='anomalies',...  5.14 us
    pallas_call x1, Pallas kernels, pack(): pl.pallas_call(functools.partial(pack_kernel, x.shape, chunks), name='pac...  4.86 us
    pallas_call x1, Pallas kernels, boundary(): pl.pallas_call(functools.partial(boundary_kernel, dims, lat_size, slots,...  4.1 us
    ppermute x1, starting transfers between devices, per_device(): corner_s = lax.ppermute(last, 'lat', up)  3.29 us
  transfers between devices with their start and end apart: 10, of which 4 were waited for; matrix products, arithmetic and copies ran while one was open for 0% of the time, Pallas kernels for 20%

profile of v4, /device:TPU:0, one launch (start us, length us, event | category | flops | bytes accessed | tf_op | source)
XLA Modules:
  0.0 65.5 jit_solution(10246709232936292650)
XLA Ops:
  0.6 4.9 %pack_halos.1 = (f32[256,32,128]{2,1,0:T(8,128)S(1)}, f32[2176,128]{1,0:T(8,128)S(1)}, f32[2176,128]{1,0:T(8,128)S(1)}, f32[288,128]{1,0:T(8,128)S(1)}, f32[144,...) custom-call(f32[32,32,8,128]{3,2,1,0:T(8,128)} %x_hbm.1, f32[32,8,128]{2,1,0:T(8,128)} %e_hbm.1, ...), custom_call_target="tpu_custom_call" | custom-call | flops 4000000 | bytes 8000000 | tf_op jit(solution)/shard_map/pack_halos/pallas_call | solution.py:116
  5.5 2.5 %collective-permute-start.4 = (f32[2176,128]{1,0:T(8,128)S(1)}, f32[2176,128]{1,0:T(8,128)S(1)}, u32[]{:S(2)}, u32[]{:S(2)}) collective-permute-start(f32[2176,128]{1,0:T(8,128)S(1)} %get-tuple-element.46), channel_id=1, source_target_pairs={{0,1},{1,2},{2,3},{4,5},{5,6},{6,7},{8,9},{9,10},{10,11},{12,13},{... | collective-permute-start | bytes 3342344 | tf_op jit(solution)/shard_map/ppermute | solution.py:743
  8.0 1.3 %collective-permute-start.5 = (f32[2176,128]{1,0:T(8,128)S(1)}, f32[2176,128]{1,0:T(8,128)S(1)}, u32[]{:S(2)}, u32[]{:S(2)}) collective-permute-start(f32[2176,128]{1,0:T(8,128)S(1)} %get-tuple-element.47), channel_id=1, source_target_pairs={{1,0},{2,1},{3,2},{5,4},{6,5},{7,6},{9,8},{10,9},{11,10},{13,12},{... | collective-permute-start | bytes 3342344 | tf_op jit(solution)/shard_map/ppermute | solution.py:744
  9.3 2.4 %collective-permute-start = (f32[144,128]{1,0:T(8,128)S(1)}, f32[144,128]{1,0:T(8,128)S(1)}, u32[]{:S(2)}, u32[]{:S(2)}) collective-permute-start(f32[144,128]{1,0:T(8,128)S(1)} %get-tuple-element.39), channel_id=1, source_target_pairs={{0,4},{4,8},{8,12},{12,16},{16,20},{20,24},{24,28},{28,0},{1,5},{5... | collective-permute-start | bytes 221192 | tf_op jit(solution)/shard_map/ppermute | solution.py:741
  11.7 3.1 %collective-permute-start.1 = (f32[144,128]{1,0:T(8,128)S(1)}, f32[144,128]{1,0:T(8,128)S(1)}, u32[]{:S(2)}, u32[]{:S(2)}) collective-permute-start(f32[144,128]{1,0:T(8,128)S(1)} %get-tuple-element.40), channel_id=1, source_target_pairs={{0,28},{4,0},{8,4},{12,8},{16,12},{20,16},{24,20},{28,24},{1,29},{... | collective-permute-start | bytes 221192 | tf_op jit(solution)/shard_map/ppermute | solution.py:742
  14.8 2.3 %collective-permute-done.west = f32[144,128]{1,0:T(8,128)S(1)} collective-permute-done((f32[144,128]{1,0:T(8,128)S(1)}, f32[144,128]{1,0:T(8,128)S(1)}, u32[]{:S(2)}, u32[]{:S(2)}) %collective-permute-start) | collective-permute-done | bytes 73760 | tf_op jit(solution)/shard_map/ppermute | solution.py:741
  17.1 0.1 corners.1
  17.2 3.3 %collective-permute-start.2 = (f32[40,128]{1,0:T(8,128)S(1)}, f32[40,128]{1,0:T(8,128)S(1)}, u32[]{:S(2)}, u32[]{:S(2)}) collective-permute-start(f32[40,128]{1,0:T(8,128)S(1)} %get-tuple-element.44), channel_id=1, source_target_pairs={{0,1},{1,2},{2,3},{4,5},{5,6},{6,7},{8,9},{9,10},{10,11},{12,13},{... | collective-permute-start | bytes 61448 | tf_op jit(solution)/shard_map/ppermute | solution.py:747
  20.5 1.3 %collective-permute-start.3 = (f32[40,128]{1,0:T(8,128)S(1)}, f32[40,128]{1,0:T(8,128)S(1)}, u32[]{:S(2)}, u32[]{:S(2)}) collective-permute-start(f32[40,128]{1,0:T(8,128)S(1)} %get-tuple-element.45), channel_id=1, source_target_pairs={{1,0},{2,1},{3,2},{5,4},{6,5},{7,6},{9,8},{10,9},{11,10},{13,12},{... | collective-permute-start | bytes 61448 | tf_op jit(solution)/shard_map/ppermute | solution.py:748
  22.4 0.0 copy-start.2
  22.5 6.9 %interior.1 = (f32[128,32,128]{2,1,0:T(8,128)S(1)}, f32[192,32,128]{2,1,0:T(8,128)S(1)}, f32[128,128]{1,0:T(8,128)S(1)}, f32[32,6,8,128]{3,2,1,0:T(8,128)S(1)}, bf16[48,128,128]{2,1,0:T(8,128)(2,1)S(1)}) custom-call(f32[256,32,128]{2,1,0:T(8,128)S(1)} %get-tuple-element.32.state, f32[4,32,8,128]{3,2,1,0:T(8,128)S(1)} %get-tuple-element.33.fields, ...), custom_call_target="tpu_custom_call" | custom-call | flops 60000000 | bytes 12000000 | tf_op jit(solution)/shard_map/interior/pallas_call | solution.py:353
  29.4 1.2 %columns.1 = (f32[256,128]{1,0:T(8,128)S(1)}, f32[256,128]{1,0:T(8,128)S(1)}, f32[8,8,128]{2,1,0:T(8,128)S(1)}) custom-call(f32[288,128]{1,0:T(8,128)S(1)} %get-tuple-element.38.edge, f32[144,128]{1,0:T(8,128)S(1)} %collective-permute-done.west, f32[144,128]{1,0:T(8,128)S(1)} %collective-permute-done.1.east), custom_call_target="tpu_custom_call" | custom-call | flops 2000000 | bytes 1000000 | tf_op jit(solution)/shard_map/columns/pallas_call | solution.py:288
  30.7 0.0 copy-start.1
  30.7 4.1 %boundary_rays.1 = (f32[128,32,128]{2,1,0:T(8,128)}, f32[64,128]{1,0:T(8,128)S(1)}, f32[128,128]{1,0:T(8,128)S(1)}, f32[128,128]{1,0:T(8,128)S(1)}, f32[128,128]{1,0:T(8,128)S(1)}, /*index=5*/f32[128,128]{1,0:T(8,128)S(1)}) custom-call(s32[48]{0:T(128)S(1)} %copy-done.2, s32[48]{0:T(128)S(1)} %copy-done.3, s32[1]{0:T(128)S(6)} %copy.14.count, ...), custom_call_target="tpu_custom_call" | custom-call | flops 30000000 | bytes 12000000 | tf_op jit(solution)/shard_map/boundary_rays/pallas_call | solution.py:463
  34.8 3.4 %collective-permute-start.6 = (f32[128,128]{1,0:T(8,128)S(1)}, f32[128,128]{1,0:T(8,128)S(1)}, u32[]{:S(2)}, u32[]{:S(2)}) collective-permute-start(f32[128,128]{1,0:T(8,128)S(1)} %get-tuple-element.49), channel_id=1, source_target_pairs={{0,1},{1,2},{2,3},{3,0},{4,5},{5,6},{6,7},{7,4},{8,9},{9,10},{10,1... | collective-permute-start | bytes 196616 | tf_op jit(solution)/shard_map/ppermute | solution.py:752
  38.2 1.7 %collective-permute-start.7 = (f32[128,128]{1,0:T(8,128)S(1)}, f32[128,128]{1,0:T(8,128)S(1)}, u32[]{:S(2)}, u32[]{:S(2)}) collective-permute-start(f32[128,128]{1,0:T(8,128)S(1)} %get-tuple-element.50), channel_id=1, source_target_pairs={{0,2},{1,3},{2,0},{3,1},{4,6},{5,7},{6,4},{7,5},{8,10},{9,11},{10,... | collective-permute-start | bytes 196616 | tf_op jit(solution)/shard_map/ppermute | solution.py:752
  39.9 1.4 %collective-permute-start.8 = (f32[128,128]{1,0:T(8,128)S(1)}, f32[128,128]{1,0:T(8,128)S(1)}, u32[]{:S(2)}, u32[]{:S(2)}) collective-permute-start(f32[128,128]{1,0:T(8,128)S(1)} %get-tuple-element.51), channel_id=1, source_target_pairs={{0,3},{1,0},{2,1},{3,2},{4,7},{5,4},{6,5},{7,6},{8,11},{9,8},{10,9... | collective-permute-start | bytes 196616 | tf_op jit(solution)/shard_map/ppermute | solution.py:752
  41.3 1.2 %collective-permute-done.7.refs_2_ = f32[128,128]{1,0:T(8,128)S(1)} collective-permute-done((f32[128,128]{1,0:T(8,128)S(1)}, f32[128,128]{1,0:T(8,128)S(1)}, u32[]{:S(2)}, u32[]{:S(2)}) %collective-permute-start.7) | collective-permute-done | bytes 65568 | tf_op jit(solution)/shard_map/ppermute | solution.py:752
  42.5 0.7 %collective-permute-done.8.refs_3_ = f32[128,128]{1,0:T(8,128)S(1)} collective-permute-done((f32[128,128]{1,0:T(8,128)S(1)}, f32[128,128]{1,0:T(8,128)S(1)}, u32[]{:S(2)}, u32[]{:S(2)}) %collective-permute-start.8) | collective-permute-done | bytes 65568 | tf_op jit(solution)/shard_map/ppermute | solution.py:752
  43.2 1.0 %moments.1 = (f32[32,512]{1,0:T(8,128)}, f32[4,128]{1,0:T(4,128)}, f32[256,128]{1,0:T(8,128)}) custom-call(f32[128,128]{1,0:T(8,128)S(1)} %get-tuple-element.48.refs_0_, f32[128,128]{1,0:T(8,128)S(1)} %collective-permute-done.6.refs_1_, f32[128,128]{1,0:T(8,128)S(1)} %collective-permute-done.7.refs_2_, f32[128,128]{1,0:T(8,128)S(1)} %collective-permute-done.8.refs_3_, ...), custom_call_target="tpu_custom_call" | custom-call | flops 4000000 | bytes 400000 | tf_op jit(solution)/shard_map/moments/pallas_call | solution.py:592
  44.2 6.4 %all-to-all-start = ((f32[32,8,128]{2,1,0:T(8,128)}), f32[32,8,128]{2,1,0:T(8,128)S(1)}, u32[]{:S(2)}, u32[]{:S(2)}) async-start(f32[32,8,128]{2,1,0:T(8,128)} %bitcast.2), calls=%async_computation | async-start | bytes 262144 | tf_op jit(solution)/shard_map/all_to_all | solution.py:757
  50.6 5.1 %anomalies.1 = (bf16[16,256,256]{2,1,0:T(8,128)(2,1)}, bf16[16,256,256]{2,1,0:T(8,128)(2,1)}, f32[256,128]{1,0:T(8,128)S(1)}) custom-call(f32[128,32,128]{2,1,0:T(8,128)S(1)} %get-tuple-element.53.inner, f32[256,128]{1,0:T(8,128)S(1)} %get-tuple-element.41.fix, f32[64,128]{1,0:T(8,128)S(1)} %get-tuple-element.54.fix_ends, ...), custom_call_target="tpu_custom_call" | custom-call | flops 8000000 | bytes 8000000 | tf_op jit(solution)/shard_map/anomalies/pallas_call | solution.py:541
  55.7 3.1 %all-to-all-done = f32[32,8,128]{2,1,0:T(8,128)S(1)} async-done(((f32[32,8,128]{2,1,0:T(8,128)}), f32[32,8,128]{2,1,0:T(8,128)S(1)}, u32[]{:S(2)}, u32[]{:S(2)}) %all-to-all-start) | async-done | bytes 131104 | tf_op jit(solution)/shard_map/all_to_all | solution.py:757
  58.8 6.7 %update.1 = f32[32,32,8,128]{3,2,1,0:T(8,128)} custom-call(f32[256,128]{1,0:T(8,128)S(1)} %bitcast.5, f32[256,128]{1,0:T(8,128)S(1)} %get-tuple-element.56.centre_ref, bf16[16,256,256]{2,1,0:T(8,128)(2,1)} %get-tuple-element.57.hi_hbm, bf16[16,256,256]{2,1,0:T(8,128)(2,1)} %get-tuple-element.58.lo_hbm), custom_call_target="tpu_custom_call" | custom-call | flops 2000000000 | bytes 8000000 | tf_op jit(solution)/shard_map/update/pallas_call | solution.py:716
  (12 shorter events, 0.0 us)
Async XLA Ops:
  5.5 25.1 %collective-permute-start.4 = (f32[2176,128]{1,0:T(8,128)S(1)}, f32[2176,128]{1,0:T(8,128)S(1)}, u32[]{:S(2)}, u32[]{:S(2)}) collective-permute-start(f32[2176,128]{1,0:T(8,128)S(1)} %get-tuple-element.46), channel_id=1, source_target_pairs={{0,1},{1,2},{2,3},{4,5},{5,6},{6,7},{8,9},{9,10},{10,11},{12,13},{... | collective-permute-start | bytes 3342344 | tf_op jit(solution)/shard_map/ppermute | solution.py:743
  8.0 22.7 %collective-permute-start.5 = (f32[2176,128]{1,0:T(8,128)S(1)}, f32[2176,128]{1,0:T(8,128)S(1)}, u32[]{:S(2)}, u32[]{:S(2)}) collective-permute-start(f32[2176,128]{1,0:T(8,128)S(1)} %get-tuple-element.47), channel_id=1, source_target_pairs={{1,0},{2,1},{3,2},{5,4},{6,5},{7,6},{9,8},{10,9},{11,10},{13,12},{... | collective-permute-start | bytes 3342344 | tf_op jit(solution)/shard_map/ppermute | solution.py:744
  9.3 7.8 %collective-permute-start = (f32[144,128]{1,0:T(8,128)S(1)}, f32[144,128]{1,0:T(8,128)S(1)}, u32[]{:S(2)}, u32[]{:S(2)}) collective-permute-start(f32[144,128]{1,0:T(8,128)S(1)} %get-tuple-element.39), channel_id=1, source_target_pairs={{0,4},{4,8},{8,12},{12,16},{16,20},{20,24},{24,28},{28,0},{1,5},{5... | collective-permute-start | bytes 221192 | tf_op jit(solution)/shard_map/ppermute | solution.py:741
  11.7 5.5 %collective-permute-start.1 = (f32[144,128]{1,0:T(8,128)S(1)}, f32[144,128]{1,0:T(8,128)S(1)}, u32[]{:S(2)}, u32[]{:S(2)}) collective-permute-start(f32[144,128]{1,0:T(8,128)S(1)} %get-tuple-element.40), channel_id=1, source_target_pairs={{0,28},{4,0},{8,4},{12,8},{16,12},{20,16},{24,20},{28,24},{1,29},{... | collective-permute-start | bytes 221192 | tf_op jit(solution)/shard_map/ppermute | solution.py:742
  17.2 13.4 %collective-permute-start.2 = (f32[40,128]{1,0:T(8,128)S(1)}, f32[40,128]{1,0:T(8,128)S(1)}, u32[]{:S(2)}, u32[]{:S(2)}) collective-permute-start(f32[40,128]{1,0:T(8,128)S(1)} %get-tuple-element.44), channel_id=1, source_target_pairs={{0,1},{1,2},{2,3},{4,5},{5,6},{6,7},{8,9},{9,10},{10,11},{12,13},{... | collective-permute-start | bytes 61448 | tf_op jit(solution)/shard_map/ppermute | solution.py:747
  20.5 10.1 %collective-permute-start.3 = (f32[40,128]{1,0:T(8,128)S(1)}, f32[40,128]{1,0:T(8,128)S(1)}, u32[]{:S(2)}, u32[]{:S(2)}) collective-permute-start(f32[40,128]{1,0:T(8,128)S(1)} %get-tuple-element.45), channel_id=1, source_target_pairs={{1,0},{2,1},{3,2},{5,4},{6,5},{7,6},{9,8},{10,9},{11,10},{13,12},{... | collective-permute-start | bytes 61448 | tf_op jit(solution)/shard_map/ppermute | solution.py:748
  22.4 8.2 %copy-start.2 = (s32[48]{0:T(128)S(1)}, s32[48]{0:T(128)}, u32[]{:S(2)}) copy-start(s32[48]{0:T(128)} %block_of.1) | copy-start | bytes 580
  22.4 8.2 %copy-start.3 = (s32[48]{0:T(128)S(1)}, s32[48]{0:T(128)}, u32[]{:S(2)}) copy-start(s32[48]{0:T(128)} %row_of.1) | copy-start | bytes 580
  30.7 12.6 %copy-start = (f32[512]{0:T(512)S(1)}, f32[512]{0:T(512)}, u32[]{:S(2)}) copy-start(f32[512]{0:T(512)} %param.20) | copy-start | bytes 6148
  30.7 12.6 %copy-start.1 = (f32[512]{0:T(512)S(1)}, f32[512]{0:T(512)}, u32[]{:S(2)}) copy-start(f32[512]{0:T(512)} %param.21) | copy-start | bytes 6148
  34.8 6.5 %collective-permute-start.6 = (f32[128,128]{1,0:T(8,128)S(1)}, f32[128,128]{1,0:T(8,128)S(1)}, u32[]{:S(2)}, u32[]{:S(2)}) collective-permute-start(f32[128,128]{1,0:T(8,128)S(1)} %get-tuple-element.49), channel_id=1, source_target_pairs={{0,1},{1,2},{2,3},{3,0},{4,5},{5,6},{6,7},{7,4},{8,9},{9,10},{10,1... | collective-permute-start | bytes 196616 | tf_op jit(solution)/shard_map/ppermute | solution.py:752
  38.2 4.3 %collective-permute-start.7 = (f32[128,128]{1,0:T(8,128)S(1)}, f32[128,128]{1,0:T(8,128)S(1)}, u32[]{:S(2)}, u32[]{:S(2)}) collective-permute-start(f32[128,128]{1,0:T(8,128)S(1)} %get-tuple-element.50), channel_id=1, source_target_pairs={{0,2},{1,3},{2,0},{3,1},{4,6},{5,7},{6,4},{7,5},{8,10},{9,11},{10,... | collective-permute-start | bytes 196616 | tf_op jit(solution)/shard_map/ppermute | solution.py:752
  39.9 3.3 %collective-permute-start.8 = (f32[128,128]{1,0:T(8,128)S(1)}, f32[128,128]{1,0:T(8,128)S(1)}, u32[]{:S(2)}, u32[]{:S(2)}) collective-permute-start(f32[128,128]{1,0:T(8,128)S(1)} %get-tuple-element.51), channel_id=1, source_target_pairs={{0,3},{1,0},{2,1},{3,2},{4,7},{5,4},{6,5},{7,6},{8,11},{9,8},{10,9... | collective-permute-start | bytes 196616 | tf_op jit(solution)/shard_map/ppermute | solution.py:752
  44.2 14.6 %all-to-all-start = ((f32[32,8,128]{2,1,0:T(8,128)}), f32[32,8,128]{2,1,0:T(8,128)S(1)}, u32[]{:S(2)}, u32[]{:S(2)}) async-start(f32[32,8,128]{2,1,0:T(8,128)} %bitcast.2), calls=%async_computation | async-start | bytes 262144 | tf_op jit(solution)/shard_map/all_to_all | solution.py:757
